TPU v7x, 256 devices: a whole 4x4x8 slice. The times are simulated.
256 devices in a mesh: lat: 4 (over x_hi, core), lon: 64 (over z, x_lo, y).
Axes of the slice: x: 4 (x_hi: 2, x_lo: 2; x = x_hi * 2 + x_lo), y: 4, z: 8, core: 2. Of those that a mesh axis runs over, the one named last changes fastest.
Arguments:
- tendencies: bfloat16 [3, 64, 2880, 128], P(None, 'lat', 'lon'), may hold values from -6 to 6
- bands: int32 [64], replicated, may hold values from 45 to 180
- winds: float32 [2, 64, 2880, 128], P(None, 'lat', 'lon'), may hold values from -6 to 6
- tracers: float32 [5, 64, 2880, 128], P(None, 'lat', 'lon'), may hold values from -6 to 6
Outputs:
- filtered: bfloat16 [3, 64, 2880, 128], P(None, 'lat', 'lon')
- advected: float32 [5, 64, 2880, 128], P(None, 'lat', 'lon')
All inputs are finite; a program needn't handle non-finite values.
Results may differ from a plain program's by a relative error of at most 0.0038.
Values may be sent and summed in bfloat16 or wider, within the bound.
No kernel may reach another device: no remote copies, remote signals or barrier semaphores. Data moves between devices by JAX's collectives and lax.ppermute only.
A program may use at most 64 MiB of HBM per device.

v0:
```python
import math

import jax
import jax.numpy as jnp
from jax import lax
from jax.sharding import PartitionSpec as P

HEMI = 720


def extended(block, sides, width, periodic):
    for axis, dim in sides:
        count = lax.axis_size(axis)
        forward = [(i, i + 1) for i in range(count - 1)]
        if periodic:
            forward.append((count - 1, 0))
        backward = [(target, source) for source, target in forward]
        low = lax.ppermute(
            lax.slice_in_dim(block, block.shape[dim] - width, None, axis=dim), axis, forward
        )
        high = lax.ppermute(lax.slice_in_dim(block, 0, width, axis=dim), axis, backward)
        block = jnp.concatenate([low, block, high], axis=dim)
    return block


def latitude_factors(row_ids, lat_count):
    grid_row = row_ids.astype(jnp.float32) + jnp.float32(HEMI // 2 - lat_count // 2)
    centre_cos = jnp.sin(math.pi * (grid_row + 0.5) / (2.0 * HEMI))
    face_cos = jnp.sin(math.pi * grid_row / (2.0 * HEMI))
    return (centre_cos, face_cos)


def damping_rows(row_ids, lat_count):
    position = row_ids.astype(jnp.float32)
    return 0.25 + 0.5 * (position + 0.5) / (lat_count / 2.0)


def wave_tables(wave_block, lon_count):
    cell_index = jnp.arange(lon_count, dtype=jnp.int32)
    phase_index = cell_index[:, None] * wave_block[None, :] % lon_count
    phase_angle = phase_index.astype(jnp.float32) * (2.0 * math.pi / lon_count)
    return (jnp.cos(phase_angle), jnp.sin(phase_angle))


def wave_weights(wave_block, band_rows, damping, lon_count):
    half_wave = lon_count // 2
    multiplier = jnp.where(
        wave_block[None, :] <= band_rows[:, None], jnp.float32(1.0), damping[:, None]
    )
    fold_count = jnp.where((wave_block == 0) | (wave_block == half_wave), 1.0, 2.0)
    fold_count = jnp.where(wave_block > half_wave, 0.0, fold_count)
    return (multiplier - 1.0) * fold_count[None, :] / lon_count


def spectral_rows(row_data, band_rows, damping):
    lon_count = row_data.shape[2]
    block_width = 128
    block_total = lon_count // 2 // block_width + 1

    def one_block(block_number, running):
        wave_block = block_number * block_width + jnp.arange(block_width, dtype=jnp.int32)
        cos_table, sin_table = wave_tables(wave_block, lon_count)
        weights = wave_weights(wave_block, band_rows, damping, lon_count)[None, :, :, None]
        cos_part = jnp.einsum("frml,mk->frkl", row_data, cos_table, precision=lax.Precision.HIGH)
        sin_part = jnp.einsum("frml,mk->frkl", row_data, sin_table, precision=lax.Precision.HIGH)
        running = running + jnp.einsum(
            "frkl,mk->frml", cos_part * weights, cos_table, precision=lax.Precision.HIGH
        )
        return running + jnp.einsum(
            "frkl,mk->frml", sin_part * weights, sin_table, precision=lax.Precision.HIGH
        )

    return row_data + lax.fori_loop(0, block_total, one_block, jnp.zeros_like(row_data))


def polar_filter(work_rows, band_rows, damping, active):

    def transform(values):
        return spectral_rows(values.astype(jnp.float32), band_rows, damping).astype(jnp.bfloat16)

    filtered_rows = lax.cond(
        active,
        transform,
        lambda values: values,
        lax.all_to_all(work_rows, "lon", split_axis=3, concat_axis=2, tiled=True),
    )
    return lax.all_to_all(filtered_rows, "lon", split_axis=2, concat_axis=3, tiled=True)


def per_device(tendencies, bands, winds, tracers):
    lat_rows = tendencies.shape[1]
    lat_devices = lax.axis_size("lat")
    lat_count = lat_devices * lat_rows
    lat_place = lax.axis_index("lat")
    polar_side = lat_place < lat_devices // 2
    row_ids = lat_place * lat_rows + jnp.arange(lat_rows, dtype=jnp.int32)
    filtered = polar_filter(
        tendencies, jnp.take(bands, row_ids), damping_rows(row_ids, lat_count), polar_side
    )
    own_ids = lat_place * lat_rows + jnp.arange(lat_rows, dtype=jnp.int32)
    centre_cos, face_cos = latitude_factors(own_ids, lat_count)
    next_centre, face_next = latitude_factors(own_ids + 1, lat_count)
    new_winds = winds + filtered[0:2].astype(jnp.float32)
    east_courant = 0.5 * jnp.tanh(new_winds[0])
    north_courant = 0.25 * jnp.tanh(new_winds[1])
    tracer_count = tracers.shape[0]
    north_stack = jnp.concatenate([tracers, north_courant[None]], axis=0)
    lat_padded = extended(north_stack.astype(jnp.bfloat16), (("lat", 1),), 1, False).astype(
        north_stack.dtype
    )
    east_stack = jnp.concatenate([tracers, east_courant[None]], axis=0)
    lon_padded = extended(east_stack.astype(jnp.bfloat16), (("lon", 2),), 1, True).astype(
        east_stack.dtype
    )
    prior_rows = lat_padded[:tracer_count, :-2]
    next_rows = lat_padded[:tracer_count, 2:]
    next_courant = lat_padded[tracer_count, 2:]
    west_cells = lon_padded[:tracer_count, :, :-2]
    east_cells = lon_padded[:tracer_count, :, 2:]
    east_next = lon_padded[tracer_count, :, 2:]
    f_west = jnp.maximum(east_courant, 0.0) * west_cells + jnp.minimum(east_courant, 0.0) * tracers
    f_east = jnp.maximum(east_next, 0.0) * tracers + jnp.minimum(east_next, 0.0) * east_cells
    g_pole = face_cos[:, None, None] * (
        jnp.maximum(north_courant, 0.0) * prior_rows + jnp.minimum(north_courant, 0.0) * tracers
    )
    g_next = face_next[:, None, None] * (
        jnp.maximum(next_courant, 0.0) * tracers + jnp.minimum(next_courant, 0.0) * next_rows
    )
    advected = tracers - (f_east - f_west) - (g_next - g_pole) / centre_cos[:, None, None]
    return (filtered, advected)


def solution(mesh):
    return jax.shard_map(
        per_device,
        mesh=mesh,
        in_specs=(
            P(None, "lat", "lon", None),
            P(),
            P(None, "lat", "lon", None),
            P(None, "lat", "lon", None),
        ),
        out_specs=(P(None, "lat", "lon", None), P(None, "lat", "lon", None)),
        check_vma=False,
    )
```

profile of v0, /device:TPU:1, one launch (start us, length us, event | category | flops | bytes accessed | tf_op | source)
XLA Modules:
  0.0 477.6 jit_solution(7744977443534993194)
XLA Ops:
  5.7 13.6 %all-to-all-start = ((bf16[64,2,2160]{2,1,0:T(2,128)(2,1)}), bf16[64,2,2160]{2,1,0:T(2,128)(2,1)S(1)}, u32[]{:S(2)}, u32[]{:S(2)}) async-start(bf16[64,2,2160]{2,1,0:T(2,128)(2,1)} %reshape.127), calls=%async_computation | async-start | bytes 1114112 | tf_op jit(solution)/shard_map/all_to_all | solution.py:85
  19.3 16.2 %all-to-all-done = bf16[64,2,2160]{2,1,0:T(2,128)(2,1)S(1)} async-done(((bf16[64,2,2160]{2,1,0:T(2,128)(2,1)}), bf16[64,2,2160]{2,1,0:T(2,128)(2,1)S(1)}, u32[]{:S(2)}, u32[]{:S(2)}) %all-to-all-start) | async-done | bytes 552992 | tf_op jit(solution)/shard_map/all_to_all | solution.py:85
  41.3 339.7 %conditional.1 = (bf16[3,16,2880,2]{2,1,3,0:T(8,128)(2,1)S(1)}) conditional(s32[]{:T(128)} %convert_element_type.59, bf16[3,16,2880,2]{2,1,3,0:T(8,128)(2,1)S(1)} %all_to_all.32, (bf16[3,16,2880,2]{2,1,3,0:T(8,128)(2,1)S(1)}, s32[16]{0:T(128)S(1)}, s32[]{:T(128)}, s32[16,1]{0,1:T(1,128)S(1)}, s32[64]{0:T(128)S(1)}, /*index=5*/f32[16]{0:T(128)S(1)}) %tuple.110), branch_computations={%region_0.1_spmd, %region_1.0_spmd} | conditional | flops 864590080 | bytes 10736655 | solution.py:81
  42.1 329.6 %while.23 = (s32[]{:T(128)}, f32[3,16,2880,2]{2,1,3,0:T(8,128)S(1)}, f32[3,16,2880,2]{2,1,3,0:T(8,128)S(1)}, s32[16]{0:T(128)S(1)}, f32[16]{0:T(128)S(1)}, /*index=5*/s32[]{:T(128)}, s32[]{:T(128)}, s32[]{:T(128)}) while((s32[]{:T(128)}, f32[3,16,2880,2]{2,1,3,0:T(8,128)S(1)}, f32[3,16,2880,2]{2,1,3,0:T(8,128)S(1)}, ...), condition=%wide.region_3.3_spmd.clone, body=%wide.region_2.2_spmd.clone.sunk | while | flops 863482880 | bytes 6861051 | solution.py:73
  60.5 6.5 %fusion.108 = f32[3,16,128,2]{2,1,3,0:T(8,128)S(1)} fusion(f32[3,16,2880,2]{2,1,3,0:T(8,128)S(1)} %get-tuple-element.416, s32[128]{0:T(128)S(1)} %iota_add_fusion.3, f32[16,128]{1,0:T(8,128)S(1)} %multiply_multiply_fusion.2), kind=kOutput, calls=%fused_computation.23.clone.1 | convolution fusion | flops 215666688 | bytes 1163776 | tf_op jit(solution)/shard_map/cond/branch_1_fun/while/body/eval_jaxpr/frml,mk->frkl/dot_general | solution.py:65
  73.3 6.4 %fusion.107 = f32[3,16,2880,2]{2,1,3,0:T(8,128)S(1)} fusion(f32[3,16,128,2]{2,1,3,0:T(8,128)S(1)} %fusion.106, f32[3,16,2880,2]{2,1,3,0:T(8,128)S(1)} %get-tuple-element.407, s32[128]{0:T(128)S(1)} %iota_add_fusion.3, pred[]{:T(512)S(6)} %compare.3), kind=kOutput, calls=%fused_computation.4.clone.1 | convolution fusion | flops 216207360 | bytes 2261505 | tf_op jit(solution)/shard_map/cond/branch_1_fun/while/body/eval_jaxpr/frkl,mk->frml/dot_general | solution.py:66
  79.8 6.5 %fusion.109 = f32[3,16,2880,2]{2,1,3,0:T(8,128)S(1)} fusion(f32[3,16,2880,2]{2,1,3,0:T(8,128)S(1)} %fusion.107, f32[3,16,128,2]{2,1,3,0:T(8,128)S(1)} %fusion.108, s32[128]{0:T(128)S(1)} %iota_add_fusion.3), kind=kOutput, calls=%fused_computation.2.clone.1 | convolution fusion | flops 215930880 | bytes 2261504 | tf_op jit(solution)/shard_map/cond/branch_1_fun/while/body/eval_jaxpr/frkl,mk->frml/dot_general | solution.py:69
  86.4 6.5 %fusion.108 = f32[3,16,128,2]{2,1,3,0:T(8,128)S(1)} fusion(f32[3,16,2880,2]{2,1,3,0:T(8,128)S(1)} %get-tuple-element.416, s32[128]{0:T(128)S(1)} %iota_add_fusion.3, f32[16,128]{1,0:T(8,128)S(1)} %multiply_multiply_fusion.2), kind=kOutput, calls=%fused_computation.23.clone.1 | convolution fusion | flops 215666688 | bytes 1163776 | tf_op jit(solution)/shard_map/cond/branch_1_fun/while/body/eval_jaxpr/frml,mk->frkl/dot_general | solution.py:65
  92.9 6.4 %fusion.106 = f32[3,16,128,2]{2,1,3,0:T(8,128)S(1)} fusion(f32[3,16,2880,2]{2,1,3,0:T(8,128)S(1)} %get-tuple-element.416, s32[128]{0:T(128)S(1)} %iota_add_fusion.3, f32[16,128]{1,0:T(8,128)S(1)} %multiply_multiply_fusion.2), kind=kOutput, calls=%fused_computation.21.clone.1 | convolution fusion | flops 215666688 | bytes 1163776 | tf_op jit(solution)/shard_map/cond/branch_1_fun/while/body/eval_jaxpr/frml,mk->frkl/dot_general | solution.py:64
  99.3 6.4 %fusion.107 = f32[3,16,2880,2]{2,1,3,0:T(8,128)S(1)} fusion(f32[3,16,128,2]{2,1,3,0:T(8,128)S(1)} %fusion.106, f32[3,16,2880,2]{2,1,3,0:T(8,128)S(1)} %get-tuple-element.407, s32[128]{0:T(128)S(1)} %iota_add_fusion.3, pred[]{:T(512)S(6)} %compare.3), kind=kOutput, calls=%fused_computation.4.clone.1 | convolution fusion | flops 216207360 | bytes 2261505 | tf_op jit(solution)/shard_map/cond/branch_1_fun/while/body/eval_jaxpr/frkl,mk->frml/dot_general | solution.py:66
  105.7 6.5 %fusion.109 = f32[3,16,2880,2]{2,1,3,0:T(8,128)S(1)} fusion(f32[3,16,2880,2]{2,1,3,0:T(8,128)S(1)} %fusion.107, f32[3,16,128,2]{2,1,3,0:T(8,128)S(1)} %fusion.108, s32[128]{0:T(128)S(1)} %iota_add_fusion.3), kind=kOutput, calls=%fused_computation.2.clone.1 | convolution fusion | flops 215930880 | bytes 2261504 | tf_op jit(solution)/shard_map/cond/branch_1_fun/while/body/eval_jaxpr/frkl,mk->frml/dot_general | solution.py:69
  112.4 6.5 %fusion.108 = f32[3,16,128,2]{2,1,3,0:T(8,128)S(1)} fusion(f32[3,16,2880,2]{2,1,3,0:T(8,128)S(1)} %get-tuple-element.416, s32[128]{0:T(128)S(1)} %iota_add_fusion.3, f32[16,128]{1,0:T(8,128)S(1)} %multiply_multiply_fusion.2), kind=kOutput, calls=%fused_computation.23.clone.1 | convolution fusion | flops 215666688 | bytes 1163776 | tf_op jit(solution)/shard_map/cond/branch_1_fun/while/body/eval_jaxpr/frml,mk->frkl/dot_general | solution.py:65
  118.8 6.4 %fusion.106 = f32[3,16,128,2]{2,1,3,0:T(8,128)S(1)} fusion(f32[3,16,2880,2]{2,1,3,0:T(8,128)S(1)} %get-tuple-element.416, s32[128]{0:T(128)S(1)} %iota_add_fusion.3, f32[16,128]{1,0:T(8,128)S(1)} %multiply_multiply_fusion.2), kind=kOutput, calls=%fused_computation.21.clone.1 | convolution fusion | flops 215666688 | bytes 1163776 | tf_op jit(solution)/shard_map/cond/branch_1_fun/while/body/eval_jaxpr/frml,mk->frkl/dot_general | solution.py:64
  125.2 6.4 %fusion.107 = f32[3,16,2880,2]{2,1,3,0:T(8,128)S(1)} fusion(f32[3,16,128,2]{2,1,3,0:T(8,128)S(1)} %fusion.106, f32[3,16,2880,2]{2,1,3,0:T(8,128)S(1)} %get-tuple-element.407, s32[128]{0:T(128)S(1)} %iota_add_fusion.3, pred[]{:T(512)S(6)} %compare.3), kind=kOutput, calls=%fused_computation.4.clone.1 | convolution fusion | flops 216207360 | bytes 2261505 | tf_op jit(solution)/shard_map/cond/branch_1_fun/while/body/eval_jaxpr/frkl,mk->frml/dot_general | solution.py:66
  131.7 6.5 %fusion.109 = f32[3,16,2880,2]{2,1,3,0:T(8,128)S(1)} fusion(f32[3,16,2880,2]{2,1,3,0:T(8,128)S(1)} %fusion.107, f32[3,16,128,2]{2,1,3,0:T(8,128)S(1)} %fusion.108, s32[128]{0:T(128)S(1)} %iota_add_fusion.3), kind=kOutput, calls=%fused_computation.2.clone.1 | convolution fusion | flops 215930880 | bytes 2261504 | tf_op jit(solution)/shard_map/cond/branch_1_fun/while/body/eval_jaxpr/frkl,mk->frml/dot_general | solution.py:69
  138.3 6.5 %fusion.108 = f32[3,16,128,2]{2,1,3,0:T(8,128)S(1)} fusion(f32[3,16,2880,2]{2,1,3,0:T(8,128)S(1)} %get-tuple-element.416, s32[128]{0:T(128)S(1)} %iota_add_fusion.3, f32[16,128]{1,0:T(8,128)S(1)} %multiply_multiply_fusion.2), kind=kOutput, calls=%fused_computation.23.clone.1 | convolution fusion | flops 215666688 | bytes 1163776 | tf_op jit(solution)/shard_map/cond/branch_1_fun/while/body/eval_jaxpr/frml,mk->frkl/dot_general | solution.py:65
  151.2 6.4 %fusion.107 = f32[3,16,2880,2]{2,1,3,0:T(8,128)S(1)} fusion(f32[3,16,128,2]{2,1,3,0:T(8,128)S(1)} %fusion.106, f32[3,16,2880,2]{2,1,3,0:T(8,128)S(1)} %get-tuple-element.407, s32[128]{0:T(128)S(1)} %iota_add_fusion.3, pred[]{:T(512)S(6)} %compare.3), kind=kOutput, calls=%fused_computation.4.clone.1 | convolution fusion | flops 216207360 | bytes 2261505 | tf_op jit(solution)/shard_map/cond/branch_1_fun/while/body/eval_jaxpr/frkl,mk->frml/dot_general | solution.py:66
  157.6 6.5 %fusion.109 = f32[3,16,2880,2]{2,1,3,0:T(8,128)S(1)} fusion(f32[3,16,2880,2]{2,1,3,0:T(8,128)S(1)} %fusion.107, f32[3,16,128,2]{2,1,3,0:T(8,128)S(1)} %fusion.108, s32[128]{0:T(128)S(1)} %iota_add_fusion.3), kind=kOutput, calls=%fused_computation.2.clone.1 | convolution fusion | flops 215930880 | bytes 2261504 | tf_op jit(solution)/shard_map/cond/branch_1_fun/while/body/eval_jaxpr/frkl,mk->frml/dot_general | solution.py:69
  164.3 6.5 %fusion.108 = f32[3,16,128,2]{2,1,3,0:T(8,128)S(1)} fusion(f32[3,16,2880,2]{2,1,3,0:T(8,128)S(1)} %get-tuple-element.416, s32[128]{0:T(128)S(1)} %iota_add_fusion.3, f32[16,128]{1,0:T(8,128)S(1)} %multiply_multiply_fusion.2), kind=kOutput, calls=%fused_computation.23.clone.1 | convolution fusion | flops 215666688 | bytes 1163776 | tf_op jit(solution)/shard_map/cond/branch_1_fun/while/body/eval_jaxpr/frml,mk->frkl/dot_general | solution.py:65
  177.1 6.4 %fusion.107 = f32[3,16,2880,2]{2,1,3,0:T(8,128)S(1)} fusion(f32[3,16,128,2]{2,1,3,0:T(8,128)S(1)} %fusion.106, f32[3,16,2880,2]{2,1,3,0:T(8,128)S(1)} %get-tuple-element.407, s32[128]{0:T(128)S(1)} %iota_add_fusion.3, pred[]{:T(512)S(6)} %compare.3), kind=kOutput, calls=%fused_computation.4.clone.1 | convolution fusion | flops 216207360 | bytes 2261505 | tf_op jit(solution)/shard_map/cond/branch_1_fun/while/body/eval_jaxpr/frkl,mk->frml/dot_general | solution.py:66
  183.6 6.5 %fusion.109 = f32[3,16,2880,2]{2,1,3,0:T(8,128)S(1)} fusion(f32[3,16,2880,2]{2,1,3,0:T(8,128)S(1)} %fusion.107, f32[3,16,128,2]{2,1,3,0:T(8,128)S(1)} %fusion.108, s32[128]{0:T(128)S(1)} %iota_add_fusion.3), kind=kOutput, calls=%fused_computation.2.clone.1 | convolution fusion | flops 215930880 | bytes 2261504 | tf_op jit(solution)/shard_map/cond/branch_1_fun/while/body/eval_jaxpr/frkl,mk->frml/dot_general | solution.py:69
  190.2 6.5 %fusion.108 = f32[3,16,128,2]{2,1,3,0:T(8,128)S(1)} fusion(f32[3,16,2880,2]{2,1,3,0:T(8,128)S(1)} %get-tuple-element.416, s32[128]{0:T(128)S(1)} %iota_add_fusion.3, f32[16,128]{1,0:T(8,128)S(1)} %multiply_multiply_fusion.2), kind=kOutput, calls=%fused_computation.23.clone.1 | convolution fusion | flops 215666688 | bytes 1163776 | tf_op jit(solution)/shard_map/cond/branch_1_fun/while/body/eval_jaxpr/frml,mk->frkl/dot_general | solution.py:65
  203.1 6.4 %fusion.107 = f32[3,16,2880,2]{2,1,3,0:T(8,128)S(1)} fusion(f32[3,16,128,2]{2,1,3,0:T(8,128)S(1)} %fusion.106, f32[3,16,2880,2]{2,1,3,0:T(8,128)S(1)} %get-tuple-element.407, s32[128]{0:T(128)S(1)} %iota_add_fusion.3, pred[]{:T(512)S(6)} %compare.3), kind=kOutput, calls=%fused_computation.4.clone.1 | convolution fusion | flops 216207360 | bytes 2261505 | tf_op jit(solution)/shard_map/cond/branch_1_fun/while/body/eval_jaxpr/frkl,mk->frml/dot_general | solution.py:66
  209.5 6.5 %fusion.109 = f32[3,16,2880,2]{2,1,3,0:T(8,128)S(1)} fusion(f32[3,16,2880,2]{2,1,3,0:T(8,128)S(1)} %fusion.107, f32[3,16,128,2]{2,1,3,0:T(8,128)S(1)} %fusion.108, s32[128]{0:T(128)S(1)} %iota_add_fusion.3), kind=kOutput, calls=%fused_computation.2.clone.1 | convolution fusion | flops 215930880 | bytes 2261504 | tf_op jit(solution)/shard_map/cond/branch_1_fun/while/body/eval_jaxpr/frkl,mk->frml/dot_general | solution.py:69
  216.1 6.5 %fusion.108 = f32[3,16,128,2]{2,1,3,0:T(8,128)S(1)} fusion(f32[3,16,2880,2]{2,1,3,0:T(8,128)S(1)} %get-tuple-element.416, s32[128]{0:T(128)S(1)} %iota_add_fusion.3, f32[16,128]{1,0:T(8,128)S(1)} %multiply_multiply_fusion.2), kind=kOutput, calls=%fused_computation.23.clone.1 | convolution fusion | flops 215666688 | bytes 1163776 | tf_op jit(solution)/shard_map/cond/branch_1_fun/while/body/eval_jaxpr/frml,mk->frkl/dot_general | solution.py:65
  229.0 6.4 %fusion.107 = f32[3,16,2880,2]{2,1,3,0:T(8,128)S(1)} fusion(f32[3,16,128,2]{2,1,3,0:T(8,128)S(1)} %fusion.106, f32[3,16,2880,2]{2,1,3,0:T(8,128)S(1)} %get-tuple-element.407, s32[128]{0:T(128)S(1)} %iota_add_fusion.3, pred[]{:T(512)S(6)} %compare.3), kind=kOutput, calls=%fused_computation.4.clone.1 | convolution fusion | flops 216207360 | bytes 2261505 | tf_op jit(solution)/shard_map/cond/branch_1_fun/while/body/eval_jaxpr/frkl,mk->frml/dot_general | solution.py:66
  235.5 6.5 %fusion.109 = f32[3,16,2880,2]{2,1,3,0:T(8,128)S(1)} fusion(f32[3,16,2880,2]{2,1,3,0:T(8,128)S(1)} %fusion.107, f32[3,16,128,2]{2,1,3,0:T(8,128)S(1)} %fusion.108, s32[128]{0:T(128)S(1)} %iota_add_fusion.3), kind=kOutput, calls=%fused_computation.2.clone.1 | convolution fusion | flops 215930880 | bytes 2261504 | tf_op jit(solution)/shard_map/cond/branch_1_fun/while/body/eval_jaxpr/frkl,mk->frml/dot_general | solution.py:69
  242.1 6.5 %fusion.108 = f32[3,16,128,2]{2,1,3,0:T(8,128)S(1)} fusion(f32[3,16,2880,2]{2,1,3,0:T(8,128)S(1)} %get-tuple-element.416, s32[128]{0:T(128)S(1)} %iota_add_fusion.3, f32[16,128]{1,0:T(8,128)S(1)} %multiply_multiply_fusion.2), kind=kOutput, calls=%fused_computation.23.clone.1 | convolution fusion | flops 215666688 | bytes 1163776 | tf_op jit(solution)/shard_map/cond/branch_1_fun/while/body/eval_jaxpr/frml,mk->frkl/dot_general | solution.py:65
  255.0 6.4 %fusion.107 = f32[3,16,2880,2]{2,1,3,0:T(8,128)S(1)} fusion(f32[3,16,128,2]{2,1,3,0:T(8,128)S(1)} %fusion.106, f32[3,16,2880,2]{2,1,3,0:T(8,128)S(1)} %get-tuple-element.407, s32[128]{0:T(128)S(1)} %iota_add_fusion.3, pred[]{:T(512)S(6)} %compare.3), kind=kOutput, calls=%fused_computation.4.clone.1 | convolution fusion | flops 216207360 | bytes 2261505 | tf_op jit(solution)/shard_map/cond/branch_1_fun/while/body/eval_jaxpr/frkl,mk->frml/dot_general | solution.py:66
  261.4 6.5 %fusion.109 = f32[3,16,2880,2]{2,1,3,0:T(8,128)S(1)} fusion(f32[3,16,2880,2]{2,1,3,0:T(8,128)S(1)} %fusion.107, f32[3,16,128,2]{2,1,3,0:T(8,128)S(1)} %fusion.108, s32[128]{0:T(128)S(1)} %iota_add_fusion.3), kind=kOutput, calls=%fused_computation.2.clone.1 | convolution fusion | flops 215930880 | bytes 2261504 | tf_op jit(solution)/shard_map/cond/branch_1_fun/while/body/eval_jaxpr/frkl,mk->frml/dot_general | solution.py:69
  268.0 6.5 %fusion.108 = f32[3,16,128,2]{2,1,3,0:T(8,128)S(1)} fusion(f32[3,16,2880,2]{2,1,3,0:T(8,128)S(1)} %get-tuple-element.416, s32[128]{0:T(128)S(1)} %iota_add_fusion.3, f32[16,128]{1,0:T(8,128)S(1)} %multiply_multiply_fusion.2), kind=kOutput, calls=%fused_computation.23.clone.1 | convolution fusion | flops 215666688 | bytes 1163776 | tf_op jit(solution)/shard_map/cond/branch_1_fun/while/body/eval_jaxpr/frml,mk->frkl/dot_general | solution.py:65
  280.9 6.4 %fusion.107 = f32[3,16,2880,2]{2,1,3,0:T(8,128)S(1)} fusion(f32[3,16,128,2]{2,1,3,0:T(8,128)S(1)} %fusion.106, f32[3,16,2880,2]{2,1,3,0:T(8,128)S(1)} %get-tuple-element.407, s32[128]{0:T(128)S(1)} %iota_add_fusion.3, pred[]{:T(512)S(6)} %compare.3), kind=kOutput, calls=%fused_computation.4.clone.1 | convolution fusion | flops 216207360 | bytes 2261505 | tf_op jit(solution)/shard_map/cond/branch_1_fun/while/body/eval_jaxpr/frkl,mk->frml/dot_general | solution.py:66
  287.4 6.5 %fusion.109 = f32[3,16,2880,2]{2,1,3,0:T(8,128)S(1)} fusion(f32[3,16,2880,2]{2,1,3,0:T(8,128)S(1)} %fusion.107, f32[3,16,128,2]{2,1,3,0:T(8,128)S(1)} %fusion.108, s32[128]{0:T(128)S(1)} %iota_add_fusion.3), kind=kOutput, calls=%fused_computation.2.clone.1 | convolution fusion | flops 215930880 | bytes 2261504 | tf_op jit(solution)/shard_map/cond/branch_1_fun/while/body/eval_jaxpr/frkl,mk->frml/dot_general | solution.py:69
  294.0 6.5 %fusion.108 = f32[3,16,128,2]{2,1,3,0:T(8,128)S(1)} fusion(f32[3,16,2880,2]{2,1,3,0:T(8,128)S(1)} %get-tuple-element.416, s32[128]{0:T(128)S(1)} %iota_add_fusion.3, f32[16,128]{1,0:T(8,128)S(1)} %multiply_multiply_fusion.2), kind=kOutput, calls=%fused_computation.23.clone.1 | convolution fusion | flops 215666688 | bytes 1163776 | tf_op jit(solution)/shard_map/cond/branch_1_fun/while/body/eval_jaxpr/frml,mk->frkl/dot_general | solution.py:65
  306.9 6.4 %fusion.107 = f32[3,16,2880,2]{2,1,3,0:T(8,128)S(1)} fusion(f32[3,16,128,2]{2,1,3,0:T(8,128)S(1)} %fusion.106, f32[3,16,2880,2]{2,1,3,0:T(8,128)S(1)} %get-tuple-element.407, s32[128]{0:T(128)S(1)} %iota_add_fusion.3, pred[]{:T(512)S(6)} %compare.3), kind=kOutput, calls=%fused_computation.4.clone.1 | convolution fusion | flops 216207360 | bytes 2261505 | tf_op jit(solution)/shard_map/cond/branch_1_fun/while/body/eval_jaxpr/frkl,mk->frml/dot_general | solution.py:66
  313.3 6.5 %fusion.109 = f32[3,16,2880,2]{2,1,3,0:T(8,128)S(1)} fusion(f32[3,16,2880,2]{2,1,3,0:T(8,128)S(1)} %fusion.107, f32[3,16,128,2]{2,1,3,0:T(8,128)S(1)} %fusion.108, s32[128]{0:T(128)S(1)} %iota_add_fusion.3), kind=kOutput, calls=%fused_computation.2.clone.1 | convolution fusion | flops 215930880 | bytes 2261504 | tf_op jit(solution)/shard_map/cond/branch_1_fun/while/body/eval_jaxpr/frkl,mk->frml/dot_general | solution.py:69
  319.9 6.5 %fusion.108 = f32[3,16,128,2]{2,1,3,0:T(8,128)S(1)} fusion(f32[3,16,2880,2]{2,1,3,0:T(8,128)S(1)} %get-tuple-element.416, s32[128]{0:T(128)S(1)} %iota_add_fusion.3, f32[16,128]{1,0:T(8,128)S(1)} %multiply_multiply_fusion.2), kind=kOutput, calls=%fused_computation.23.clone.1 | convolution fusion | flops 215666688 | bytes 1163776 | tf_op jit(solution)/shard_map/cond/branch_1_fun/while/body/eval_jaxpr/frml,mk->frkl/dot_general | solution.py:65
  332.8 6.4 %fusion.107 = f32[3,16,2880,2]{2,1,3,0:T(8,128)S(1)} fusion(f32[3,16,128,2]{2,1,3,0:T(8,128)S(1)} %fusion.106, f32[3,16,2880,2]{2,1,3,0:T(8,128)S(1)} %get-tuple-element.407, s32[128]{0:T(128)S(1)} %iota_add_fusion.3, pred[]{:T(512)S(6)} %compare.3), kind=kOutput, calls=%fused_computation.4.clone.1 | convolution fusion | flops 216207360 | bytes 2261505 | tf_op jit(solution)/shard_map/cond/branch_1_fun/while/body/eval_jaxpr/frkl,mk->frml/dot_general | solution.py:66
  339.2 6.5 %fusion.109 = f32[3,16,2880,2]{2,1,3,0:T(8,128)S(1)} fusion(f32[3,16,2880,2]{2,1,3,0:T(8,128)S(1)} %fusion.107, f32[3,16,128,2]{2,1,3,0:T(8,128)S(1)} %fusion.108, s32[128]{0:T(128)S(1)} %iota_add_fusion.3), kind=kOutput, calls=%fused_computation.2.clone.1 | convolution fusion | flops 215930880 | bytes 2261504 | tf_op jit(solution)/shard_map/cond/branch_1_fun/while/body/eval_jaxpr/frkl,mk->frml/dot_general | solution.py:69
  345.9 6.5 %fusion.108 = f32[3,16,128,2]{2,1,3,0:T(8,128)S(1)} fusion(f32[3,16,2880,2]{2,1,3,0:T(8,128)S(1)} %get-tuple-element.416, s32[128]{0:T(128)S(1)} %iota_add_fusion.3, f32[16,128]{1,0:T(8,128)S(1)} %multiply_multiply_fusion.2), kind=kOutput, calls=%fused_computation.23.clone.1 | convolution fusion | flops 215666688 | bytes 1163776 | tf_op jit(solution)/shard_map/cond/branch_1_fun/while/body/eval_jaxpr/frml,mk->frkl/dot_general | solution.py:65
  358.8 6.4 %fusion.107 = f32[3,16,2880,2]{2,1,3,0:T(8,128)S(1)} fusion(f32[3,16,128,2]{2,1,3,0:T(8,128)S(1)} %fusion.106, f32[3,16,2880,2]{2,1,3,0:T(8,128)S(1)} %get-tuple-element.407, s32[128]{0:T(128)S(1)} %iota_add_fusion.3, pred[]{:T(512)S(6)} %compare.3), kind=kOutput, calls=%fused_computation.4.clone.1 | convolution fusion | flops 216207360 | bytes 2261505 | tf_op jit(solution)/shard_map/cond/branch_1_fun/while/body/eval_jaxpr/frkl,mk->frml/dot_general | solution.py:66
  365.2 6.5 %fusion.109 = f32[3,16,2880,2]{2,1,3,0:T(8,128)S(1)} fusion(f32[3,16,2880,2]{2,1,3,0:T(8,128)S(1)} %fusion.107, f32[3,16,128,2]{2,1,3,0:T(8,128)S(1)} %fusion.108, s32[128]{0:T(128)S(1)} %iota_add_fusion.3), kind=kOutput, calls=%fused_computation.2.clone.1 | convolution fusion | flops 215930880 | bytes 2261504 | tf_op jit(solution)/shard_map/cond/branch_1_fun/while/body/eval_jaxpr/frkl,mk->frml/dot_general | solution.py:69
  380.9 7.8 %copy.90 = bf16[3,16,2880,2]{1,3,0,2:T(2,128)(2,1)} copy(bf16[3,16,2880,2]{2,1,3,0:T(8,128)(2,1)S(1)} %get-tuple-element.422) | data formatting | bytes 1105920 | tf_op jit(solution)/shard_map/cond | solution.py:81
  388.7 9.5 %reshape.129 = bf16[64,2,2160]{2,1,0:T(2,128)(2,1)} reshape(bf16[2880,3,2,16]{3,2,1,0:T(2,128)(2,1)} %bitcast.103) | data formatting | bytes 1105920
  398.3 7.2 %all-to-all-start.1 = ((bf16[64,2,2160]{2,1,0:T(2,128)(2,1)}), bf16[64,2,2160]{2,1,0:T(2,128)(2,1)S(1)}, u32[]{:S(2)}, u32[]{:S(2)}) async-start(bf16[64,2,2160]{2,1,0:T(2,128)(2,1)} %reshape.129), calls=%async_computation.1 | async-start | bytes 1114112 | tf_op jit(solution)/shard_map/all_to_all | solution.py:87
  405.8 15.6 %all-to-all-done.1 = bf16[64,2,2160]{2,1,0:T(2,128)(2,1)S(1)} async-done(((bf16[64,2,2160]{2,1,0:T(2,128)(2,1)}), bf16[64,2,2160]{2,1,0:T(2,128)(2,1)S(1)}, u32[]{:S(2)}, u32[]{:S(2)}) %all-to-all-start.1) | async-done | bytes 552992 | tf_op jit(solution)/shard_map/all_to_all | solution.py:87
  426.8 9.3 %copy.92 = bf16[3,16,64,45,2]{2,1,4,3,0:T(8,128)(2,1)S(1)} copy(bf16[3,16,64,45,2]{1,4,0,3,2:T(2,128)(2,1)} %bitcast.101) | data formatting | bytes 1105920 | tf_op jit(solution)/shard_map/all_to_all | solution.py:87
  451.4 9.2 %copy.102 = bf16[3,16,64,45,2]{3,1,4,2,0:T(8,128)(2,1)S(1)} copy(bf16[3,16,64,45,2]{1,4,0,3,2:T(2,128)(2,1)} %bitcast.102) | data formatting | bytes 1105920 | tf_op jit(solution)/shard_map/all_to_all | solution.py:87
  (99 shorter events, 114.6 us)
Async XLA Ops:
  5.7 29.8 %all-to-all-start = ((bf16[64,2,2160]{2,1,0:T(2,128)(2,1)}), bf16[64,2,2160]{2,1,0:T(2,128)(2,1)S(1)}, u32[]{:S(2)}, u32[]{:S(2)}) async-start(bf16[64,2,2160]{2,1,0:T(2,128)(2,1)} %reshape.127), calls=%async_computation | async-start | bytes 1114112 | tf_op jit(solution)/shard_map/all_to_all | solution.py:85
  39.0 2.2 copy-start
  388.7 16.8 %copy-start.1 = (f32[5,16,45,128]{3,1,2,0:T(8,128)S(1)}, f32[5,16,45,128]{3,1,2,0:T(8,128)}, u32[]{:S(2)}) copy-start(f32[5,16,45,128]{3,1,2,0:T(8,128)} %param.11) | copy-start | bytes 5529604
  398.3 23.1 %all-to-all-start.1 = ((bf16[64,2,2160]{2,1,0:T(2,128)(2,1)}), bf16[64,2,2160]{2,1,0:T(2,128)(2,1)S(1)}, u32[]{:S(2)}, u32[]{:S(2)}) async-start(bf16[64,2,2160]{2,1,0:T(2,128)(2,1)} %reshape.129), calls=%async_computation.1 | async-start | bytes 1114112 | tf_op jit(solution)/shard_map/all_to_all | solution.py:87
  445.5 24.7 %collective-permute-start = (bf16[6,16,1,128]{3,1,2,0:T(8,128)(2,1)}, bf16[6,16,1,128]{3,1,2,0:T(8,128)(2,1)S(1)}, u32[]{:S(2)}, u32[]{:S(2)}) collective-permute-start(bf16[6,16,1,128]{3,1,2,0:T(8,128)(2,1)} %get-tuple-element.351), channel_id=1, source_target_pairs={{0,1},{1,2},{2,3},{3,4},{4,5},{5,6},{6,7},{7,8},{8,9},{9,10},{10,1... | collective-permute-start | bytes 73736 | tf_op jit(solution)/shard_map/ppermute | solution.py:18
  445.9 24.3 %collective-permute-start.1 = (bf16[6,16,1,128]{3,1,2,0:T(8,128)(2,1)}, bf16[6,16,1,128]{3,1,2,0:T(8,128)(2,1)}, u32[]{:S(2)}, u32[]{:S(2)}) collective-permute-start(bf16[6,16,1,128]{3,1,2,0:T(8,128)(2,1)} %get-tuple-element.352), channel_id=1, source_target_pairs={{1,0},{2,1},{3,2},{4,3},{5,4},{6,5},{7,6},{8,7},{9,8},{10,9},{11,1... | collective-permute-start | bytes 73736 | tf_op jit(solution)/shard_map/ppermute | solution.py:21
  462.5 8.7 %collective-permute-start.2 = (bf16[6,1,45,128]{3,1,2,0:T(2,128)(2,1)S(1)}, bf16[6,1,45,128]{3,1,2,0:T(2,128)(2,1)S(1)}, u32[]{:S(2)}, u32[]{:S(2)}) collective-permute-start(bf16[6,1,45,128]{3,1,2,0:T(2,128)(2,1)S(1)} %get-tuple-element.353), channel_id=1, source_target_pairs={{0,64},{64,128},{128,192},{1,65},{65,129},{129,193},{2,66},{66,130... | collective-permute-start | bytes 207368 | tf_op jit(solution)/shard_map/ppermute | solution.py:18
  464.4 7.9 %collective-permute-start.3 = (bf16[6,1,45,128]{3,1,2,0:T(2,128)(2,1)S(1)}, bf16[6,1,45,128]{3,1,2,0:T(2,128)(2,1)S(1)}, u32[]{:S(2)}, u32[]{:S(2)}) collective-permute-start(bf16[6,1,45,128]{3,1,2,0:T(2,128)(2,1)S(1)} %get-tuple-element.354), channel_id=1, source_target_pairs={{64,0},{128,64},{192,128},{65,1},{129,65},{193,129},{66,2},{130,66... | collective-permute-start | bytes 207368 | tf_op jit(solution)/shard_map/ppermute | solution.py:21
  473.2 1.5 copy-start.2
  473.2 1.5 copy-start.3
  473.2 1.6 copy-start.4
  473.3 1.7 copy-start.5
where the time goes:
time: 483 us; the launch traced here: 478 us
  matrix products  310 us (64%)
  local copies, waits for them, and re-layouts  60.3 us (12%)
  starting transfers between devices  34.2 us (7%)
  waiting for transfers between devices  32.9 us (7%)
  loops' own time  28 us (6%)
  other arithmetic  11.5 us (2%)
    dot_general x12, matrix products, one_block(): jnp.einsum('frkl,mk->frml', sin_part * weights, sin_table, precision=lax....  77.9 us
    dot_general x12, matrix products, one_block(): jnp.einsum('frml,mk->frkl', row_data, sin_table, precision=lax.Precision....  77.5 us
    dot_general x12, matrix products, one_block(): jnp.einsum('frkl,mk->frml', cos_part * weights, cos_table, precision=lax....  77.2 us
    dot_general x12, matrix products, one_block(): jnp.einsum('frml,mk->frkl', row_data, cos_table, precision=lax.Precision....  77 us
    unnamed x18, local copies, waits for them, and re-layouts  25.6 us
    another operation x1, loops' own time, spectral_rows(): lax.fori_loop(0, block_total, one_block, jnp.zeros_like(row_data))  18.9 us
    all_to_all x2, local copies, waits for them, and re-layouts, polar_filter(): lax.all_to_all(filtered_rows, 'lon', split_axis=2, concat_axis=3, tiled=T...  18.4 us
    all_to_all x1, waiting for transfers between devices, polar_filter(): lax.all_to_all(work_rows, 'lon', split_axis=3, concat_axis=2, tiled=True)  16.2 us
  transfers between devices with their start and end apart: 6, of which 3 were waited for; matrix products, arithmetic and copies ran while one was open for 3% of the time, Pallas kernels for 0%

commit v1 on v0

v1 whole, which is shorter than its diff:
```python
import math

import jax
import jax.numpy as jnp
import numpy as np
from jax import lax
from jax.experimental import pallas as pl
from jax.experimental.pallas import tpu as pltpu
from jax.sharding import PartitionSpec as P

HEMI = 720
KMAX = 180
COEF = 384
SEG = 48
COLS = 9


def trig_tables(lon_count, segments):
    width = lon_count // segments
    k = np.zeros(COEF)
    k[: KMAX + 1] = np.arange(KMAX + 1)
    k[KMAX + 1 : 2 * KMAX + 1] = np.arange(1, KMAX + 1)
    is_cos = np.zeros(COEF, bool)
    is_cos[: KMAX + 1] = True
    used = np.arange(COEF) < 2 * KMAX + 1
    over_p = 2 * np.pi * np.outer(np.arange(segments) * width, k) / lon_count
    over_q = 2 * np.pi * np.outer(np.arange(SEG), k) / lon_count
    p_one = np.where(is_cos, np.cos(over_p), np.sin(over_p)) * used
    p_two = np.where(is_cos, -np.sin(over_p), np.cos(over_p)) * used
    tables = (p_one, p_two, np.cos(over_q), np.sin(over_q))
    return tuple(t.astype(np.float32) for t in tables), k.astype(np.int32), used


def pack_kernel(tend_ref, next_ref, out_ref, wide_ref):
    fields, width, lat_rows, levels = tend_ref.shape
    slots = fields * lat_rows
    pad = out_ref.shape[1] - width
    for f in range(fields):
        wide_ref[...] = tend_ref[f].astype(jnp.float32).reshape(width * lat_rows, levels)
        for r in range(lat_rows):
            row = wide_ref[pl.ds(r, width, stride=lat_rows), :]
            out_ref[f * lat_rows + r, :width] = row.astype(jnp.bfloat16)
            out_ref[f * lat_rows + r, width:] = jnp.zeros((pad, levels), jnp.bfloat16)
    out_ref[slots, :width] = next_ref[...]
    out_ref[slots, width:] = jnp.zeros((pad, levels), jnp.bfloat16)
    for s in range(slots + 1, out_ref.shape[0]):
        out_ref[s] = jnp.zeros(out_ref.shape[1:], jnp.bfloat16)


def transform_kernel(rows_ref, table_ref, weight_ref, out_ref):
    spectrum = lax.dot_general(
        rows_ref[...], table_ref[...], (((0,), (0,)), ((), ())), preferred_element_type=jnp.float32
    )
    weighted = (spectrum * weight_ref[...]).astype(jnp.bfloat16)
    out_ref[...] = lax.dot_general(
        table_ref[...], weighted, (((1,), (1,)), ((), ())), preferred_element_type=jnp.float32
    ).astype(jnp.bfloat16)


def advect_kernel(
    low_ref,
    factor_ref,
    tend_ref,
    wind_ref,
    tracer_ref,
    before_ref,
    high_ref,
    side_ref,
    below_ref,
    top_ref,
    filt_ref,
    out_ref,
    wide_ref,
    north_ref,
    flux_ref,
):
    step = pl.program_id(0)
    block = pl.num_programs(0) - 1 - step
    count, _, lat_rows, levels = tracer_ref.shape
    width = below_ref.shape[1]
    damp, face, face_next, inverse = (factor_ref[i] for i in range(4))
    sublane = lax.broadcasted_iota(jnp.int32, (lat_rows, levels), 0)
    is_first = sublane == 0
    is_last = sublane == lat_rows - 1

    def low_at(f, column):
        start = pl.multiple_of((f * SEG + column) * lat_rows, lat_rows)
        return wide_ref[pl.ds(start, lat_rows), :]

    @pl.when(step == 0)
    def _():
        for f in range(3):
            for r in range(lat_rows):
                wide_ref[pl.ds(f * SEG * lat_rows + r, SEG, stride=lat_rows), :] = low_ref[
                    f * lat_rows + r
                ].astype(jnp.float32)
        filt = (
            factor_ref[4, 0:1] * below_ref[count + 1] + low_ref[3 * lat_rows, :width].astype(jnp.float32)
        ).astype(jnp.bfloat16)
        north_ref[0:width] = 0.25 * jnp.tanh(below_ref[count] + filt.astype(jnp.float32))
        filt = (damp * high_ref[count + 1] + low_at(0, width)).astype(jnp.bfloat16)
        east = 0.5 * jnp.tanh(high_ref[count] + filt.astype(jnp.float32))
        for q in range(count):
            flux_ref[q] = (
                jnp.maximum(east, 0.0) * tracer_ref[q, COLS - 1] + jnp.minimum(east, 0.0) * high_ref[q]
            )

    for local in reversed(range(COLS)):
        column = block * COLS + local
        filtered = []
        for f in range(3):
            value = (damp * tend_ref[f, local].astype(jnp.float32) + low_at(f, column)).astype(
                jnp.bfloat16
            )
            filt_ref[f, local] = value
            filtered.append(value)
        east = 0.5 * jnp.tanh(wind_ref[0, local] + filtered[0].astype(jnp.float32))
        north = 0.25 * jnp.tanh(wind_ref[1, local] + filtered[1].astype(jnp.float32))
        north_next = jnp.where(
            is_last, north_ref[pl.ds(column, 1), :], pltpu.roll(north, lat_rows - 1, 0)
        )
        west_plus = jnp.maximum(east, 0.0)
        west_minus = jnp.minimum(east, 0.0)
        pole_plus = face * jnp.maximum(north, 0.0)
        pole_minus = face * jnp.minimum(north, 0.0)
        next_plus = face_next * jnp.maximum(north_next, 0.0)
        next_minus = face_next * jnp.minimum(north_next, 0.0)
        for q in range(count):
            here = tracer_ref[q, local]
            if local > 0:
                west = tracer_ref[q, local - 1]
            else:
                west = jnp.where(block == 0, side_ref[q], before_ref[q, 0])
            prior = jnp.where(is_first, top_ref[q, pl.ds(column, 1), :], pltpu.roll(here, 1, 0))
            after = jnp.where(
                is_last, below_ref[q, pl.ds(column, 1), :], pltpu.roll(here, lat_rows - 1, 0)
            )
            f_east = flux_ref[q]
            f_west = west_plus * west + west_minus * here
            flux_ref[q] = f_west
            g_pole = pole_plus * prior + pole_minus * here
            g_next = next_plus * here + next_minus * after
            out_ref[q, local] = here - (f_east - f_west) - (g_next - g_pole) * inverse


def per_device(tendencies, bands, winds, tracers):
    fields, lat_rows, width, levels = tendencies.shape
    count = tracers.shape[0]
    lat_devices = lax.axis_size("lat")
    segments = lax.axis_size("lon")
    lat_count = lat_devices * lat_rows
    lon_count = segments * width
    lat_place = lax.axis_index("lat")
    lon_place = lax.axis_index("lon")
    slots = fields * lat_rows
    tendencies, winds, tracers = (a.transpose(0, 2, 1, 3) for a in (tendencies, winds, tracers))

    to_prior = [(i + 1, i) for i in range(lat_devices - 1)]
    to_next = [(i, i + 1) for i in range(lat_devices - 1)]
    west_ring = [((i + 1) % segments, i) for i in range(segments)]
    east_ring = [(i, (i + 1) % segments) for i in range(segments)]

    next_row = lax.ppermute(tendencies[1, :, 0], "lat", to_prior)
    send = pl.pallas_call(
        pack_kernel,
        out_shape=jax.ShapeDtypeStruct((segments, SEG, levels), jnp.bfloat16),
        scratch_shapes=[pltpu.VMEM((width * lat_rows, levels), jnp.float32)],
        name="pack",
    )(tendencies, next_row)
    rows = lax.all_to_all(send, "lon", split_axis=0, concat_axis=0, tiled=True)

    ids = lat_place * lat_rows + jnp.arange(lat_rows + 1, dtype=jnp.int32)
    position = ids.astype(jnp.float32)
    polar = ids < lat_count // 2
    damping = jnp.where(polar, 0.25 + 0.5 * (position + 0.5) / (lat_count / 2.0), 1.0)
    grid_row = position + jnp.float32(HEMI // 2 - lat_count // 2)
    face_cos = jnp.sin(math.pi * grid_row / (2.0 * HEMI))
    centre_cos = jnp.sin(math.pi * (grid_row + 0.5) / (2.0 * HEMI))
    factors = jnp.stack(
        [
            damping[:lat_rows],
            face_cos[:lat_rows],
            face_cos[1:],
            1.0 / centre_cos[:lat_rows],
            jnp.full((lat_rows,), damping[lat_rows]),
        ]
    )
    factors = jnp.broadcast_to(factors[:, :, None], (5, lat_rows, levels))

    (p_one, p_two, q_one, q_two), waves, used = trig_tables(lon_count, segments)
    mine = jnp.where(lon_place < slots, lon_place % lat_rows, lat_rows)
    my_id = lat_place * lat_rows + mine
    my_band = bands[jnp.minimum(my_id, lat_count - 1)]
    fold = jnp.asarray(np.where(used, np.where(waves == 0, 1.0, 2.0), 0.0) / lon_count, jnp.float32)
    weight = jnp.where(jnp.asarray(waves) <= my_band, (1.0 - damping[mine]) * fold, 0.0)[None, :]
    table = (
        jnp.asarray(p_one)[:, None, :] * jnp.asarray(q_one)[None, :, :]
        + jnp.asarray(p_two)[:, None, :] * jnp.asarray(q_two)[None, :, :]
    )
    table = table.astype(jnp.bfloat16).reshape(segments * SEG, COEF)

    high = jnp.concatenate(
        [tracers[:, 0], winds[0:1, 0], tendencies[0:1, 0].astype(jnp.float32)], axis=0
    )
    high = lax.ppermute(high.astype(jnp.bfloat16), "lon", west_ring).astype(jnp.float32)
    side = lax.ppermute(tracers[:, width - 1].astype(jnp.bfloat16), "lon", east_ring)
    side = side.astype(jnp.float32)
    below = jnp.concatenate([tracers[:, :, 0], winds[1:2, :, 0]], axis=0).astype(jnp.bfloat16)
    below = lax.ppermute(below, "lat", to_prior)
    below = jnp.concatenate([below, next_row[None]], axis=0).astype(jnp.float32)
    top = lax.ppermute(tracers[:, :, lat_rows - 1].astype(jnp.bfloat16), "lat", to_next)
    top = top.astype(jnp.float32)

    low = pl.pallas_call(
        transform_kernel,
        out_shape=jax.ShapeDtypeStruct((segments * SEG, levels), jnp.bfloat16),
        name="transform",
    )(rows.reshape(segments * SEG, levels), table, weight)
    low = lax.all_to_all(
        low.reshape(segments, SEG, levels), "lon", split_axis=0, concat_axis=0, tiled=True
    )

    blocks = width // COLS

    def whole(array):
        return pl.BlockSpec(array.shape, lambda i: (0,) * array.ndim)

    def part(size):
        return pl.BlockSpec((size, COLS, lat_rows, levels), lambda i: (0, blocks - 1 - i, 0, 0))

    filtered, advected = pl.pallas_call(
        advect_kernel,
        grid=(blocks,),
        in_specs=[
            whole(low),
            whole(factors),
            part(fields),
            part(2),
            part(count),
            pl.BlockSpec(
                (count, 1, lat_rows, levels),
                lambda i: (0, jnp.maximum((blocks - 1 - i) * COLS - 1, 0), 0, 0),
            ),
            whole(high),
            whole(side),
            whole(below),
            whole(top),
        ],
        out_specs=[part(fields), part(count)],
        out_shape=[
            jax.ShapeDtypeStruct(tendencies.shape, jnp.bfloat16),
            jax.ShapeDtypeStruct(tracers.shape, jnp.float32),
        ],
        scratch_shapes=[
            pltpu.VMEM((fields * SEG * lat_rows, levels), jnp.float32),
            pltpu.VMEM((SEG, levels), jnp.float32),
            pltpu.VMEM((count, lat_rows, levels), jnp.float32),
        ],
        name="advect",
    )(low, factors, tendencies, winds, tracers, tracers, high, side, below, top)
    return (filtered.transpose(0, 2, 1, 3), advected.transpose(0, 2, 1, 3))


def solution(mesh):
    return jax.shard_map(
        per_device,
        mesh=mesh,
        in_specs=(
            P(None, "lat", "lon", None),
            P(),
            P(None, "lat", "lon", None),
            P(None, "lat", "lon", None),
        ),
        out_specs=(P(None, "lat", "lon", None), P(None, "lat", "lon", None)),
        check_vma=False,
    )
```

time: 483 us -> 89.2 us (0.18)
  matrix products: 310 us -> 0 us
  local copies, waits for them, and re-layouts: 60.3 us -> 10.6 us
  loops' own time: 28 us -> 0 us
  waiting for transfers between devices: 32.9 us -> 19.5 us
  Pallas kernels: 0 us -> 13 us
  other arithmetic: 11.5 us -> 6.5 us
    dot_general x48 -> x0, matrix products: 310 us -> none  [the longest x12 77.9 us: one_block(): jnp.einsum('frkl,mk->frml', sin_part * weights, sin_table, precision=lax....]
    another operation x2 -> x0, loops' own time: 28 us -> none  [the longest x1 18.9 us: spectral_rows(): lax.fori_loop(0, block_total, one_block, jnp.zeros_like(row_data))]
    all_to_all x4 -> x0, local copies, waits for them, and re-layouts: 21.2 us -> none  [the longest x2 18.4 us: polar_filter(): lax.all_to_all(filtered_rows, 'lon', split_axis=2, concat_axis=3, tiled=T...]
    unnamed x18 -> x29, local copies, waits for them, and re-layouts: 25.6 us -> 5.6 us
    all_to_all x2, waiting for transfers between devices: 31.8 us -> 13.2 us  [the longest x1 11.1 us: per_device(): rows = lax.all_to_all(send, 'lon', split_axis=0, concat_axis=0, tiled=True)]
    pallas_call x0 -> x3, Pallas kernels: none -> 13 us  [the longest x1 6.45 us: per_device(): pl.pallas_call(advect_kernel, grid=(blocks,), in_specs=[whole(low), whole...]
    cond x1 -> x0, local copies, waits for them, and re-layouts: 7.77 us -> none  [polar_filter(): lax.cond(active, transform, lambda values: values, lax.all_to_all(work_ro...]
    ppermute x4 -> x5, waiting for transfers between devices: 1.09 us -> 6.27 us  [the longest x1 2.29 us: per_device(): next_row = lax.ppermute(tendencies[1, :, 0], 'lat', to_prior)]
  transfers between devices with their start and end apart: 6 -> 7, of which waited for: 3 -> 5; matrix products, arithmetic and copies ran while one was open for 3% -> 13% of each run, Pallas kernels for 0% -> 5%
where the time goes in v1:
time: 89.2 us; the launch traced here: 88.5 us
  starting transfers between devices  37.4 us (42%)
  waiting for transfers between devices  19.5 us (22%)
  Pallas kernels  13 us (15%)
  local copies, waits for them, and re-layouts  10.6 us (12%)
  other arithmetic  6.5 us (7%)
  between operations  1.5 us (2%)
    all_to_all x1, starting transfers between devices, per_device(): rows = lax.all_to_all(send, 'lon', split_axis=0, concat_axis=0, tiled=True)  12.8 us
    all_to_all x1, waiting for transfers between devices, per_device(): rows = lax.all_to_all(send, 'lon', split_axis=0, concat_axis=0, tiled=True)  11.1 us
    pallas_call x1, Pallas kernels, per_device(): pl.pallas_call(advect_kernel, grid=(blocks,), in_specs=[whole(low), whole...  6.45 us
    all_to_all x1, starting transfers between devices, per_device(): lax.all_to_all(low.reshape(segments, SEG, levels), 'lon', split_axis=0, c...  6.1 us
    ppermute x1, starting transfers between devices, per_device(): lax.ppermute(high.astype(jnp.bfloat16), 'lon', west_ring)  5.62 us
    unnamed x29, local copies, waits for them, and re-layouts  5.6 us
    ppermute x1, starting transfers between devices, per_device(): next_row = lax.ppermute(tendencies[1, :, 0], 'lat', to_prior)  5.1 us
    ppermute x1, starting transfers between devices, per_device(): lax.ppermute(tracers[:, :, lat_rows - 1].astype(jnp.bfloat16), 'lat', to_...  4.7 us
  transfers between devices with their start and end apart: 7, of which 5 were waited for; matrix products, arithmetic and copies ran while one was open for 13% of the time, Pallas kernels for 5%

profile of v1, /device:TPU:1, one launch (start us, length us, event | category | flops | bytes accessed | tf_op | source)
XLA Modules:
  0.0 88.5 jit_solution(11900562340314081172)
XLA Ops:
  0.6 0.0 copy-start
  0.6 1.3 %copy.48 = bf16[3,16,45,128]{3,2,1,0:T(8,128)(2,1)S(1)} copy(bf16[3,16,45,128]{3,1,2,0:T(8,128)(2,1)} %param.10) | data formatting | bytes 1105920 | tf_op args[0]
  2.0 0.0 copy-start.5
  2.0 0.8 copy-done.5
  2.8 5.1 %collective-permute-start = (bf16[45,128]{1,0:T(8,128)(2,1)S(1)}, bf16[45,128]{1,0:T(8,128)(2,1)S(1)}, u32[]{:S(2)}, u32[]{:S(2)}) collective-permute-start(bf16[45,128]{1,0:T(8,128)(2,1)S(1)} %slice_bitcast_fusion.3), channel_id=1, source_target_pairs={{64,0},{128,64},{192,128},{65,1},{129,65},{193,129},{66,2},{130,66... | collective-permute-start | bytes 34568 | tf_op jit(solution)/shard_map/ppermute | solution.py:163
  7.9 2.3 %collective-permute-done.next_ref = bf16[45,128]{1,0:T(8,128)(2,1)S(1)} collective-permute-done((bf16[45,128]{1,0:T(8,128)(2,1)S(1)}, bf16[45,128]{1,0:T(8,128)(2,1)S(1)}, u32[]{:S(2)}, u32[]{:S(2)}) %collective-permute-start) | collective-permute-done | bytes 11552 | tf_op jit(solution)/shard_map/ppermute | solution.py:163
  10.2 0.6 copy-done.7
  10.8 2.5 %pack.1 = bf16[64,48,128]{2,1,0:T(8,128)(2,1)} custom-call(bf16[3,45,16,128]{3,2,1,0:T(8,128)(2,1)} %bitcast.52, bf16[45,128]{1,0:T(8,128)(2,1)} %copy-done.7), custom_call_target="tpu_custom_call" | custom-call | tf_op jit(solution)/shard_map/pack/pallas_call | solution.py:164
  13.3 12.8 %all-to-all-start = ((bf16[64,48,128]{2,1,0:T(8,128)(2,1)}), bf16[64,48,128]{2,1,0:T(8,128)(2,1)S(1)}, u32[]{:S(2)}, u32[]{:S(2)}) async-start(bf16[64,48,128]{2,1,0:T(8,128)(2,1)} %pack.1), calls=%async_computation | async-start | bytes 1572864 | tf_op jit(solution)/shard_map/all_to_all | solution.py:170
  26.2 0.0 copy-done
  26.2 0.0 copy-start.6
  26.2 0.6 copy.46
  26.8 0.0 copy-start.4
  26.8 0.9 %copy-done.4 = bf16[5,16,45,128]{3,2,0,1:T(8,128)(2,1)} copy-done((bf16[5,16,45,128]{3,2,0,1:T(8,128)(2,1)}, bf16[5,16,45,128]{3,2,0,1:T(8,128)(2,1)S(1)}, u32[]{:S(2)}) %copy-start.4) | copy-done | bytes 921624
  27.8 0.1 fusion
  27.8 1.1 %collective-permute-start.2 = (bf16[5,16,128]{2,1,0:T(8,128)(2,1)S(1)}, bf16[5,16,128]{2,1,0:T(8,128)(2,1)S(1)}, u32[]{:S(2)}, u32[]{:S(2)}) collective-permute-start(bf16[5,16,128]{2,1,0:T(8,128)(2,1)S(1)} %bitcast.65), channel_id=1, source_target_pairs={{0,1},{1,2},{2,3},{3,4},{4,5},{5,6},{6,7},{7,8},{8,9},{9,10},{10,1... | collective-permute-start | bytes 61448 | tf_op jit(solution)/shard_map/ppermute | solution.py:206
  28.9 0.8 slice.61
  29.7 0.0 copy-done.11
  29.7 0.6 dynamic_slice.6
  30.3 0.6 fusion.1
  31.6 0.6 multiply_select_fusion
  32.2 0.6 broadcast_in_dim.26.weight_ref
  32.8 0.0 copy-done.3
  32.8 0.2 copy.47
  33.1 3.2 %add_convert_fusion = bf16[64,48,384]{2,1,0:T(8,128)(2,1)} fusion(f32[48,384]{1,0:T(8,128)} %constant.76.clone, f32[64,384]{1,0:T(8,128)S(1)} %copy-done.6, f32[48,384]{1,0:T(8,128)} %constant.74.clone, f32[64,384]{1,0:T(8,128)} %constant.73.clone), kind=kLoop, calls=%fused_computation | loop fusion | flops 4718592 | bytes 2703360 | tf_op jit(solution)/shard_map/convert_element_type | solution.py:200
  36.3 11.1 %all-to-all-done = bf16[64,48,128]{2,1,0:T(8,128)(2,1)S(1)} async-done(((bf16[64,48,128]{2,1,0:T(8,128)(2,1)}), bf16[64,48,128]{2,1,0:T(8,128)(2,1)S(1)}, u32[]{:S(2)}, u32[]{:S(2)}) %all-to-all-start) | async-done | bytes 786464 | tf_op jit(solution)/shard_map/all_to_all | solution.py:170
  47.4 0.9 copy-done.1
  48.3 4.1 %transform.1 = bf16[3072,128]{1,0:T(8,128)(2,1)} custom-call(bf16[3072,128]{1,0:T(8,128)(2,1)} %bitcast.54, bf16[3072,384]{1,0:T(8,128)(2,1)} %bitcast.51, f32[1,384]{1,0:T(1,128)} %broadcast_in_dim.26.weight_ref), custom_call_target="tpu_custom_call" | custom-call | tf_op jit(solution)/shard_map/transform/pallas_call | solution.py:214
  52.4 6.1 %all-to-all-start.1 = ((bf16[64,48,128]{2,1,0:T(8,128)(2,1)}), bf16[64,48,128]{2,1,0:T(8,128)(2,1)S(1)}, u32[]{:S(2)}, u32[]{:S(2)}) async-start(bf16[64,48,128]{2,1,0:T(8,128)(2,1)} %bitcast.55), calls=%async_computation.1 | async-start | bytes 1572864 | tf_op jit(solution)/shard_map/all_to_all | solution.py:219
  58.5 5.6 %collective-permute-start.1 = (bf16[7,16,128]{2,1,0:T(8,128)(2,1)S(1)}, bf16[7,16,128]{2,1,0:T(8,128)(2,1)S(1)}, u32[]{:S(2)}, u32[]{:S(2)}) collective-permute-start(bf16[7,16,128]{2,1,0:T(8,128)(2,1)S(1)} %pad_maximum_fusion.1), channel_id=1, source_target_pairs={{1,0},{2,1},{3,2},{4,3},{5,4},{6,5},{7,6},{8,7},{9,8},{10,9},{11,1... | collective-permute-start | bytes 86024 | tf_op jit(solution)/shard_map/ppermute | solution.py:205
  64.1 0.9 slice_bitcast_fusion
  65.0 4.7 %collective-permute-start.4 = (bf16[5,45,128]{2,1,0:T(8,128)(2,1)S(1)}, bf16[5,45,128]{2,1,0:T(8,128)(2,1)S(1)}, u32[]{:S(2)}, u32[]{:S(2)}) collective-permute-start(bf16[5,45,128]{2,1,0:T(8,128)(2,1)S(1)} %get-tuple-element.6), channel_id=1, source_target_pairs={{0,64},{64,128},{128,192},{1,65},{65,129},{129,193},{2,66},{66,130... | collective-permute-start | bytes 172808 | tf_op jit(solution)/shard_map/ppermute | solution.py:211
  69.7 1.9 %collective-permute-start.3 = (bf16[6,45,128]{2,1,0:T(8,128)(2,1)S(1)}, bf16[6,45,128]{2,1,0:T(8,128)(2,1)S(1)}, u32[]{:S(2)}, u32[]{:S(2)}) collective-permute-start(bf16[6,45,128]{2,1,0:T(8,128)(2,1)S(1)} %pad_maximum_fusion), channel_id=1, source_target_pairs={{64,0},{128,64},{192,128},{65,1},{129,65},{193,129},{66,2},{130,66... | collective-permute-start | bytes 207368 | tf_op jit(solution)/shard_map/ppermute | solution.py:209
  71.7 0.1 slice_bitcast_fusion.4
  71.8 0.6 stack_broadcast_in_dim.3
  72.4 0.0 collective-permute-done.2
  72.4 0.6 convert_element_type.50.side_ref
  73.0 1.9 %collective-permute-done.1 = bf16[7,16,128]{2,1,0:T(8,128)(2,1)S(1)} collective-permute-done((bf16[7,16,128]{2,1,0:T(8,128)(2,1)S(1)}, bf16[7,16,128]{2,1,0:T(8,128)(2,1)S(1)}, u32[]{:S(2)}, u32[]{:S(2)}) %collective-permute-start.1) | collective-permute-done | bytes 28704 | tf_op jit(solution)/shard_map/ppermute | solution.py:205
  74.9 0.6 convert_element_type.48.high_ref
  75.6 0.0 collective-permute-done.4
  75.6 0.7 convert_element_type.53.top_ref
  76.2 2.1 %collective-permute-done.3 = bf16[6,45,128]{2,1,0:T(8,128)(2,1)S(1)} collective-permute-done((bf16[6,45,128]{2,1,0:T(8,128)(2,1)S(1)}, bf16[6,45,128]{2,1,0:T(8,128)(2,1)S(1)}, u32[]{:S(2)}, u32[]{:S(2)}) %collective-permute-start.3) | collective-permute-done | bytes 69152 | tf_op jit(solution)/shard_map/ppermute | solution.py:209
  78.3 0.0 copy-done.8
  78.3 0.7 maximum_convert_fusion.below_ref
  79.0 2.1 %all-to-all-done.1.low_ref = bf16[64,48,128]{2,1,0:T(8,128)(2,1)S(1)} async-done(((bf16[64,48,128]{2,1,0:T(8,128)(2,1)}), bf16[64,48,128]{2,1,0:T(8,128)(2,1)S(1)}, u32[]{:S(2)}, u32[]{:S(2)}) %all-to-all-start.1) | async-done | bytes 786464 | tf_op jit(solution)/shard_map/all_to_all | solution.py:219
  81.1 0.8 broadcast_in_dim.27.factor_ref
  82.0 0.1 copy-done.2
  82.0 6.4 %advect.1 = (bf16[3,45,16,128]{3,2,1,0:T(8,128)(2,1)}, f32[5,45,16,128]{3,2,1,0:T(8,128)}) custom-call(bf16[64,48,128]{2,1,0:T(8,128)(2,1)} %copy-done.2, f32[5,16,128]{2,1,0:T(8,128)} %broadcast_in_dim.27.factor_ref, bf16[3,45,16,128]{3,2,1,0:T(8,128)(2,1)} %bitcast.53, f32[2,45,16,128]{3,2,1,0:T(8,128)} %bitcast.56, f32[5,45,16,128]{3,2,1,0:T(8,128)} %bitcast.49, ...), custom_call_target="tpu_custom_call" | custom-call | tf_op jit(solution)/shard_map/advect/pallas_call | solution.py:231
  (25 shorter events, 0.2 us)
Async XLA Ops:
  0.6 25.5 %copy-start = (f32[5,16,45,128]{3,1,2,0:T(8,128)S(1)}, f32[5,16,45,128]{3,1,2,0:T(8,128)}, u32[]{:S(2)}) copy-start(f32[5,16,45,128]{3,1,2,0:T(8,128)} %param.13) | copy-start | bytes 5529604
  2.0 0.9 copy-start.5
  2.8 7.4 %collective-permute-start = (bf16[45,128]{1,0:T(8,128)(2,1)S(1)}, bf16[45,128]{1,0:T(8,128)(2,1)S(1)}, u32[]{:S(2)}, u32[]{:S(2)}) collective-permute-start(bf16[45,128]{1,0:T(8,128)(2,1)S(1)} %slice_bitcast_fusion.3), channel_id=1, source_target_pairs={{64,0},{128,64},{192,128},{65,1},{129,65},{193,129},{66,2},{130,66... | collective-permute-start | bytes 34568 | tf_op jit(solution)/shard_map/ppermute | solution.py:163
  10.2 0.6 copy-start.7
  13.3 16.4 %copy-start.11 = (s32[64]{0:T(128)S(1)}, s32[64]{0:T(128)}, u32[]{:S(2)}) copy-start(s32[64]{0:T(128)} %param.11) | copy-start | bytes 772
  13.3 18.3 %copy-start.9 = (s32[384]{0:T(512)S(1)}, s32[384]{0:T(512)}, u32[]{:S(2)}) copy-start(s32[384]{0:T(512)} %constant.72.clone) | copy-start | bytes 4612
  13.3 18.3 %copy-start.10 = (f32[384]{0:T(512)S(1)}, f32[384]{0:T(512)}, u32[]{:S(2)}) copy-start(f32[384]{0:T(512)} %constant.71.clone) | copy-start | bytes 4612
  13.3 19.5 %copy-start.3 = (f32[2,16,45,128]{3,1,2,0:T(8,128)S(1)}, f32[2,16,45,128]{3,1,2,0:T(8,128)}, u32[]{:S(2)}) copy-start(f32[2,16,45,128]{3,1,2,0:T(8,128)} %param.12) | copy-start | bytes 2211844
  13.3 34.1 %all-to-all-start = ((bf16[64,48,128]{2,1,0:T(8,128)(2,1)}), bf16[64,48,128]{2,1,0:T(8,128)(2,1)S(1)}, u32[]{:S(2)}, u32[]{:S(2)}) async-start(bf16[64,48,128]{2,1,0:T(8,128)(2,1)} %pack.1), calls=%async_computation | async-start | bytes 1572864 | tf_op jit(solution)/shard_map/all_to_all | solution.py:170
  26.2 6.9 %copy-start.6 = (f32[64,384]{1,0:T(8,128)S(1)}, f32[64,384]{1,0:T(8,128)}, u32[]{:S(2)}) copy-start(f32[64,384]{1,0:T(8,128)} %constant.75.clone) | copy-start | bytes 294916
  26.8 0.9 %copy-start.4 = (bf16[5,16,45,128]{3,2,0,1:T(8,128)(2,1)}, bf16[5,16,45,128]{3,2,0,1:T(8,128)(2,1)S(1)}, u32[]{:S(2)}) copy-start(bf16[5,16,45,128]{3,2,0,1:T(8,128)(2,1)S(1)} %copy.46) | copy-start | bytes 2764804
  27.8 44.6 %collective-permute-start.2 = (bf16[5,16,128]{2,1,0:T(8,128)(2,1)S(1)}, bf16[5,16,128]{2,1,0:T(8,128)(2,1)S(1)}, u32[]{:S(2)}, u32[]{:S(2)}) collective-permute-start(bf16[5,16,128]{2,1,0:T(8,128)(2,1)S(1)} %bitcast.65), channel_id=1, source_target_pairs={{0,1},{1,2},{2,3},{3,4},{4,5},{5,6},{6,7},{7,8},{8,9},{9,10},{10,1... | collective-permute-start | bytes 61448 | tf_op jit(solution)/shard_map/ppermute | solution.py:206
  47.4 0.9 %copy-start.1 = (bf16[64,48,128]{2,1,0:T(8,128)(2,1)}, bf16[64,48,128]{2,1,0:T(8,128)(2,1)S(1)}, u32[]{:S(2)}) copy-start(bf16[64,48,128]{2,1,0:T(8,128)(2,1)S(1)} %all-to-all-done) | copy-start | bytes 2359300
  48.3 30.0 %copy-start.8 = (bf16[45,128]{1,0:T(8,128)(2,1)S(1)}, bf16[45,128]{1,0:T(8,128)(2,1)}, u32[]{:S(2)}) copy-start(bf16[45,128]{1,0:T(8,128)(2,1)} %copy-done.7) | copy-start | bytes 34564
  52.4 28.8 %all-to-all-start.1 = ((bf16[64,48,128]{2,1,0:T(8,128)(2,1)}), bf16[64,48,128]{2,1,0:T(8,128)(2,1)S(1)}, u32[]{:S(2)}, u32[]{:S(2)}) async-start(bf16[64,48,128]{2,1,0:T(8,128)(2,1)} %bitcast.55), calls=%async_computation.1 | async-start | bytes 1572864 | tf_op jit(solution)/shard_map/all_to_all | solution.py:219
  58.5 16.4 %collective-permute-start.1 = (bf16[7,16,128]{2,1,0:T(8,128)(2,1)S(1)}, bf16[7,16,128]{2,1,0:T(8,128)(2,1)S(1)}, u32[]{:S(2)}, u32[]{:S(2)}) collective-permute-start(bf16[7,16,128]{2,1,0:T(8,128)(2,1)S(1)} %pad_maximum_fusion.1), channel_id=1, source_target_pairs={{1,0},{2,1},{3,2},{4,3},{5,4},{6,5},{7,6},{8,7},{9,8},{10,9},{11,1... | collective-permute-start | bytes 86024 | tf_op jit(solution)/shard_map/ppermute | solution.py:205
  65.0 10.6 %collective-permute-start.4 = (bf16[5,45,128]{2,1,0:T(8,128)(2,1)S(1)}, bf16[5,45,128]{2,1,0:T(8,128)(2,1)S(1)}, u32[]{:S(2)}, u32[]{:S(2)}) collective-permute-start(bf16[5,45,128]{2,1,0:T(8,128)(2,1)S(1)} %get-tuple-element.6), channel_id=1, source_target_pairs={{0,64},{64,128},{128,192},{1,65},{65,129},{129,193},{2,66},{66,130... | collective-permute-start | bytes 172808 | tf_op jit(solution)/shard_map/ppermute | solution.py:211
  69.7 8.6 %collective-permute-start.3 = (bf16[6,45,128]{2,1,0:T(8,128)(2,1)S(1)}, bf16[6,45,128]{2,1,0:T(8,128)(2,1)S(1)}, u32[]{:S(2)}, u32[]{:S(2)}) collective-permute-start(bf16[6,45,128]{2,1,0:T(8,128)(2,1)S(1)} %pad_maximum_fusion), channel_id=1, source_target_pairs={{64,0},{128,64},{192,128},{65,1},{129,65},{193,129},{66,2},{130,66... | collective-permute-start | bytes 207368 | tf_op jit(solution)/shard_map/ppermute | solution.py:209
  81.1 0.9 %copy-start.2 = (bf16[64,48,128]{2,1,0:T(8,128)(2,1)}, bf16[64,48,128]{2,1,0:T(8,128)(2,1)S(1)}, u32[]{:S(2)}) copy-start(bf16[64,48,128]{2,1,0:T(8,128)(2,1)S(1)} %all-to-all-done.1.low_ref) | copy-start | bytes 2359300

commit v2 on v1

v2 whole, which is shorter than its diff:
```python
import math

import jax
import jax.numpy as jnp
import numpy as np
from jax import lax
from jax.experimental import pallas as pl
from jax.experimental.pallas import tpu as pltpu
from jax.sharding import PartitionSpec as P

HEMI = 720
KMAX = 180
COEF = 384
SEG = 48
LIMIT = 24 << 20
CHUNKS = 4
COLS = 9


def trig_tables(lon_count, segments):
    width = lon_count // segments
    k = np.zeros(COEF)
    k[: KMAX + 1] = np.arange(KMAX + 1)
    k[KMAX + 1 : 2 * KMAX + 1] = np.arange(1, KMAX + 1)
    is_cos = np.zeros(COEF, bool)
    is_cos[: KMAX + 1] = True
    used = np.arange(COEF) < 2 * KMAX + 1
    over_p = 2 * np.pi * np.outer(np.arange(segments) * width, k) / lon_count
    over_q = 2 * np.pi * np.outer(np.arange(SEG), k) / lon_count
    p_one = np.where(is_cos, np.cos(over_p), np.sin(over_p)) * used
    p_two = np.where(is_cos, -np.sin(over_p), np.cos(over_p)) * used
    tables = (p_one, p_two, np.cos(over_q), np.sin(over_q))
    return tuple(t.astype(np.float32) for t in tables), k.astype(np.int32), used


def pack_kernel(tend_ref, out_ref, tend, wide, rows, in_sems, out_sems):
    fields, width, lat_rows, levels = tend.shape
    pad = rows.shape[1] - width
    loads = [pltpu.make_async_copy(tend_ref.at[f], tend.at[f], in_sems.at[f]) for f in range(fields)]
    for load in loads:
        load.start()
    stores = []
    blocks = rows.shape[0] // lat_rows
    for f in reversed(range(blocks)):
        part = pl.ds(f * lat_rows, lat_rows)
        if f < fields:
            loads[f].wait()
            wide[f] = tend[f].astype(jnp.float32).reshape(width * lat_rows, levels)
            for r in range(lat_rows):
                row = wide[f, pl.ds(r, width, stride=lat_rows), :]
                rows[f * lat_rows + r, :width] = row.astype(jnp.bfloat16)
                rows[f * lat_rows + r, width:] = jnp.zeros((pad, levels), jnp.bfloat16)
        else:
            rows[part] = jnp.zeros((lat_rows,) + rows.shape[1:], jnp.bfloat16)
        store = pltpu.make_async_copy(rows.at[part], out_ref.at[part], out_sems.at[f])
        store.start()
        stores.append(store)
    for store in stores:
        store.wait()


def transform_kernel(
    place_ref, bands_ref, waves_ref, fold_ref, rows_ref, table_ref, out_ref, table, result, in_sems, out_sems
):
    row, half = place_ref[0], place_ref[1]
    damp = jnp.where(row < half, 0.25 + 0.5 * (row.astype(jnp.float32) + 0.5) / half.astype(jnp.float32), 1.0)
    weight = jnp.where(waves_ref[...] <= bands_ref[row], (1.0 - damp) * fold_ref[...], 0.0)
    size = table.shape[0] // CHUNKS

    def part(i):
        return pl.ds(i * size, size)

    loads = [
        pltpu.make_async_copy(table_ref.at[part(i)], table.at[part(i)], in_sems.at[i])
        for i in range(CHUNKS)
    ]
    stores = [
        pltpu.make_async_copy(result.at[part(i)], out_ref.at[part(i)], out_sems.at[i])
        for i in range(CHUNKS)
    ]
    for load in loads:
        load.start()
    spectrum = 0.0
    for i in range(CHUNKS):
        loads[i].wait()
        spectrum += lax.dot_general(
            rows_ref[part(i)],
            table[part(i)],
            (((0,), (0,)), ((), ())),
            preferred_element_type=jnp.float32,
        )
    weighted = (spectrum * weight).astype(jnp.bfloat16)
    for i in range(CHUNKS):
        result[part(i)] = lax.dot_general(
            table[part(i)], weighted, (((1,), (1,)), ((), ())), preferred_element_type=jnp.float32
        ).astype(jnp.bfloat16)
        stores[i].start()
    for store in stores:
        store.wait()


def filter_kernel(place_ref, low_ref, factor_ref, tend_ref, high_ref, filt_ref, edge_ref, wide_ref):
    fields, width, lat_rows, levels = tend_ref.shape
    damp = factor_ref[place_ref[2], 0]
    for f in range(fields):
        for r in range(lat_rows):
            wide_ref[f, pl.ds(r, SEG, stride=lat_rows), :] = low_ref[f * lat_rows + r].astype(jnp.float32)
        if f == 0:
            filt = damp * high_ref[high_ref.shape[0] - 1].astype(jnp.float32)
            filt += wide_ref[f, width * lat_rows : (width + 1) * lat_rows]
            filt = filt.astype(jnp.bfloat16).astype(jnp.float32)
            edge_ref[...] = 0.5 * jnp.tanh(high_ref[high_ref.shape[0] - 2].astype(jnp.float32) + filt)
        low = wide_ref[f, : width * lat_rows].reshape(width, lat_rows, levels)
        filt_ref[f] = (damp[None] * tend_ref[f].astype(jnp.float32) + low).astype(jnp.bfloat16)


def advect_kernel(
    place_ref,
    filt_ref,
    factor_ref,
    wind_ref,
    tracer_ref,
    before_ref,
    edge_ref,
    high_ref,
    side_ref,
    below_ref,
    top_ref,
    next_low_ref,
    out_ref,
    north_ref,
    flux_ref,
    below_wide,
    top_wide,
):
    step = pl.program_id(0)
    block = pl.num_programs(0) - 1 - step
    count, _, lat_rows, levels = tracer_ref.shape
    width = below_ref.shape[1]
    lat = place_ref[2]
    _, face, face_next, inverse = (factor_ref[lat, i] for i in range(4))
    sublane = lax.broadcasted_iota(jnp.int32, (lat_rows, levels), 0)
    is_first = sublane == 0
    is_last = sublane == lat_rows - 1

    @pl.when(step == 0)
    def _():
        below_wide[:, :width] = below_ref[...].astype(jnp.float32)
        top_wide[:, :width] = top_ref[...].astype(jnp.float32)
        filt = factor_ref[lat, 4, 0:1] * below_wide[count + 1, :width]
        filt = (filt + next_low_ref[:width].astype(jnp.float32)).astype(jnp.bfloat16)
        north_ref[:width] = 0.25 * jnp.tanh(below_wide[count, :width] + filt.astype(jnp.float32))
        east = edge_ref[...]
        for q in range(count):
            flux_ref[q] = jnp.maximum(east, 0.0) * tracer_ref[q, COLS - 1] + jnp.minimum(
                east, 0.0
            ) * high_ref[q].astype(jnp.float32)

    for local in reversed(range(COLS)):
        column = block * COLS + local
        east = 0.5 * jnp.tanh(wind_ref[0, local] + filt_ref[0, local].astype(jnp.float32))
        north = 0.25 * jnp.tanh(wind_ref[1, local] + filt_ref[1, local].astype(jnp.float32))
        north_next = jnp.where(
            is_last, north_ref[pl.ds(column, 1), :], pltpu.roll(north, lat_rows - 1, 0)
        )
        west_plus = jnp.maximum(east, 0.0)
        west_minus = jnp.minimum(east, 0.0)
        pole_plus = face * jnp.maximum(north, 0.0)
        pole_minus = face * jnp.minimum(north, 0.0)
        next_plus = face_next * jnp.maximum(north_next, 0.0)
        next_minus = face_next * jnp.minimum(north_next, 0.0)
        for q in range(count):
            here = tracer_ref[q, local]
            if local > 0:
                west = tracer_ref[q, local - 1]
            else:
                west = jnp.where(block == 0, side_ref[q].astype(jnp.float32), before_ref[q, 0])
            prior = jnp.where(is_first, top_wide[q, pl.ds(column, 1), :], pltpu.roll(here, 1, 0))
            after = jnp.where(
                is_last, below_wide[q, pl.ds(column, 1), :], pltpu.roll(here, lat_rows - 1, 0)
            )
            f_east = flux_ref[q]
            f_west = west_plus * west + west_minus * here
            flux_ref[q] = f_west
            g_pole = pole_plus * prior + pole_minus * here
            g_next = next_plus * here + next_minus * after
            out_ref[q, local] = here - (f_east - f_west) - (g_next - g_pole) * inverse


def row_factors(lat_devices, lat_rows, levels):
    ids = np.arange(lat_devices * lat_rows + 1)
    half = lat_devices * lat_rows // 2
    damping = np.where(ids < half, 0.25 + 0.5 * (ids + 0.5) / half, 1.0)
    grid_row = ids + HEMI // 2 - half
    face = np.sin(math.pi * grid_row / (2.0 * HEMI))
    centre = np.sin(math.pi * (grid_row + 0.5) / (2.0 * HEMI))
    rows = np.stack(
        [damping[:-1], face[:-1], face[1:], 1.0 / centre[:-1], np.repeat(damping[lat_rows::lat_rows], lat_rows)]
    )
    rows = rows.reshape(5, lat_devices, lat_rows).swapaxes(0, 1).astype(np.float32)
    return np.broadcast_to(rows[..., None], rows.shape + (levels,))


def in_vmem(array):
    return pltpu.with_memory_space_constraint(array, pltpu.VMEM)


def in_hbm(array):
    return pltpu.with_memory_space_constraint(array, pltpu.HBM)


def per_device(tendencies, bands, winds, tracers):
    fields, lat_rows, width, levels = tendencies.shape
    count = tracers.shape[0]
    lat_devices = lax.axis_size("lat")
    segments = lax.axis_size("lon")
    lat_place = lax.axis_index("lat")
    lon_place = lax.axis_index("lon")
    tendencies, winds, tracers = (a.transpose(0, 2, 1, 3) for a in (tendencies, winds, tracers))

    to_prior = [(i + 1, i) for i in range(lat_devices - 1)]
    to_next = [(i, i + 1) for i in range(lat_devices - 1)]
    west_ring = [((i + 1) % segments, i) for i in range(segments)]
    east_ring = [(i, (i + 1) % segments) for i in range(segments)]
    vmem = pl.BlockSpec(memory_space=pltpu.VMEM)
    smem = pl.BlockSpec(memory_space=pltpu.SMEM)
    hbm = pl.BlockSpec(memory_space=pltpu.HBM)
    params = pltpu.CompilerParams(vmem_limit_bytes=LIMIT)
    bf16 = jnp.bfloat16

    send = pl.pallas_call(
        pack_kernel,
        in_specs=[hbm],
        out_specs=hbm,
        out_shape=pltpu.HBM((segments, SEG, levels), bf16),
        scratch_shapes=[
            pltpu.VMEM(tendencies.shape, bf16),
            pltpu.VMEM((fields, width * lat_rows, levels), jnp.float32),
            pltpu.VMEM((segments, SEG, levels), bf16),
            pltpu.SemaphoreType.DMA((fields,)),
            pltpu.SemaphoreType.DMA((segments // lat_rows,)),
        ],
        compiler_params=params,
        name="pack",
    )(in_hbm(tendencies))
    with jax.named_scope("forth"):
        rows = lax.all_to_all(send, "lon", split_axis=0, concat_axis=0, tiled=True)

    factors = jnp.asarray(row_factors(lat_devices, lat_rows, levels))
    place = jnp.stack(
        [
            lat_place * lat_rows + lon_place % lat_rows,
            jnp.int32(lat_devices * lat_rows // 2),
            lat_place,
        ]
    )
    (p_one, p_two, q_one, q_two), waves, used = trig_tables(segments * width, segments)
    fold = np.where(used, np.where(waves == 0, 1.0, 2.0), 0.0) / (segments * width)
    with jax.named_scope("table"):
        table = (
            jnp.asarray(p_one)[:, None, :] * jnp.asarray(q_one)[None, :, :]
            + jnp.asarray(p_two)[:, None, :] * jnp.asarray(q_two)[None, :, :]
        )
        table = table.astype(bf16).reshape(segments * SEG, COEF)

    with jax.named_scope("edges"):
        high = jnp.concatenate(
            [tracers[:, 0].astype(bf16), winds[0:1, 0].astype(bf16), tendencies[0:1, 0]], axis=0
        )
        side = tracers[:, width - 1].astype(bf16)
        below = jnp.concatenate(
            [tracers[:, :, 0].astype(bf16), winds[1:2, :, 0].astype(bf16), tendencies[1:2, :, 0]], axis=0
        )
        top = tracers[:, :, lat_rows - 1].astype(bf16)
    with jax.named_scope("columns"):
        high = lax.ppermute(high, "lon", west_ring)
        side = lax.ppermute(side, "lon", east_ring)
    rows, table, factors, high, side, below, top = lax.optimization_barrier(
        (rows, table, factors, high, side, below, top)
    )

    low = pl.pallas_call(
        transform_kernel,
        in_specs=[smem, smem, vmem, vmem, vmem, hbm],
        out_specs=hbm,
        out_shape=pltpu.HBM((segments * SEG, levels), bf16),
        scratch_shapes=[
            pltpu.VMEM((segments * SEG, COEF), bf16),
            pltpu.VMEM((segments * SEG, levels), bf16),
            pltpu.SemaphoreType.DMA((CHUNKS,)),
            pltpu.SemaphoreType.DMA((CHUNKS,)),
        ],
        compiler_params=params,
        name="transform",
    )(
        place,
        bands,
        jnp.asarray(waves)[None],
        jnp.asarray(fold, jnp.float32)[None],
        in_vmem(rows.reshape(segments * SEG, levels)),
        in_hbm(table),
    )
    low, below, top = lax.optimization_barrier((low, below, top))
    with jax.named_scope("back"):
        low = lax.all_to_all(
            low.reshape(segments, SEG, levels), "lon", split_axis=0, concat_axis=0, tiled=True
        )
    with jax.named_scope("below"):
        below = lax.ppermute(below, "lat", to_prior)
    with jax.named_scope("top"):
        top = lax.ppermute(top, "lat", to_next)
    next_low = lax.ppermute(low[lat_rows], "lat", to_prior[: lat_devices // 2 - 1])

    filtered, edge = pl.pallas_call(
        filter_kernel,
        in_specs=[smem] + [vmem] * 4,
        out_specs=[vmem] * 2,
        out_shape=[
            jax.ShapeDtypeStruct(tendencies.shape, bf16),
            jax.ShapeDtypeStruct((lat_rows, levels), jnp.float32),
        ],
        scratch_shapes=[pltpu.VMEM((fields, SEG * lat_rows, levels), jnp.float32)],
        compiler_params=params,
        name="filter",
    )(place, in_vmem(low), in_vmem(factors), in_vmem(tendencies), in_vmem(high))

    blocks = width // COLS

    def whole(array):
        return pl.BlockSpec(array.shape, lambda i: (0,) * array.ndim)

    def part(size):
        return pl.BlockSpec((size, COLS, lat_rows, levels), lambda i: (0, blocks - 1 - i, 0, 0))

    advected = pl.pallas_call(
        advect_kernel,
        grid=(blocks,),
        in_specs=[
            smem,
            part(2),
            whole(factors),
            part(2),
            part(count),
            pl.BlockSpec(
                (count, 1, lat_rows, levels),
                lambda i: (0, jnp.maximum((blocks - 1 - i) * COLS - 1, 0), 0, 0),
            ),
            whole(edge),
            whole(high),
            whole(side),
            whole(below),
            whole(top),
            whole(next_low),
        ],
        out_specs=part(count),
        out_shape=jax.ShapeDtypeStruct(tracers.shape, jnp.float32),
        scratch_shapes=[
            pltpu.VMEM((SEG, levels), jnp.float32),
            pltpu.VMEM((count, lat_rows, levels), jnp.float32),
            pltpu.VMEM((count + 2, SEG, levels), jnp.float32),
            pltpu.VMEM((count, SEG, levels), jnp.float32),
        ],
        compiler_params=params,
        name="advect",
    )(
        place,
        in_hbm(filtered),
        factors,
        in_hbm(winds),
        in_hbm(tracers),
        in_hbm(tracers),
        edge,
        high,
        side,
        below,
        top,
        next_low,
    )
    return (filtered.transpose(0, 2, 1, 3), advected.transpose(0, 2, 1, 3))


def solution(mesh):
    return jax.shard_map(
        per_device,
        mesh=mesh,
        in_specs=(
            P(None, "lat", "lon", None),
            P(),
            P(None, "lat", "lon", None),
            P(None, "lat", "lon", None),
        ),
        out_specs=(P(None, "lat", "lon", None), P(None, "lat", "lon", None)),
        check_vma=False,
    )
```

time: 89.2 us -> 83.7 us (0.938)
  local copies, waits for them, and re-layouts: 10.6 us -> 2.16 us
  starting transfers between devices: 37.4 us -> 42.2 us
  other arithmetic: 6.5 us -> 2.29 us
  waiting for transfers between devices: 19.5 us -> 21.4 us
  Pallas kernels: 13 us -> 14.2 us
    all_to_all x1, waiting for transfers between devices: 11.1 us -> 0.71 us  [per_device(): rows = lax.all_to_all(send, 'lon', split_axis=0, concat_axis=0, tiled=True)]
    all_to_all x1, waiting for transfers between devices: 2.15 us -> 11.1 us  [per_device(): lax.all_to_all(low.reshape(segments, SEG, levels), 'lon', split_axis=0, c...]
    ppermute x4, waiting for transfers between devices: 4.19 us -> 9.6 us  [the longest x1 9.6 us: per_device(): side = lax.ppermute(side, 'lon', east_ring)]
    unnamed x29 -> x28, local copies, waits for them, and re-layouts: 5.6 us -> 1.1 us
    convert_element_type x5 -> x1, other arithmetic: 5.76 us -> 2.19 us  [per_device(): table = table.astype(bf16).reshape(segments * SEG, COEF)]
    ppermute x4, starting transfers between devices: 16.5 us -> 18.9 us  [the longest x1 6.85 us: per_device(): lax.ppermute(low[lat_rows], 'lat', to_prior[:lat_devices // 2 - 1])]
    ppermute x1, waiting for transfers between devices: 2.08 us -> 0.01 us  [per_device(): below = lax.ppermute(below, 'lat', to_prior)]
    all_to_all x1, starting transfers between devices: 6.1 us -> 7.69 us  [per_device(): lax.all_to_all(low.reshape(segments, SEG, levels), 'lon', split_axis=0, c...]
  transfers between devices with their start and end apart: 7 -> 7, of which waited for: 5 -> 3; matrix products, arithmetic and copies ran while one was open for 13% -> 5% of each run, Pallas kernels for 5% -> 2%
where the time goes in v2:
time: 83.7 us; the launch traced here: 83.2 us
  starting transfers between devices  42.2 us (50%)
  waiting for transfers between devices  21.4 us (26%)
  Pallas kernels  14.2 us (17%)
  other arithmetic  2.29 us (3%)
  local copies, waits for them, and re-layouts  2.16 us (3%)
  between operations  0.95 us (1%)
    all_to_all x1, starting transfers between devices, per_device(): rows = lax.all_to_all(send, 'lon', split_axis=0, concat_axis=0, tiled=True)  13.7 us
    all_to_all x1, waiting for transfers between devices, per_device(): lax.all_to_all(low.reshape(segments, SEG, levels), 'lon', split_axis=0, c...  11.1 us
    ppermute x1, waiting for transfers between devices, per_device(): side = lax.ppermute(side, 'lon', east_ring)  9.6 us
    all_to_all x1, starting transfers between devices, per_device(): lax.all_to_all(low.reshape(segments, SEG, levels), 'lon', split_axis=0, c...  7.69 us
    ppermute x1, starting transfers between devices, per_device(): lax.ppermute(low[lat_rows], 'lat', to_prior[:lat_devices // 2 - 1])  6.85 us
    ppermute x1, starting transfers between devices, per_device(): top = lax.ppermute(top, 'lat', to_next)  6.17 us
    pallas_call x1, Pallas kernels, per_device(): pl.pallas_call(advect_kernel, grid=(blocks,), in_specs=[smem, part(2), wh...  5.35 us
    ppermute x1, starting transfers between devices, per_device(): high = lax.ppermute(high, 'lon', west_ring)  4.78 us
  transfers between devices with their start and end apart: 7, of which 3 were waited for; matrix products, arithmetic and copies ran while one was open for 5% of the time, Pallas kernels for 2%

profile of v2, /device:TPU:1, one launch (start us, length us, event | category | flops | bytes accessed | tf_op | source)
XLA Modules:
  0.0 83.2 jit_solution(217442033498921492)
XLA Ops:
  0.6 0.0 copy-start.4
  0.6 2.5 %pack.1 = bf16[64,48,128]{2,1,0:T(8,128)(2,1)} custom-call(bf16[3,45,16,128]{3,2,1,0:T(8,128)(2,1)} %bitcast.39), custom_call_target="tpu_custom_call" | custom-call | tf_op jit(solution)/shard_map/pack/pallas_call | solution.py:231
  3.2 0.0 copy-start
  3.2 13.7 %all-to-all-start = ((bf16[64,48,128]{2,1,0:T(8,128)(2,1)}), bf16[64,48,128]{2,1,0:T(8,128)(2,1)S(1)}, u32[]{:S(2)}, u32[]{:S(2)}) async-start(bf16[64,48,128]{2,1,0:T(8,128)(2,1)} %pack.1), calls=%async_computation | async-start | bytes 1572864 | tf_op jit(solution)/shard_map/forth/all_to_all | solution.py:247
  16.9 0.0 copy-done.4
  16.9 0.0 copy-start.5
  16.9 0.0 copy-start.7
  16.9 0.0 copy-start.8
  17.0 0.0 copy-start.9
  17.0 0.6 copy.48
  17.6 0.0 copy-start.6
  17.6 0.0 copy-start.10
  17.6 0.1 fusion
  17.7 1.1 %collective-permute-start.1 = (bf16[5,16,128]{2,1,0:T(8,128)(2,1)S(1)}, bf16[5,16,128]{2,1,0:T(8,128)(2,1)S(1)}, u32[]{:S(2)}, u32[]{:S(2)}) collective-permute-start(bf16[5,16,128]{2,1,0:T(8,128)(2,1)S(1)} %bitcast.56), channel_id=1, source_target_pairs={{0,1},{1,2},{2,3},{3,4},{4,5},{5,6},{6,7},{7,8},{8,9},{9,10},{10,1... | collective-permute-start | bytes 61448 | tf_op jit(solution)/shard_map/columns/ppermute | solution.py:277
  18.8 0.0 copy-done
  18.8 0.2 copy.50
  19.0 0.0 copy-done.5
  19.0 0.0 copy-start.1
  19.0 0.0 copy-start.2
  19.0 0.0 copy-start.3
  19.0 0.2 copy.49
  19.3 0.0 copy-done.6
  19.3 4.8 %collective-permute-start = (bf16[7,16,128]{2,1,0:T(8,128)(2,1)S(1)}, bf16[7,16,128]{2,1,0:T(8,128)(2,1)S(1)}, u32[]{:S(2)}, u32[]{:S(2)}) collective-permute-start(bf16[7,16,128]{2,1,0:T(8,128)(2,1)S(1)} %pad_maximum_fusion.1), channel_id=1, source_target_pairs={{1,0},{2,1},{3,2},{4,3},{5,4},{6,5},{7,6},{8,7},{9,8},{10,9},{11,1... | collective-permute-start | bytes 86024 | tf_op jit(solution)/shard_map/columns/ppermute | solution.py:276
  24.1 0.9 %slice_bitcast_fusion = (bf16[5,45,128]{2,1,0:T(8,128)(2,1)S(1)}, bf16[5,45,128]{2,1,0:T(8,128)(2,1)S(1)}) fusion(bf16[5,45,16,128]{3,1,0,2:T(8,128)(2,1)} %bitcast.49), kind=kLoop, calls=%fused_computation.5 | loop fusion | bytes 230400 | tf_op jit(solution)/shard_map/edges/convert_element_type | solution.py:274
  25.0 0.0 copy-done.7
  25.0 0.0 copy-done.8
  25.0 0.0 copy-done.9
  25.0 0.0 copy-done.10
  25.1 2.2 %add_convert_fusion = bf16[64,48,384]{2,1,0:T(8,128)(2,1)} fusion(f32[48,384]{1,0:T(8,128)S(1)} %copy-done.9, f32[64,384]{1,0:T(8,128)S(1)} %copy-done.7, f32[48,384]{1,0:T(8,128)S(1)} %copy-done.10, f32[64,384]{1,0:T(8,128)S(1)} %copy-done.8), kind=kLoop, calls=%fused_computation | loop fusion | flops 4718592 | bytes 2703360 | tf_op jit(solution)/shard_map/table/convert_element_type | solution.py:264
  27.2 0.1 pad_add_fusion.place_ref
  27.3 9.6 %collective-permute-done.1.side_ref = bf16[5,16,128]{2,1,0:T(8,128)(2,1)S(1)} collective-permute-done((bf16[5,16,128]{2,1,0:T(8,128)(2,1)S(1)}, bf16[5,16,128]{2,1,0:T(8,128)(2,1)S(1)}, u32[]{:S(2)}, u32[]{:S(2)}) %collective-permute-start.1) | collective-permute-done | bytes 20512 | tf_op jit(solution)/shard_map/columns/ppermute | solution.py:277
  36.9 0.0 collective-permute-done.high_ref
  36.9 0.7 all-to-all-done
  37.6 0.0 copy-done.1
  37.6 0.0 copy-done.3
  37.6 0.0 copy-start.11
  37.7 4.3 %transform.1 = bf16[3072,128]{1,0:T(8,128)(2,1)} custom-call(s32[3]{0:T(128)S(1)} %pad_add_fusion.place_ref, s32[64]{0:T(128)S(1)} %copy-done.3, s32[1,384]{1,0:T(1,128)S(1)} %copy-done.2, f32[1,384]{1,0:T(1,128)S(1)} %copy-done.1, bf16[3072,128]{1,0:T(8,128)(2,1)S(1)} %bitcast.41, bf16[3072,384]{1,0:T(8,128)(2,1)} %bitcast.44), custom_call_target="tpu_custom_call" | custom-call | tf_op jit(solution)/shard_map/transform/pallas_call | solution.py:282
  41.9 7.7 %all-to-all-start.1 = ((bf16[64,48,128]{2,1,0:T(8,128)(2,1)}), bf16[64,48,128]{2,1,0:T(8,128)(2,1)S(1)}, u32[]{:S(2)}, u32[]{:S(2)}) async-start(bf16[64,48,128]{2,1,0:T(8,128)(2,1)} %bitcast.45), calls=%async_computation.1 | async-start | bytes 1572864 | tf_op jit(solution)/shard_map/back/all_to_all | solution.py:305
  49.6 6.2 %collective-permute-start.3 = (bf16[5,45,128]{2,1,0:T(8,128)(2,1)S(1)}, bf16[5,45,128]{2,1,0:T(8,128)(2,1)S(1)}, u32[]{:S(2)}, u32[]{:S(2)}) collective-permute-start(bf16[5,45,128]{2,1,0:T(8,128)(2,1)S(1)} %get-tuple-element.25), channel_id=1, source_target_pairs={{0,64},{64,128},{128,192},{1,65},{65,129},{129,193},{2,66},{66,130... | collective-permute-start | bytes 172808 | tf_op jit(solution)/shard_map/top/ppermute | solution.py:311
  55.8 1.9 %collective-permute-start.2 = (bf16[7,45,128]{2,1,0:T(8,128)(2,1)S(1)}, bf16[7,45,128]{2,1,0:T(8,128)(2,1)S(1)}, u32[]{:S(2)}, u32[]{:S(2)}) collective-permute-start(bf16[7,45,128]{2,1,0:T(8,128)(2,1)S(1)} %pad_maximum_fusion), channel_id=1, source_target_pairs={{64,0},{128,64},{192,128},{65,1},{129,65},{193,129},{66,2},{130,66... | collective-permute-start | bytes 241928 | tf_op jit(solution)/shard_map/below/ppermute | solution.py:309
  57.7 11.1 %all-to-all-done.1.low_ref = bf16[64,48,128]{2,1,0:T(8,128)(2,1)S(1)} async-done(((bf16[64,48,128]{2,1,0:T(8,128)(2,1)}), bf16[64,48,128]{2,1,0:T(8,128)(2,1)S(1)}, u32[]{:S(2)}, u32[]{:S(2)}) %all-to-all-start.1) | async-done | bytes 786464 | tf_op jit(solution)/shard_map/back/all_to_all | solution.py:305
  68.8 6.9 %collective-permute-start.4 = (bf16[48,128]{1,0:T(8,128)(2,1)S(1)}, bf16[48,128]{1,0:T(8,128)(2,1)S(1)}, u32[]{:S(2)}, u32[]{:S(2)}) collective-permute-start(bf16[48,128]{1,0:T(8,128)(2,1)S(1)} %slice_bitcast_fusion.2), channel_id=1, source_target_pairs={{64,0},{65,1},{66,2},{67,3},{68,4},{69,5},{70,6},{71,7},{72,8},{73... | collective-permute-start | bytes 36872 | tf_op jit(solution)/shard_map/ppermute | solution.py:312
  75.7 0.1 jit_solution_.3.factor_ref
  75.8 2.0 %filter.1 = (bf16[3,45,16,128]{3,2,1,0:T(8,128)(2,1)}, f32[16,128]{1,0:T(8,128)S(1)}) custom-call(s32[3]{0:T(128)S(1)} %pad_add_fusion.place_ref, bf16[64,48,128]{2,1,0:T(8,128)(2,1)S(1)} %all-to-all-done.1.low_ref, f32[4,5,16,128]{3,2,1,0:T(8,128)S(1)} %jit_solution_.3.factor_ref, bf16[3,45,16,128]{3,2,1,0:T(8,128)(2,1)S(1)} %bitcast.40, ...), custom_call_target="tpu_custom_call" | custom-call | tf_op jit(solution)/shard_map/filter/pallas_call | solution.py:314
  77.8 0.0 collective-permute-done.3.top_ref
  77.8 0.0 collective-permute-done.2.below_ref
  77.8 0.0 collective-permute-done.4.next_low_ref
  77.9 5.3 %advect.1 = f32[5,45,16,128]{3,2,1,0:T(8,128)} custom-call(s32[3]{0:T(128)S(1)} %pad_add_fusion.place_ref, bf16[3,45,16,128]{3,2,1,0:T(8,128)(2,1)} %get-tuple-element.21.filt_ref, f32[4,5,16,128]{3,2,1,0:T(8,128)S(1)} %jit_solution_.3.factor_ref, f32[2,45,16,128]{3,2,1,0:T(8,128)} %bitcast.46, f32[5,45,16,128]{3,2,1,0:T(8,128)} %bitcast.42, ...), custom_call_target="tpu_custom_call" | custom-call | tf_op jit(solution)/shard_map/advect/pallas_call | solution.py:335
  (11 shorter events, 0.1 us)
Async XLA Ops:
  0.6 16.3 %copy-start.4 = (f32[5,16,45,128]{3,1,2,0:T(8,128)S(1)}, f32[5,16,45,128]{3,1,2,0:T(8,128)}, u32[]{:S(2)}) copy-start(f32[5,16,45,128]{3,1,2,0:T(8,128)} %param.14) | copy-start | bytes 5529604
  3.2 15.6 %copy-start = (bf16[3,16,45,128]{3,1,2,0:T(8,128)(2,1)S(1)}, bf16[3,16,45,128]{3,1,2,0:T(8,128)(2,1)}, u32[]{:S(2)}) copy-start(bf16[3,16,45,128]{3,1,2,0:T(8,128)(2,1)} %param.11) | copy-start | bytes 1658884
  3.2 34.4 %all-to-all-start = ((bf16[64,48,128]{2,1,0:T(8,128)(2,1)}), bf16[64,48,128]{2,1,0:T(8,128)(2,1)S(1)}, u32[]{:S(2)}, u32[]{:S(2)}) async-start(bf16[64,48,128]{2,1,0:T(8,128)(2,1)} %pack.1), calls=%async_computation | async-start | bytes 1572864 | tf_op jit(solution)/shard_map/forth/all_to_all | solution.py:247
  16.9 2.0 %copy-start.5 = (f32[2,16,45,128]{3,1,2,0:T(8,128)S(1)}, f32[2,16,45,128]{3,1,2,0:T(8,128)}, u32[]{:S(2)}) copy-start(f32[2,16,45,128]{3,1,2,0:T(8,128)} %param.13) | copy-start | bytes 2211844
  16.9 8.1 %copy-start.7 = (f32[64,384]{1,0:T(8,128)S(1)}, f32[64,384]{1,0:T(8,128)}, u32[]{:S(2)}) copy-start(f32[64,384]{1,0:T(8,128)} %constant.41.clone) | copy-start | bytes 294916
  16.9 8.1 %copy-start.8 = (f32[64,384]{1,0:T(8,128)S(1)}, f32[64,384]{1,0:T(8,128)}, u32[]{:S(2)}) copy-start(f32[64,384]{1,0:T(8,128)} %constant.39.clone) | copy-start | bytes 294916
  17.0 8.1 %copy-start.9 = (f32[48,384]{1,0:T(8,128)S(1)}, f32[48,384]{1,0:T(8,128)}, u32[]{:S(2)}) copy-start(f32[48,384]{1,0:T(8,128)} %constant.42.clone) | copy-start | bytes 221188
  17.6 1.7 %copy-start.6 = (bf16[5,16,45,128]{3,2,0,1:T(8,128)(2,1)}, bf16[5,16,45,128]{3,2,0,1:T(8,128)(2,1)S(1)}, u32[]{:S(2)}) copy-start(bf16[5,16,45,128]{3,2,0,1:T(8,128)(2,1)S(1)} %copy.48) | copy-start | bytes 2764804
  17.6 7.4 %copy-start.10 = (f32[48,384]{1,0:T(8,128)S(1)}, f32[48,384]{1,0:T(8,128)}, u32[]{:S(2)}) copy-start(f32[48,384]{1,0:T(8,128)} %constant.40.clone) | copy-start | bytes 221188
  17.7 19.2 %collective-permute-start.1 = (bf16[5,16,128]{2,1,0:T(8,128)(2,1)S(1)}, bf16[5,16,128]{2,1,0:T(8,128)(2,1)S(1)}, u32[]{:S(2)}, u32[]{:S(2)}) collective-permute-start(bf16[5,16,128]{2,1,0:T(8,128)(2,1)S(1)} %bitcast.56), channel_id=1, source_target_pairs={{0,1},{1,2},{2,3},{3,4},{4,5},{5,6},{6,7},{7,8},{8,9},{9,10},{10,1... | collective-permute-start | bytes 61448 | tf_op jit(solution)/shard_map/columns/ppermute | solution.py:277
  19.0 18.7 %copy-start.1 = (f32[1,384]{1,0:T(1,128)S(1)}, f32[1,384]{1,0:T(1,128)}, u32[]{:S(2)}) copy-start(f32[1,384]{1,0:T(1,128)} %constant.49.fold_ref) | copy-start | bytes 4612
  19.0 18.7 %copy-start.2 = (s32[1,384]{1,0:T(1,128)S(1)}, s32[1,384]{1,0:T(1,128)}, u32[]{:S(2)}) copy-start(s32[1,384]{1,0:T(1,128)} %constant.48.waves_ref) | copy-start | bytes 4612
  19.0 18.7 %copy-start.3 = (s32[64]{0:T(128)S(1)}, s32[64]{0:T(128)}, u32[]{:S(2)}) copy-start(s32[64]{0:T(128)} %bands_ref.1) | copy-start | bytes 772
  19.3 17.6 %collective-permute-start = (bf16[7,16,128]{2,1,0:T(8,128)(2,1)S(1)}, bf16[7,16,128]{2,1,0:T(8,128)(2,1)S(1)}, u32[]{:S(2)}, u32[]{:S(2)}) collective-permute-start(bf16[7,16,128]{2,1,0:T(8,128)(2,1)S(1)} %pad_maximum_fusion.1), channel_id=1, source_target_pairs={{1,0},{2,1},{3,2},{4,3},{5,4},{6,5},{7,6},{8,7},{9,8},{10,9},{11,1... | collective-permute-start | bytes 86024 | tf_op jit(solution)/shard_map/columns/ppermute | solution.py:276
  37.6 38.0 %copy-start.11 = (f32[4,5,16]{2,1,0:T(8,128)S(1)}, f32[4,5,16]{2,1,0:T(8,128)}, u32[]{:S(2)}) copy-start(f32[4,5,16]{2,1,0:T(8,128)} %constant.38.clone) | copy-start | bytes 3844
  41.9 26.9 %all-to-all-start.1 = ((bf16[64,48,128]{2,1,0:T(8,128)(2,1)}), bf16[64,48,128]{2,1,0:T(8,128)(2,1)S(1)}, u32[]{:S(2)}, u32[]{:S(2)}) async-start(bf16[64,48,128]{2,1,0:T(8,128)(2,1)} %bitcast.45), calls=%async_computation.1 | async-start | bytes 1572864 | tf_op jit(solution)/shard_map/back/all_to_all | solution.py:305
  49.6 28.2 %collective-permute-start.3 = (bf16[5,45,128]{2,1,0:T(8,128)(2,1)S(1)}, bf16[5,45,128]{2,1,0:T(8,128)(2,1)S(1)}, u32[]{:S(2)}, u32[]{:S(2)}) collective-permute-start(bf16[5,45,128]{2,1,0:T(8,128)(2,1)S(1)} %get-tuple-element.25), channel_id=1, source_target_pairs={{0,64},{64,128},{128,192},{1,65},{65,129},{129,193},{2,66},{66,130... | collective-permute-start | bytes 172808 | tf_op jit(solution)/shard_map/top/ppermute | solution.py:311
  55.8 22.0 %collective-permute-start.2 = (bf16[7,45,128]{2,1,0:T(8,128)(2,1)S(1)}, bf16[7,45,128]{2,1,0:T(8,128)(2,1)S(1)}, u32[]{:S(2)}, u32[]{:S(2)}) collective-permute-start(bf16[7,45,128]{2,1,0:T(8,128)(2,1)S(1)} %pad_maximum_fusion), channel_id=1, source_target_pairs={{64,0},{128,64},{192,128},{65,1},{129,65},{193,129},{66,2},{130,66... | collective-permute-start | bytes 241928 | tf_op jit(solution)/shard_map/below/ppermute | solution.py:309
  68.8 9.0 %collective-permute-start.4 = (bf16[48,128]{1,0:T(8,128)(2,1)S(1)}, bf16[48,128]{1,0:T(8,128)(2,1)S(1)}, u32[]{:S(2)}, u32[]{:S(2)}) collective-permute-start(bf16[48,128]{1,0:T(8,128)(2,1)S(1)} %slice_bitcast_fusion.2), channel_id=1, source_target_pairs={{64,0},{65,1},{66,2},{67,3},{68,4},{69,5},{70,6},{71,7},{72,8},{73... | collective-permute-start | bytes 36872 | tf_op jit(solution)/shard_map/ppermute | solution.py:312

commit v3 on v2

v3 whole, which is shorter than its diff:
```python
import math

import jax
import jax.numpy as jnp
import numpy as np
from jax import lax
from jax.experimental import pallas as pl
from jax.experimental.pallas import tpu as pltpu
from jax.sharding import PartitionSpec as P

HEMI = 720
KMAX = 180
COEF = 384
SEG = 48
LIMIT = 24 << 20
CHUNKS = 4
COLS = 9


def trig_tables(lon_count, segments):
    width = lon_count // segments
    k = np.zeros(COEF)
    k[: KMAX + 1] = np.arange(KMAX + 1)
    k[KMAX + 1 : 2 * KMAX + 1] = np.arange(1, KMAX + 1)
    is_cos = np.zeros(COEF, bool)
    is_cos[: KMAX + 1] = True
    used = np.arange(COEF) < 2 * KMAX + 1
    over_p = 2 * np.pi * np.outer(np.arange(segments) * width, k) / lon_count
    over_q = 2 * np.pi * np.outer(np.arange(SEG), k) / lon_count
    p_one = np.where(is_cos, np.cos(over_p), np.sin(over_p)) * used
    p_two = np.where(is_cos, -np.sin(over_p), np.cos(over_p)) * used
    tables = (p_one, p_two, np.cos(over_q), np.sin(over_q))
    return tuple(t.astype(np.float32) for t in tables), k.astype(np.int32), used


def pack_kernel(tend_ref, out_ref, tend, wide, rows, in_sems, out_sems):
    fields, width, lat_rows, levels = tend.shape
    pad = rows.shape[1] - width
    loads = [pltpu.make_async_copy(tend_ref.at[f], tend.at[f], in_sems.at[f]) for f in range(fields)]
    for load in loads:
        load.start()
    stores = []
    blocks = rows.shape[0] // lat_rows
    for f in reversed(range(blocks)):
        part = pl.ds(f * lat_rows, lat_rows)
        if f < fields:
            loads[f].wait()
            wide[f] = tend[f].astype(jnp.float32).reshape(width * lat_rows, levels)
            for r in range(lat_rows):
                row = wide[f, pl.ds(r, width, stride=lat_rows), :]
                rows[f * lat_rows + r, :width] = row.astype(jnp.bfloat16)
                rows[f * lat_rows + r, width:] = jnp.zeros((pad, levels), jnp.bfloat16)
        else:
            rows[part] = jnp.zeros((lat_rows,) + rows.shape[1:], jnp.bfloat16)
        store = pltpu.make_async_copy(rows.at[part], out_ref.at[part], out_sems.at[f])
        store.start()
        stores.append(store)
    for store in stores:
        store.wait()


def transform_kernel(rows_ref, weight_ref, table_ref, out_ref, rows, result, in_sems, out_sems):
    size = result.shape[0] // CHUNKS
    parts = [pl.ds(i * size, size) for i in range(CHUNKS)]
    loads = [
        pltpu.make_async_copy(rows_ref.at[part], rows.at[part], in_sems.at[i])
        for i, part in enumerate(parts)
    ]
    stores = [
        pltpu.make_async_copy(result.at[part], out_ref.at[part], out_sems.at[i])
        for i, part in enumerate(parts)
    ]
    for load in loads:
        load.start()
    spectrum = 0.0
    for load, part in zip(loads, parts):
        load.wait()
        spectrum += lax.dot_general(
            rows[part], table_ref[part], (((0,), (0,)), ((), ())), preferred_element_type=jnp.float32
        )
    weighted = (spectrum * weight_ref[...]).astype(jnp.bfloat16)
    for store, part in zip(stores, parts):
        result[part] = lax.dot_general(
            table_ref[part], weighted, (((1,), (1,)), ((), ())), preferred_element_type=jnp.float32
        ).astype(jnp.bfloat16)
        store.start()
    for store in stores:
        store.wait()


def filter_kernel(
    low_ref,
    factor_ref,
    tend_ref,
    wind_hbm,
    high_ref,
    filt_ref,
    courant_ref,
    wide_ref,
    filt,
    wind_ref,
    sems,
    wind_sems,
):
    fields, width, lat_rows, levels = tend_ref.shape
    loads = [pltpu.make_async_copy(wind_hbm.at[f], wind_ref.at[f], wind_sems.at[f]) for f in range(2)]
    for load in loads:
        load.start()
    size = width * lat_rows
    damp = jnp.broadcast_to(factor_ref[lax.axis_index("lat"), 0], (lat_rows, levels))
    stores = []
    for f in range(fields):
        for r in range(lat_rows):
            wide_ref[f, pl.ds(r, SEG, stride=lat_rows), :] = low_ref[f * lat_rows + r].astype(jnp.float32)
        low = wide_ref[f, :size].reshape(width, lat_rows, levels)
        value = (damp[None] * tend_ref[f].astype(jnp.float32) + low).astype(jnp.bfloat16)
        filt[f] = value
        stores.append(pltpu.make_async_copy(filt.at[f], filt_ref.at[f], sems.at[f]))
        stores[f].start()
        if f < 2:
            loads[f].wait()
            courant_ref[f, :width] = (0.5, 0.25)[f] * jnp.tanh(wind_ref[f] + value.astype(jnp.float32))
        if f == 0:
            last = high_ref.shape[0] - 1
            edge = damp * high_ref[last].astype(jnp.float32) + wide_ref[f, size : size + lat_rows]
            edge = edge.astype(jnp.bfloat16).astype(jnp.float32)
            courant_ref[f, width] = 0.5 * jnp.tanh(high_ref[last - 1].astype(jnp.float32) + edge)
    for store in stores:
        store.wait()


def advect_kernel(
    courant_ref,
    factor_ref,
    tracer_hbm,
    high_ref,
    side_ref,
    below_ref,
    top_ref,
    next_low_ref,
    out_hbm,
    tracer_ref,
    out_ref,
    north_ref,
    below_wide,
    top_wide,
    in_sems,
    out_sems,
):
    count, width, lat_rows, levels = tracer_ref.shape
    pieces = width // COLS
    loads = []
    stores = []
    for i in range(pieces):
        part = pl.ds(i * COLS, COLS)
        loads.append(
            pltpu.make_async_copy(tracer_hbm.at[:, part], tracer_ref.at[:, part], in_sems.at[i])
        )
        stores.append(pltpu.make_async_copy(out_ref.at[:, part], out_hbm.at[:, part], out_sems.at[i]))
    for load in reversed(loads):
        load.start()
    lat = lax.axis_index("lat")
    face, face_next, inverse = (
        jnp.broadcast_to(factor_ref[lat, i], (lat_rows, levels)) for i in (1, 2, 3)
    )
    sublane = lax.broadcasted_iota(jnp.int32, (lat_rows, levels), 0)
    is_first = sublane == 0
    is_last = sublane == lat_rows - 1
    below_wide[:, :width] = below_ref[...].astype(jnp.float32)
    top_wide[:, :width] = top_ref[...].astype(jnp.float32)
    filt = factor_ref[lat, 4, 0:1] * below_wide[count + 1, :width]
    filt = (filt + next_low_ref[:width].astype(jnp.float32)).astype(jnp.bfloat16)
    north_ref[:width] = 0.25 * jnp.tanh(below_wide[count, :width] + filt.astype(jnp.float32))
    loads[pieces - 1].wait()
    east = courant_ref[0, width]
    flux = [
        jnp.maximum(east, 0.0) * tracer_ref[q, width - 1]
        + jnp.minimum(east, 0.0) * high_ref[q].astype(jnp.float32)
        for q in range(count)
    ]
    for piece in reversed(range(pieces)):
        if piece > 0:
            loads[piece - 1].wait()
        for column in reversed(range(piece * COLS, (piece + 1) * COLS)):
            east = courant_ref[0, column]
            north = courant_ref[1, column]
            north_next = jnp.where(
                is_last, north_ref[column : column + 1], pltpu.roll(north, lat_rows - 1, 0)
            )
            west_plus = jnp.maximum(east, 0.0)
            west_minus = jnp.minimum(east, 0.0)
            pole_plus = face * jnp.maximum(north, 0.0)
            pole_minus = face * jnp.minimum(north, 0.0)
            next_plus = face_next * jnp.maximum(north_next, 0.0)
            next_minus = face_next * jnp.minimum(north_next, 0.0)
            for q in range(count):
                here = tracer_ref[q, column]
                if column > 0:
                    west = tracer_ref[q, column - 1]
                else:
                    west = side_ref[q].astype(jnp.float32)
                prior = jnp.where(
                    is_first, top_wide[q, column : column + 1], pltpu.roll(here, 1, 0)
                )
                after = jnp.where(
                    is_last, below_wide[q, column : column + 1], pltpu.roll(here, lat_rows - 1, 0)
                )
                f_west = west_plus * west + west_minus * here
                g_pole = pole_plus * prior + pole_minus * here
                g_next = next_plus * here + next_minus * after
                out_ref[q, column] = here - (flux[q] - f_west) - (g_next - g_pole) * inverse
                flux[q] = f_west
        stores[piece].start()
    for store in stores:
        store.wait()


def row_factors(lat_devices, lat_rows):
    ids = np.arange(lat_devices * lat_rows + 1)
    half = lat_devices * lat_rows // 2
    damping = np.where(ids < half, 0.25 + 0.5 * (ids + 0.5) / half, 1.0)
    grid_row = ids + HEMI // 2 - half
    face = np.sin(math.pi * grid_row / (2.0 * HEMI))
    centre = np.sin(math.pi * (grid_row + 0.5) / (2.0 * HEMI))
    rows = np.stack(
        [damping[:-1], face[:-1], face[1:], 1.0 / centre[:-1], np.repeat(damping[lat_rows::lat_rows], lat_rows)]
    )
    rows = rows.reshape(5, lat_devices, lat_rows).swapaxes(0, 1).astype(np.float32)
    return rows[..., None]


def in_vmem(array):
    return pltpu.with_memory_space_constraint(array, pltpu.VMEM)


def in_hbm(array):
    return pltpu.with_memory_space_constraint(array, pltpu.HBM)


def per_device(tendencies, bands, winds, tracers):
    fields, lat_rows, width, levels = tendencies.shape
    count = tracers.shape[0]
    lat_devices = lax.axis_size("lat")
    segments = lax.axis_size("lon")
    lat_place = lax.axis_index("lat")
    lon_place = lax.axis_index("lon")
    tendencies, winds, tracers = (a.transpose(0, 2, 1, 3) for a in (tendencies, winds, tracers))

    to_prior = [(i + 1, i) for i in range(lat_devices - 1)]
    to_next = [(i, i + 1) for i in range(lat_devices - 1)]
    west_ring = [((i + 1) % segments, i) for i in range(segments)]
    east_ring = [(i, (i + 1) % segments) for i in range(segments)]
    vmem = pl.BlockSpec(memory_space=pltpu.VMEM)
    hbm = pl.BlockSpec(memory_space=pltpu.HBM)
    params = pltpu.CompilerParams(vmem_limit_bytes=LIMIT)
    bf16 = jnp.bfloat16

    send = pl.pallas_call(
        pack_kernel,
        in_specs=[hbm],
        out_specs=hbm,
        out_shape=pltpu.HBM((segments, SEG, levels), bf16),
        scratch_shapes=[
            pltpu.VMEM(tendencies.shape, bf16),
            pltpu.VMEM((fields, width * lat_rows, levels), jnp.float32),
            pltpu.VMEM((segments, SEG, levels), bf16),
            pltpu.SemaphoreType.DMA((fields,)),
            pltpu.SemaphoreType.DMA((segments // lat_rows,)),
        ],
        compiler_params=params,
        name="pack",
    )(in_hbm(tendencies))
    with jax.named_scope("forth"):
        rows = lax.all_to_all(send, "lon", split_axis=0, concat_axis=0, tiled=True)

    factors = jnp.asarray(row_factors(lat_devices, lat_rows))
    (p_one, p_two, q_one, q_two), waves, used = trig_tables(segments * width, segments)
    row = lat_place * lat_rows + lon_place % lat_rows
    half = lat_devices * lat_rows // 2
    damping = 0.25 + 0.5 * (row.astype(jnp.float32) + 0.5) / half
    damping = jnp.where(row < half, damping, 1.0)
    fold = np.where(used, np.where(waves == 0, 1.0, 2.0), 0.0) / (segments * width)
    weight = (1.0 - damping) * jnp.asarray(fold, jnp.float32)[None]
    weight = jnp.where(jnp.asarray(waves)[None] <= bands[row], weight, 0.0)
    with jax.named_scope("table"):
        table = (
            jnp.asarray(p_one)[:, None, :] * jnp.asarray(q_one)[None, :, :]
            + jnp.asarray(p_two)[:, None, :] * jnp.asarray(q_two)[None, :, :]
        )
        table = table.astype(bf16).reshape(segments * SEG, COEF)

    with jax.named_scope("edges"):
        high = jnp.concatenate(
            [tracers[:, 0].astype(bf16), winds[0:1, 0].astype(bf16), tendencies[0:1, 0]], axis=0
        )
        side = tracers[:, width - 1].astype(bf16)
        below = jnp.concatenate(
            [tracers[:, :, 0].astype(bf16), winds[1:2, :, 0].astype(bf16), tendencies[1:2, :, 0]], axis=0
        )
        top = tracers[:, :, lat_rows - 1].astype(bf16)
    with jax.named_scope("columns"):
        high = lax.ppermute(high, "lon", west_ring)
        side = lax.ppermute(side, "lon", east_ring)
    rows, table, weight, factors, high, side, below, top = lax.optimization_barrier(
        (rows, table, weight, factors, high, side, below, top)
    )

    low = pl.pallas_call(
        transform_kernel,
        in_specs=[hbm, vmem, vmem],
        out_specs=hbm,
        out_shape=pltpu.HBM((segments * SEG, levels), bf16),
        scratch_shapes=[
            pltpu.VMEM((segments * SEG, levels), bf16),
            pltpu.VMEM((segments * SEG, levels), bf16),
            pltpu.SemaphoreType.DMA((CHUNKS,)),
            pltpu.SemaphoreType.DMA((CHUNKS,)),
        ],
        compiler_params=params,
        name="transform",
    )(in_hbm(rows.reshape(segments * SEG, levels)), in_vmem(weight), in_vmem(table))
    low, below, top = lax.optimization_barrier((low, below, top))
    with jax.named_scope("back"):
        low = lax.all_to_all(
            low.reshape(segments, SEG, levels), "lon", split_axis=0, concat_axis=0, tiled=True
        )
    with jax.named_scope("below"):
        below = lax.ppermute(below, "lat", to_prior)
    with jax.named_scope("top"):
        top = lax.ppermute(top, "lat", to_next)
    next_low = lax.ppermute(low[lat_rows], "lat", to_prior[: lat_devices // 2 - 1])

    filtered, courant = pl.pallas_call(
        filter_kernel,
        in_specs=[vmem, vmem, vmem, hbm, vmem],
        out_specs=[hbm, vmem],
        out_shape=[
            pltpu.HBM(tendencies.shape, bf16),
            pltpu.VMEM((2, width + 1, lat_rows, levels), jnp.float32),
        ],
        scratch_shapes=[
            pltpu.VMEM((fields, SEG * lat_rows, levels), jnp.float32),
            pltpu.VMEM(tendencies.shape, bf16),
            pltpu.VMEM(winds.shape, jnp.float32),
            pltpu.SemaphoreType.DMA((fields,)),
            pltpu.SemaphoreType.DMA((2,)),
        ],
        compiler_params=params,
        name="filter",
    )(in_vmem(low), in_vmem(factors), in_vmem(tendencies), in_hbm(winds), in_vmem(high))
    advected = pl.pallas_call(
        advect_kernel,
        in_specs=[vmem, vmem, hbm] + [vmem] * 5,
        out_specs=hbm,
        out_shape=pltpu.HBM(tracers.shape, jnp.float32),
        scratch_shapes=[
            pltpu.VMEM(tracers.shape, jnp.float32),
            pltpu.VMEM(tracers.shape, jnp.float32),
            pltpu.VMEM((SEG, levels), jnp.float32),
            pltpu.VMEM((count + 2, SEG, levels), jnp.float32),
            pltpu.VMEM((count, SEG, levels), jnp.float32),
            pltpu.SemaphoreType.DMA((width // COLS,)),
            pltpu.SemaphoreType.DMA((width // COLS,)),
        ],
        compiler_params=params,
        name="advect",
    )(
        courant,
        in_vmem(factors),
        in_hbm(tracers),
        in_vmem(high),
        in_vmem(side),
        in_vmem(below),
        in_vmem(top),
        in_vmem(next_low),
    )
    return (filtered.transpose(0, 2, 1, 3), advected.transpose(0, 2, 1, 3))


def solution(mesh):
    return jax.shard_map(
        per_device,
        mesh=mesh,
        in_specs=(
            P(None, "lat", "lon", None),
            P(),
            P(None, "lat", "lon", None),
            P(None, "lat", "lon", None),
        ),
        out_specs=(P(None, "lat", "lon", None), P(None, "lat", "lon", None)),
        check_vma=False,
    )
```

time: 83.7 us -> 81.2 us (0.970)
  Pallas kernels: 14.2 us -> 11.8 us
    pallas_call x3, Pallas kernels: 11.7 us -> 9.25 us  [the longest x1 3.56 us: per_device(): pl.pallas_call(transform_kernel, in_specs=[hbm, vmem, vmem], out_specs=hb...]
    convert_element_type x1, other arithmetic: 2.19 us -> 0.79 us  [per_device(): table = table.astype(bf16).reshape(segments * SEG, COEF)]
    convert_element_type x1, local copies, waits for them, and re-layouts: 0.87 us -> 0.01 us  [per_device(): top = tracers[:, :, lat_rows - 1].astype(bf16)]
  transfers between devices with their start and end apart: 7 -> 7, of which waited for: 3 -> 3; matrix products, arithmetic and copies ran while one was open for 5% -> 5% of each run, Pallas kernels for 2% -> 3%
where the time goes in v3:
time: 81.2 us; the launch traced here: 80.8 us
  starting transfers between devices  42.3 us (52%)
  waiting for transfers between devices  21.8 us (27%)
  Pallas kernels  11.8 us (15%)
  other arithmetic  2.05 us (3%)
  local copies, waits for them, and re-layouts  1.81 us (2%)
  between operations  0.97 us (1%)
    all_to_all x1, starting transfers between devices, per_device(): rows = lax.all_to_all(send, 'lon', split_axis=0, concat_axis=0, tiled=True)  13.9 us
    all_to_all x1, waiting for transfers between devices, per_device(): lax.all_to_all(low.reshape(segments, SEG, levels), 'lon', split_axis=0, c...  11 us
    ppermute x1, waiting for transfers between devices, per_device(): side = lax.ppermute(side, 'lon', east_ring)  10.1 us
    all_to_all x1, starting transfers between devices, per_device(): lax.all_to_all(low.reshape(segments, SEG, levels), 'lon', split_axis=0, c...  7.68 us
    ppermute x1, starting transfers between devices, per_device(): lax.ppermute(low[lat_rows], 'lat', to_prior[:lat_devices // 2 - 1])  6.86 us
    ppermute x1, starting transfers between devices, per_device(): top = lax.ppermute(top, 'lat', to_next)  6.18 us
    ppermute x1, starting transfers between devices, per_device(): high = lax.ppermute(high, 'lon', west_ring)  4.74 us
    pallas_call x1, Pallas kernels, per_device(): pl.pallas_call(transform_kernel, in_specs=[hbm, vmem, vmem], out_specs=hb...  3.56 us
  transfers between devices with their start and end apart: 7, of which 3 were waited for; matrix products, arithmetic and copies ran while one was open for 5% of the time, Pallas kernels for 3%

profile of v3, /device:TPU:1, one launch (start us, length us, event | category | flops | bytes accessed | tf_op | source)
XLA Modules:
  0.0 80.8 jit_solution(14232304835106607797)
XLA Ops:
  0.6 0.0 copy-start.2
  0.6 2.5 %pack.1 = bf16[64,48,128]{2,1,0:T(8,128)(2,1)} custom-call(bf16[3,45,16,128]{3,2,1,0:T(8,128)(2,1)} %bitcast.39), custom_call_target="tpu_custom_call" | custom-call | tf_op jit(solution)/shard_map/pack/pallas_call | solution.py:258
  3.2 0.0 copy-start
  3.2 13.9 %all-to-all-start = ((bf16[64,48,128]{2,1,0:T(8,128)(2,1)}), bf16[64,48,128]{2,1,0:T(8,128)(2,1)}, u32[]{:S(2)}, u32[]{:S(2)}) async-start(bf16[64,48,128]{2,1,0:T(8,128)(2,1)} %pack.1), calls=%async_computation | async-start | bytes 1572864 | tf_op jit(solution)/shard_map/forth/all_to_all | solution.py:274
  17.1 0.0 copy-done.2
  17.1 0.0 copy-start.3
  17.2 0.0 copy-start.8
  17.2 0.0 copy-start.9
  17.2 0.0 copy-start.4
  17.2 0.6 copy.46
  17.8 0.0 copy-start.10
  17.8 0.0 copy-start.5
  17.8 0.0 copy-start.6
  17.9 0.0 copy-start.7
  17.9 0.1 fusion
  18.0 1.0 %collective-permute-start.1 = (bf16[5,16,128]{2,1,0:T(8,128)(2,1)S(1)}, bf16[5,16,128]{2,1,0:T(8,128)(2,1)S(1)}, u32[]{:S(2)}, u32[]{:S(2)}) collective-permute-start(bf16[5,16,128]{2,1,0:T(8,128)(2,1)S(1)} %bitcast.52), channel_id=1, source_target_pairs={{0,1},{1,2},{2,3},{3,4},{4,5},{5,6},{6,7},{7,8},{8,9},{9,10},{10,1... | collective-permute-start | bytes 61448 | tf_op jit(solution)/shard_map/columns/ppermute | solution.py:303
  19.0 0.0 copy-done
  19.0 0.2 copy.48
  19.1 0.0 copy-done.3
  19.2 0.2 copy.47
  19.5 0.6 pad_maximum_fusion.1
  20.1 4.7 %collective-permute-start = (bf16[7,16,128]{2,1,0:T(8,128)(2,1)}, bf16[7,16,128]{2,1,0:T(8,128)(2,1)S(1)}, u32[]{:S(2)}, u32[]{:S(2)}) collective-permute-start(bf16[7,16,128]{2,1,0:T(8,128)(2,1)} %pad_maximum_fusion.1), channel_id=1, source_target_pairs={{1,0},{2,1},{3,2},{4,3},{5,4},{6,5},{7,6},{8,7},{9,8},{10,9},{11,1... | collective-permute-start | bytes 86024 | tf_op jit(solution)/shard_map/columns/ppermute | solution.py:302
  24.8 0.0 copy-done.10
  24.8 0.6 dynamic_slice.3
  25.4 0.0 copy-done.8
  25.4 0.0 copy-done.9
  25.4 0.6 multiply_select_fusion
  26.1 0.0 copy-done.4
  26.1 0.0 copy-done.5
  26.1 0.0 copy-done.6
  26.1 0.0 copy-done.7
  26.1 0.8 add_convert_fusion
  27.0 10.1 %collective-permute-done.1.side_ref = bf16[5,16,128]{2,1,0:T(8,128)(2,1)S(1)} collective-permute-done((bf16[5,16,128]{2,1,0:T(8,128)(2,1)S(1)}, bf16[5,16,128]{2,1,0:T(8,128)(2,1)S(1)}, u32[]{:S(2)}, u32[]{:S(2)}) %collective-permute-start.1) | collective-permute-done | bytes 20512 | tf_op jit(solution)/shard_map/columns/ppermute | solution.py:303
  37.0 0.0 collective-permute-done.high_ref
  37.0 0.7 all-to-all-done
  37.7 0.0 copy-start.1
  37.7 3.6 %transform.1 = bf16[3072,128]{1,0:T(8,128)(2,1)} custom-call(bf16[3072,128]{1,0:T(8,128)(2,1)} %bitcast.12.rows_ref, f32[1,384]{1,0:T(1,128)S(1)} %select_n.25.weight_ref, bf16[3072,384]{1,0:T(8,128)(2,1)S(1)} %bitcast.38), custom_call_target="tpu_custom_call" | custom-call | tf_op jit(solution)/shard_map/transform/pallas_call | solution.py:308
  41.3 7.7 %all-to-all-start.1 = ((bf16[64,48,128]{2,1,0:T(8,128)(2,1)}), bf16[64,48,128]{2,1,0:T(8,128)(2,1)S(1)}, u32[]{:S(2)}, u32[]{:S(2)}) async-start(bf16[64,48,128]{2,1,0:T(8,128)(2,1)} %bitcast.42), calls=%async_computation.1 | async-start | bytes 1572864 | tf_op jit(solution)/shard_map/back/all_to_all | solution.py:324
  49.0 6.2 %collective-permute-start.3 = (bf16[5,45,128]{2,1,0:T(8,128)(2,1)S(1)}, bf16[5,45,128]{2,1,0:T(8,128)(2,1)S(1)}, u32[]{:S(2)}, u32[]{:S(2)}) collective-permute-start(bf16[5,45,128]{2,1,0:T(8,128)(2,1)S(1)} %get-tuple-element.27), channel_id=1, source_target_pairs={{0,64},{64,128},{128,192},{1,65},{65,129},{129,193},{2,66},{66,130... | collective-permute-start | bytes 172808 | tf_op jit(solution)/shard_map/top/ppermute | solution.py:330
  55.2 1.9 %collective-permute-start.2 = (bf16[7,45,128]{2,1,0:T(8,128)(2,1)S(1)}, bf16[7,45,128]{2,1,0:T(8,128)(2,1)S(1)}, u32[]{:S(2)}, u32[]{:S(2)}) collective-permute-start(bf16[7,45,128]{2,1,0:T(8,128)(2,1)S(1)} %pad_maximum_fusion), channel_id=1, source_target_pairs={{64,0},{128,64},{192,128},{65,1},{129,65},{193,129},{66,2},{130,66... | collective-permute-start | bytes 241928 | tf_op jit(solution)/shard_map/below/ppermute | solution.py:328
  57.1 11.0 %all-to-all-done.1.low_ref = bf16[64,48,128]{2,1,0:T(8,128)(2,1)S(1)} async-done(((bf16[64,48,128]{2,1,0:T(8,128)(2,1)}), bf16[64,48,128]{2,1,0:T(8,128)(2,1)S(1)}, u32[]{:S(2)}, u32[]{:S(2)}) %all-to-all-start.1) | async-done | bytes 786464 | tf_op jit(solution)/shard_map/back/all_to_all | solution.py:324
  68.2 6.9 %collective-permute-start.4 = (bf16[48,128]{1,0:T(8,128)(2,1)S(1)}, bf16[48,128]{1,0:T(8,128)(2,1)S(1)}, u32[]{:S(2)}, u32[]{:S(2)}) collective-permute-start(bf16[48,128]{1,0:T(8,128)(2,1)S(1)} %slice_bitcast_fusion.2), channel_id=1, source_target_pairs={{64,0},{65,1},{66,2},{67,3},{68,4},{69,5},{70,6},{71,7},{72,8},{73... | collective-permute-start | bytes 36872 | tf_op jit(solution)/shard_map/ppermute | solution.py:331
  75.0 0.0 copy-done.1
  75.0 2.4 %filter.1 = (bf16[3,45,16,128]{3,2,1,0:T(8,128)(2,1)}, f32[2,46,16,128]{3,2,1,0:T(8,128)S(1)}) custom-call(bf16[64,48,128]{2,1,0:T(8,128)(2,1)S(1)} %all-to-all-done.1.low_ref, f32[4,5,16,1]{3,2,1,0:T(8,128)S(1)} %copy-done.1, bf16[3,45,16,128]{3,2,1,0:T(8,128)(2,1)S(1)} %bitcast.40, f32[2,45,16,128]{3,2,1,0:T(8,128)} %bitcast.43, ...), custom_call_target="tpu_custom_call" | custom-call | tf_op jit(solution)/shard_map/filter/pallas_call | solution.py:333
  77.4 0.0 collective-permute-done.3.top_ref
  77.5 0.0 collective-permute-done.2.below_ref
  77.5 0.0 collective-permute-done.4.next_low_ref
  77.5 3.3 %advect.1 = f32[5,45,16,128]{3,2,1,0:T(8,128)} custom-call(f32[2,46,16,128]{3,2,1,0:T(8,128)S(1)} %get-tuple-element.24.courant_ref, f32[4,5,16,1]{3,2,1,0:T(8,128)S(1)} %copy-done.1, f32[5,45,16,128]{3,2,1,0:T(8,128)} %bitcast.41, bf16[7,16,128]{2,1,0:T(8,128)(2,1)S(1)} %collective-permute-done.high_ref, ...), custom_call_target="tpu_custom_call" | custom-call | tf_op jit(solution)/shard_map/advect/pallas_call | solution.py:351
  (10 shorter events, 0.1 us)
Async XLA Ops:
  0.6 16.5 %copy-start.2 = (f32[5,16,45,128]{3,1,2,0:T(8,128)S(1)}, f32[5,16,45,128]{3,1,2,0:T(8,128)}, u32[]{:S(2)}) copy-start(f32[5,16,45,128]{3,1,2,0:T(8,128)} %param.14) | copy-start | bytes 5529604
  3.2 15.8 %copy-start = (bf16[3,16,45,128]{3,1,2,0:T(8,128)(2,1)S(1)}, bf16[3,16,45,128]{3,1,2,0:T(8,128)(2,1)}, u32[]{:S(2)}) copy-start(bf16[3,16,45,128]{3,1,2,0:T(8,128)(2,1)} %param.11) | copy-start | bytes 1658884
  3.2 34.6 %all-to-all-start = ((bf16[64,48,128]{2,1,0:T(8,128)(2,1)}), bf16[64,48,128]{2,1,0:T(8,128)(2,1)}, u32[]{:S(2)}, u32[]{:S(2)}) async-start(bf16[64,48,128]{2,1,0:T(8,128)(2,1)} %pack.1), calls=%async_computation | async-start | bytes 1572864 | tf_op jit(solution)/shard_map/forth/all_to_all | solution.py:274
  17.1 2.0 %copy-start.3 = (f32[2,16,45,128]{3,1,2,0:T(8,128)S(1)}, f32[2,16,45,128]{3,1,2,0:T(8,128)}, u32[]{:S(2)}) copy-start(f32[2,16,45,128]{3,1,2,0:T(8,128)} %param.13) | copy-start | bytes 2211844
  17.2 8.3 %copy-start.8 = (s32[384]{0:T(512)S(1)}, s32[384]{0:T(512)}, u32[]{:S(2)}) copy-start(s32[384]{0:T(512)} %constant.55.clone) | copy-start | bytes 4612
  17.2 8.3 %copy-start.9 = (f32[384]{0:T(512)S(1)}, f32[384]{0:T(512)}, u32[]{:S(2)}) copy-start(f32[384]{0:T(512)} %constant.54.clone) | copy-start | bytes 4612
  17.2 8.9 %copy-start.4 = (f32[64,384]{1,0:T(8,128)S(1)}, f32[64,384]{1,0:T(8,128)}, u32[]{:S(2)}) copy-start(f32[64,384]{1,0:T(8,128)} %constant.58.clone) | copy-start | bytes 294916
  17.8 7.0 %copy-start.10 = (s32[64]{0:T(128)S(1)}, s32[64]{0:T(128)}, u32[]{:S(2)}) copy-start(s32[64]{0:T(128)} %param.12) | copy-start | bytes 772
  17.8 8.3 %copy-start.5 = (f32[64,384]{1,0:T(8,128)S(1)}, f32[64,384]{1,0:T(8,128)}, u32[]{:S(2)}) copy-start(f32[64,384]{1,0:T(8,128)} %constant.56.clone) | copy-start | bytes 294916
  17.8 8.3 %copy-start.6 = (f32[48,384]{1,0:T(8,128)S(1)}, f32[48,384]{1,0:T(8,128)}, u32[]{:S(2)}) copy-start(f32[48,384]{1,0:T(8,128)} %constant.59.clone) | copy-start | bytes 221188
  17.9 8.3 %copy-start.7 = (f32[48,384]{1,0:T(8,128)S(1)}, f32[48,384]{1,0:T(8,128)}, u32[]{:S(2)}) copy-start(f32[48,384]{1,0:T(8,128)} %constant.57.clone) | copy-start | bytes 221188
  18.0 19.1 %collective-permute-start.1 = (bf16[5,16,128]{2,1,0:T(8,128)(2,1)S(1)}, bf16[5,16,128]{2,1,0:T(8,128)(2,1)S(1)}, u32[]{:S(2)}, u32[]{:S(2)}) collective-permute-start(bf16[5,16,128]{2,1,0:T(8,128)(2,1)S(1)} %bitcast.52), channel_id=1, source_target_pairs={{0,1},{1,2},{2,3},{3,4},{4,5},{5,6},{6,7},{7,8},{8,9},{9,10},{10,1... | collective-permute-start | bytes 61448 | tf_op jit(solution)/shard_map/columns/ppermute | solution.py:303
  20.1 16.9 %collective-permute-start = (bf16[7,16,128]{2,1,0:T(8,128)(2,1)}, bf16[7,16,128]{2,1,0:T(8,128)(2,1)S(1)}, u32[]{:S(2)}, u32[]{:S(2)}) collective-permute-start(bf16[7,16,128]{2,1,0:T(8,128)(2,1)} %pad_maximum_fusion.1), channel_id=1, source_target_pairs={{1,0},{2,1},{3,2},{4,3},{5,4},{6,5},{7,6},{8,7},{9,8},{10,9},{11,1... | collective-permute-start | bytes 86024 | tf_op jit(solution)/shard_map/columns/ppermute | solution.py:302
  37.7 37.3 %copy-start.1 = (f32[4,5,16,1]{3,2,1,0:T(8,128)S(1)}, f32[4,5,16,1]{3,2,1,0:T(8,128)}, u32[]{:S(2)}) copy-start(f32[4,5,16,1]{3,2,1,0:T(8,128)} %constant.53.clone.factor_ref) | copy-start | bytes 3844
  41.3 26.9 %all-to-all-start.1 = ((bf16[64,48,128]{2,1,0:T(8,128)(2,1)}), bf16[64,48,128]{2,1,0:T(8,128)(2,1)S(1)}, u32[]{:S(2)}, u32[]{:S(2)}) async-start(bf16[64,48,128]{2,1,0:T(8,128)(2,1)} %bitcast.42), calls=%async_computation.1 | async-start | bytes 1572864 | tf_op jit(solution)/shard_map/back/all_to_all | solution.py:324
  49.0 28.5 %collective-permute-start.3 = (bf16[5,45,128]{2,1,0:T(8,128)(2,1)S(1)}, bf16[5,45,128]{2,1,0:T(8,128)(2,1)S(1)}, u32[]{:S(2)}, u32[]{:S(2)}) collective-permute-start(bf16[5,45,128]{2,1,0:T(8,128)(2,1)S(1)} %get-tuple-element.27), channel_id=1, source_target_pairs={{0,64},{64,128},{128,192},{1,65},{65,129},{129,193},{2,66},{66,130... | collective-permute-start | bytes 172808 | tf_op jit(solution)/shard_map/top/ppermute | solution.py:330
  55.2 22.3 %collective-permute-start.2 = (bf16[7,45,128]{2,1,0:T(8,128)(2,1)S(1)}, bf16[7,45,128]{2,1,0:T(8,128)(2,1)S(1)}, u32[]{:S(2)}, u32[]{:S(2)}) collective-permute-start(bf16[7,45,128]{2,1,0:T(8,128)(2,1)S(1)} %pad_maximum_fusion), channel_id=1, source_target_pairs={{64,0},{128,64},{192,128},{65,1},{129,65},{193,129},{66,2},{130,66... | collective-permute-start | bytes 241928 | tf_op jit(solution)/shard_map/below/ppermute | solution.py:328
  68.2 9.3 %collective-permute-start.4 = (bf16[48,128]{1,0:T(8,128)(2,1)S(1)}, bf16[48,128]{1,0:T(8,128)(2,1)S(1)}, u32[]{:S(2)}, u32[]{:S(2)}) collective-permute-start(bf16[48,128]{1,0:T(8,128)(2,1)S(1)} %slice_bitcast_fusion.2), channel_id=1, source_target_pairs={{64,0},{65,1},{66,2},{67,3},{68,4},{69,5},{70,6},{71,7},{72,8},{73... | collective-permute-start | bytes 36872 | tf_op jit(solution)/shard_map/ppermute | solution.py:331

commit v4 on v3

--- a/solution.py
+++ b/solution.py
@@ -12,7 +12,11 @@
 KMAX = 180
 COEF = 384
 SEG = 48
+HEAD = 40
+QUARTER = 32
+MAIN = 96
 LIMIT = 24 << 20
+LOADS = 5
 CHUNKS = 4
 COLS = 9
 
@@ -33,57 +37,114 @@
     return tuple(t.astype(np.float32) for t in tables), k.astype(np.int32), used
 
 
+def squeeze(head, tail):
+    lane = lax.broadcasted_iota(jnp.int32, tail.shape, tail.ndim - 1)
+    size = tail.shape[-2]
+    groups = [
+        jnp.where(
+            lane < MAIN,
+            head[..., i * size : (i + 1) * size, :],
+            pltpu.roll(tail, MAIN - i * QUARTER, tail.ndim - 1),
+        )
+        for i in range(MAIN // QUARTER)
+    ]
+    return jnp.concatenate(groups + [head[..., MAIN // QUARTER * size :, :]], axis=-2)
+
+
+def tail_of(head):
+    size = SEG - HEAD
+    moved = [
+        pltpu.roll(head[..., i * size : (i + 1) * size, :], (i + 1) * QUARTER, head.ndim - 1)
+        for i in range(MAIN // QUARTER)
+    ]
+    lane = lax.broadcasted_iota(jnp.int32, moved[0].shape, head.ndim - 1)
+    return jnp.where(lane < QUARTER, moved[0], jnp.where(lane < 2 * QUARTER, moved[1], moved[2]))
+
+
+def expand(head):
+    return jnp.concatenate([head, tail_of(head)], axis=-2)
+
+
+def with_rest(row, rest, f):
+    lane = lax.broadcasted_iota(jnp.int32, row.shape, row.ndim - 1)
+    return jnp.where(lane < MAIN, row, pltpu.roll(rest, MAIN - f * QUARTER, row.ndim - 1))
+
+
 def pack_kernel(tend_ref, out_ref, tend, wide, rows, in_sems, out_sems):
     fields, width, lat_rows, levels = tend.shape
-    pad = rows.shape[1] - width
+    size = width * lat_rows
     loads = [pltpu.make_async_copy(tend_ref.at[f], tend.at[f], in_sems.at[f]) for f in range(fields)]
     for load in loads:
         load.start()
     stores = []
-    blocks = rows.shape[0] // lat_rows
-    for f in reversed(range(blocks)):
-        part = pl.ds(f * lat_rows, lat_rows)
-        if f < fields:
-            loads[f].wait()
-            wide[f] = tend[f].astype(jnp.float32).reshape(width * lat_rows, levels)
-            for r in range(lat_rows):
-                row = wide[f, pl.ds(r, width, stride=lat_rows), :]
-                rows[f * lat_rows + r, :width] = row.astype(jnp.bfloat16)
-                rows[f * lat_rows + r, width:] = jnp.zeros((pad, levels), jnp.bfloat16)
-        else:
-            rows[part] = jnp.zeros((lat_rows,) + rows.shape[1:], jnp.bfloat16)
-        store = pltpu.make_async_copy(rows.at[part], out_ref.at[part], out_sems.at[f])
+
+    def send(block):
+        part = pl.ds(block * lat_rows, lat_rows)
+        store = pltpu.make_async_copy(rows.at[part], out_ref.at[part], out_sems.at[block])
         store.start()
         stores.append(store)
+
+    for f in range(fields):
+        wide[f, size:] = jnp.zeros((SEG * lat_rows - size, levels), jnp.float32)
+    for f in range(fields):
+        loads[f].wait()
+        wide[f, :size] = tend[f].astype(jnp.float32).reshape(size, levels)
+        for r in range(lat_rows):
+            row = wide[f, pl.ds(r, SEG, stride=lat_rows), :]
+            rows[f * lat_rows + r] = squeeze(row[:HEAD], row[HEAD:]).astype(jnp.bfloat16)
+        send(f)
+    lane = lax.broadcasted_iota(jnp.int32, (SEG, levels), 1)
+    for r in range(lat_rows):
+        moved = [
+            pltpu.roll(wide[f, pl.ds(r, SEG, stride=lat_rows), :], (f + 1) * QUARTER, 1)
+            for f in range(fields)
+        ]
+        row = jnp.where(lane < QUARTER, moved[0], jnp.where(lane < 2 * QUARTER, moved[1], moved[2]))
+        rows[fields * lat_rows + r] = squeeze(row[:HEAD], row[HEAD:]).astype(jnp.bfloat16)
+    send(fields)
     for store in stores:
         store.wait()
 
 
-def transform_kernel(rows_ref, weight_ref, table_ref, out_ref, rows, result, in_sems, out_sems):
-    size = result.shape[0] // CHUNKS
-    parts = [pl.ds(i * size, size) for i in range(CHUNKS)]
+def transform_kernel(
+    rows_ref, weight_ref, head_ref, tail_ref, out_ref, rows, result, in_sems, out_sems
+):
+    total, levels = rows.shape
+    tails = SEG - HEAD
+    segments = total // HEAD
+    piece = total // LOADS
     loads = [
-        pltpu.make_async_copy(rows_ref.at[part], rows.at[part], in_sems.at[i])
-        for i, part in enumerate(parts)
-    ]
-    stores = [
-        pltpu.make_async_copy(result.at[part], out_ref.at[part], out_sems.at[i])
-        for i, part in enumerate(parts)
+        pltpu.make_async_copy(
+            rows_ref.at[pl.ds(i * piece, piece)], rows.at[pl.ds(i * piece, piece)], in_sems.at[i]
+        )
+        for i in range(LOADS)
     ]
     for load in loads:
         load.start()
+    forward = (((0,), (0,)), ((), ()))
+    back = (((1,), (1,)), ((), ()))
     spectrum = 0.0
-    for load, part in zip(loads, parts):
+    for i, load in enumerate(loads):
         load.wait()
+        part = pl.ds(i * piece, piece)
         spectrum += lax.dot_general(
-            rows[part], table_ref[part], (((0,), (0,)), ((), ())), preferred_element_type=jnp.float32
-        )
+            rows[part], head_ref[part], forward, preferred_element_type=jnp.float32
+        )
+    tail = tail_of(rows[...].astype(jnp.float32).reshape(segments, HEAD, levels))
+    tail = tail.reshape(segments * tails, levels).astype(jnp.bfloat16)
+    spectrum += lax.dot_general(tail, tail_ref[...], forward, preferred_element_type=jnp.float32)
     weighted = (spectrum * weight_ref[...]).astype(jnp.bfloat16)
-    for store, part in zip(stores, parts):
-        result[part] = lax.dot_general(
-            table_ref[part], weighted, (((1,), (1,)), ((), ())), preferred_element_type=jnp.float32
-        ).astype(jnp.bfloat16)
-        store.start()
+    tail = lax.dot_general(tail_ref[...], weighted, back, preferred_element_type=jnp.float32)
+    tail = tail.reshape(segments, tails, levels)
+    count = segments // CHUNKS
+    stores = []
+    for i in range(CHUNKS):
+        part = pl.ds(i * count * HEAD, count * HEAD)
+        head = lax.dot_general(head_ref[part], weighted, back, preferred_element_type=jnp.float32)
+        head = squeeze(head.reshape(count, HEAD, levels), tail[i * count : (i + 1) * count])
+        result[part] = head.reshape(count * HEAD, levels).astype(jnp.bfloat16)
+        stores.append(pltpu.make_async_copy(result.at[part], out_ref.at[part], out_sems.at[i]))
+        stores[i].start()
     for store in stores:
         store.wait()
 
@@ -97,6 +158,7 @@
     filt_ref,
     courant_ref,
     wide_ref,
+    rest_ref,
     filt,
     wind_ref,
     sems,
@@ -109,9 +171,12 @@
     size = width * lat_rows
     damp = jnp.broadcast_to(factor_ref[lax.axis_index("lat"), 0], (lat_rows, levels))
     stores = []
+    for r in range(lat_rows):
+        rest_ref[r] = expand(low_ref[fields * lat_rows + r].astype(jnp.float32))
     for f in range(fields):
         for r in range(lat_rows):
-            wide_ref[f, pl.ds(r, SEG, stride=lat_rows), :] = low_ref[f * lat_rows + r].astype(jnp.float32)
+            row = expand(low_ref[f * lat_rows + r].astype(jnp.float32))
+            wide_ref[f, pl.ds(r, SEG, stride=lat_rows), :] = with_rest(row, rest_ref[r], f)
         low = wide_ref[f, :size].reshape(width, lat_rows, levels)
         value = (damp[None] * tend_ref[f].astype(jnp.float32) + low).astype(jnp.bfloat16)
         filt[f] = value
@@ -169,7 +234,8 @@
     below_wide[:, :width] = below_ref[...].astype(jnp.float32)
     top_wide[:, :width] = top_ref[...].astype(jnp.float32)
     filt = factor_ref[lat, 4, 0:1] * below_wide[count + 1, :width]
-    filt = (filt + next_low_ref[:width].astype(jnp.float32)).astype(jnp.bfloat16)
+    row, rest = (expand(next_low_ref[i].astype(jnp.float32)) for i in range(2))
+    filt = (filt + with_rest(row, rest, 1)[:width]).astype(jnp.bfloat16)
     north_ref[:width] = 0.25 * jnp.tanh(below_wide[count, :width] + filt.astype(jnp.float32))
     loads[pieces - 1].wait()
     east = courant_ref[0, width]
@@ -259,11 +325,11 @@
         pack_kernel,
         in_specs=[hbm],
         out_specs=hbm,
-        out_shape=pltpu.HBM((segments, SEG, levels), bf16),
+        out_shape=pltpu.HBM((segments, HEAD, levels), bf16),
         scratch_shapes=[
             pltpu.VMEM(tendencies.shape, bf16),
-            pltpu.VMEM((fields, width * lat_rows, levels), jnp.float32),
-            pltpu.VMEM((segments, SEG, levels), bf16),
+            pltpu.VMEM((fields, SEG * lat_rows, levels), jnp.float32),
+            pltpu.VMEM((segments, HEAD, levels), bf16),
             pltpu.SemaphoreType.DMA((fields,)),
             pltpu.SemaphoreType.DMA((segments // lat_rows,)),
         ],
@@ -283,11 +349,15 @@
     weight = (1.0 - damping) * jnp.asarray(fold, jnp.float32)[None]
     weight = jnp.where(jnp.asarray(waves)[None] <= bands[row], weight, 0.0)
     with jax.named_scope("table"):
-        table = (
-            jnp.asarray(p_one)[:, None, :] * jnp.asarray(q_one)[None, :, :]
-            + jnp.asarray(p_two)[:, None, :] * jnp.asarray(q_two)[None, :, :]
-        )
-        table = table.astype(bf16).reshape(segments * SEG, COEF)
+        head_table, tail_table = (
+            (
+                jnp.asarray(p_one)[:, None, :] * jnp.asarray(q_one[part])[None, :, :]
+                + jnp.asarray(p_two)[:, None, :] * jnp.asarray(q_two[part])[None, :, :]
+            )
+            .astype(bf16)
+            .reshape(-1, COEF)
+            for part in (slice(0, HEAD), slice(HEAD, SEG))
+        )
 
     with jax.named_scope("edges"):
         high = jnp.concatenate(
@@ -301,34 +371,40 @@
     with jax.named_scope("columns"):
         high = lax.ppermute(high, "lon", west_ring)
         side = lax.ppermute(side, "lon", east_ring)
-    rows, table, weight, factors, high, side, below, top = lax.optimization_barrier(
-        (rows, table, weight, factors, high, side, below, top)
+    rows, head_table, tail_table, weight, high, side, below, top = lax.optimization_barrier(
+        (rows, head_table, tail_table, weight, high, side, below, top)
     )
 
     low = pl.pallas_call(
         transform_kernel,
-        in_specs=[hbm, vmem, vmem],
+        in_specs=[hbm, vmem, vmem, vmem],
         out_specs=hbm,
-        out_shape=pltpu.HBM((segments * SEG, levels), bf16),
+        out_shape=pltpu.HBM((segments * HEAD, levels), bf16),
         scratch_shapes=[
-            pltpu.VMEM((segments * SEG, levels), bf16),
-            pltpu.VMEM((segments * SEG, levels), bf16),
-            pltpu.SemaphoreType.DMA((CHUNKS,)),
+            pltpu.VMEM((segments * HEAD, levels), bf16),
+            pltpu.VMEM((segments * HEAD, levels), bf16),
+            pltpu.SemaphoreType.DMA((LOADS,)),
             pltpu.SemaphoreType.DMA((CHUNKS,)),
         ],
         compiler_params=params,
         name="transform",
-    )(in_hbm(rows.reshape(segments * SEG, levels)), in_vmem(weight), in_vmem(table))
+    )(
+        in_hbm(rows.reshape(segments * HEAD, levels)),
+        in_vmem(weight),
+        in_vmem(head_table),
+        in_vmem(tail_table),
+    )
     low, below, top = lax.optimization_barrier((low, below, top))
     with jax.named_scope("back"):
         low = lax.all_to_all(
-            low.reshape(segments, SEG, levels), "lon", split_axis=0, concat_axis=0, tiled=True
+            low.reshape(segments, HEAD, levels), "lon", split_axis=0, concat_axis=0, tiled=True
         )
     with jax.named_scope("below"):
         below = lax.ppermute(below, "lat", to_prior)
     with jax.named_scope("top"):
         top = lax.ppermute(top, "lat", to_next)
-    next_low = lax.ppermute(low[lat_rows], "lat", to_prior[: lat_devices // 2 - 1])
+    next_low = jnp.stack([low[lat_rows], low[fields * lat_rows]])
+    next_low = lax.ppermute(next_low, "lat", to_prior[: lat_devices // 2 - 1])
 
     filtered, courant = pl.pallas_call(
         filter_kernel,
@@ -340,6 +416,7 @@
         ],
         scratch_shapes=[
             pltpu.VMEM((fields, SEG * lat_rows, levels), jnp.float32),
+            pltpu.VMEM((lat_rows, SEG, levels), jnp.float32),
             pltpu.VMEM(tendencies.shape, bf16),
             pltpu.VMEM(winds.shape, jnp.float32),
             pltpu.SemaphoreType.DMA((fields,)),

time: 81.2 us -> 76.6 us (0.943)
  waiting for transfers between devices: 21.8 us -> 17.2 us
    ppermute x1, waiting for transfers between devices: 10.1 us -> 7.69 us  [per_device(): side = lax.ppermute(side, 'lon', east_ring)]
    all_to_all x1, waiting for transfers between devices: 11 us -> 8.75 us  [per_device(): lax.all_to_all(low.reshape(segments, HEAD, levels), 'lon', split_axis=0,...]
  transfers between devices with their start and end apart: 7 -> 7, of which waited for: 3 -> 3; matrix products, arithmetic and copies ran while one was open for 5% -> 4% of each run, Pallas kernels for 3% -> 3%
where the time goes in v4:
time: 76.6 us; the launch traced here: 76.2 us
  starting transfers between devices  42.2 us (55%)
  waiting for transfers between devices  17.2 us (22%)
  Pallas kernels  12.6 us (16%)
  local copies, waits for them, and re-layouts  1.8 us (2%)
  other arithmetic  1.43 us (2%)
  between operations  1.01 us (1%)
    all_to_all x1, starting transfers between devices, per_device(): rows = lax.all_to_all(send, 'lon', split_axis=0, concat_axis=0, tiled=True)  13.9 us
    all_to_all x1, waiting for transfers between devices, per_device(): lax.all_to_all(low.reshape(segments, HEAD, levels), 'lon', split_axis=0,...  8.75 us
    ppermute x1, waiting for transfers between devices, per_device(): side = lax.ppermute(side, 'lon', east_ring)  7.69 us
    all_to_all x1, starting transfers between devices, per_device(): lax.all_to_all(low.reshape(segments, HEAD, levels), 'lon', split_axis=0,...  7.64 us
    ppermute x1, starting transfers between devices, per_device(): next_low = lax.ppermute(next_low, 'lat', to_prior[:lat_devices // 2 - 1])  6.55 us
    ppermute x1, starting transfers between devices, per_device(): top = lax.ppermute(top, 'lat', to_next)  6.27 us
    ppermute x1, starting transfers between devices, per_device(): high = lax.ppermute(high, 'lon', west_ring)  4.82 us
    pallas_call x1, Pallas kernels, per_device(): pl.pallas_call(transform_kernel, in_specs=[hbm, vmem, vmem, vmem], out_sp...  3.83 us
  transfers between devices with their start and end apart: 7, of which 3 were waited for; matrix products, arithmetic and copies ran while one was open for 4% of the time, Pallas kernels for 3%

profile of v4, /device:TPU:1, one launch (start us, length us, event | category | flops | bytes accessed | tf_op | source)
XLA Modules:
  0.0 76.2 jit_solution(12823006908471768258)
XLA Ops:
  0.6 0.0 copy-start.2
  0.6 3.1 %pack.1 = bf16[64,40,128]{2,1,0:T(8,128)(2,1)} custom-call(bf16[3,45,16,128]{3,2,1,0:T(8,128)(2,1)} %bitcast.39), custom_call_target="tpu_custom_call" | custom-call | tf_op jit(solution)/shard_map/pack/pallas_call | solution.py:324
  3.8 0.0 copy-start
  3.8 13.9 %all-to-all-start = ((bf16[64,40,128]{2,1,0:T(8,128)(2,1)}), bf16[64,40,128]{2,1,0:T(8,128)(2,1)}, u32[]{:S(2)}, u32[]{:S(2)}) async-start(bf16[64,40,128]{2,1,0:T(8,128)(2,1)} %pack.1), calls=%async_computation | async-start | bytes 1310720 | tf_op jit(solution)/shard_map/forth/all_to_all | solution.py:340
  17.7 0.0 copy-done.2
  17.7 0.0 copy-start.3
  17.8 0.6 copy.48
  18.4 0.0 copy-start.12
  18.4 0.0 copy-start.10
  18.4 0.0 copy-start.11
  18.4 0.0 copy-start.4
  18.4 0.0 copy-start.5
  18.4 0.0 copy-start.8
  18.5 0.0 copy-start.9
  18.5 0.0 copy-start.6
  18.5 0.0 copy-start.7
  18.5 0.1 fusion.1
  18.6 1.0 %collective-permute-start.1 = (bf16[5,16,128]{2,1,0:T(8,128)(2,1)S(1)}, bf16[5,16,128]{2,1,0:T(8,128)(2,1)S(1)}, u32[]{:S(2)}, u32[]{:S(2)}) collective-permute-start(bf16[5,16,128]{2,1,0:T(8,128)(2,1)S(1)} %bitcast.52), channel_id=1, source_target_pairs={{0,1},{1,2},{2,3},{3,4},{4,5},{5,6},{6,7},{7,8},{8,9},{9,10},{10,1... | collective-permute-start | bytes 61448 | tf_op jit(solution)/shard_map/columns/ppermute | solution.py:373
  19.6 0.0 copy-done
  19.6 0.2 copy.50
  19.8 0.0 copy-done.3
  19.8 0.2 copy.49
  20.1 4.8 %collective-permute-start = (bf16[7,16,128]{2,1,0:T(8,128)(2,1)S(1)}, bf16[7,16,128]{2,1,0:T(8,128)(2,1)S(1)}, u32[]{:S(2)}, u32[]{:S(2)}) collective-permute-start(bf16[7,16,128]{2,1,0:T(8,128)(2,1)S(1)} %pad_maximum_fusion.1), channel_id=1, source_target_pairs={{1,0},{2,1},{3,2},{4,3},{5,4},{6,5},{7,6},{8,7},{9,8},{10,9},{11,1... | collective-permute-start | bytes 86024 | tf_op jit(solution)/shard_map/columns/ppermute | solution.py:372
  24.9 0.0 copy-done.12
  24.9 0.6 dynamic_slice.3
  25.5 0.0 copy-done.10
  25.5 0.0 copy-done.11
  25.5 0.6 multiply_select_fusion
  26.2 0.0 copy-done.4
  26.2 0.0 copy-done.5
  26.2 0.0 copy-done.8
  26.2 0.0 copy-done.9
  26.2 0.1 fusion.tail_ref
  26.4 0.6 add_convert_fusion
  27.1 7.7 %collective-permute-done.1.side_ref = bf16[5,16,128]{2,1,0:T(8,128)(2,1)S(1)} collective-permute-done((bf16[5,16,128]{2,1,0:T(8,128)(2,1)S(1)}, bf16[5,16,128]{2,1,0:T(8,128)(2,1)S(1)}, u32[]{:S(2)}, u32[]{:S(2)}) %collective-permute-start.1) | collective-permute-done | bytes 20512 | tf_op jit(solution)/shard_map/columns/ppermute | solution.py:373
  34.7 0.0 collective-permute-done.high_ref
  34.7 0.7 all-to-all-done
  35.5 3.8 %transform.1 = bf16[2560,128]{1,0:T(8,128)(2,1)} custom-call(bf16[2560,128]{1,0:T(8,128)(2,1)} %bitcast.13.rows_ref, f32[1,384]{1,0:T(1,128)S(1)} %select_n.25.weight_ref, bf16[2560,384]{1,0:T(8,128)(2,1)S(1)} %bitcast.38, bf16[512,384]{1,0:T(8,128)(2,1)S(1)} %fusion.tail_ref), custom_call_target="tpu_custom_call" | custom-call | tf_op jit(solution)/shard_map/transform/pallas_call | solution.py:378
  39.3 7.6 %all-to-all-start.1 = ((bf16[64,40,128]{2,1,0:T(8,128)(2,1)}), bf16[64,40,128]{2,1,0:T(8,128)(2,1)S(1)}, u32[]{:S(2)}, u32[]{:S(2)}) async-start(bf16[64,40,128]{2,1,0:T(8,128)(2,1)} %bitcast.43), calls=%async_computation.1 | async-start | bytes 1310720 | tf_op jit(solution)/shard_map/back/all_to_all | solution.py:399
  47.0 6.3 %collective-permute-start.3 = (bf16[5,45,128]{2,1,0:T(8,128)(2,1)S(1)}, bf16[5,45,128]{2,1,0:T(8,128)(2,1)S(1)}, u32[]{:S(2)}, u32[]{:S(2)}) collective-permute-start(bf16[5,45,128]{2,1,0:T(8,128)(2,1)S(1)} %get-tuple-element.27), channel_id=1, source_target_pairs={{0,64},{64,128},{128,192},{1,65},{65,129},{129,193},{2,66},{66,130... | collective-permute-start | bytes 172808 | tf_op jit(solution)/shard_map/top/ppermute | solution.py:405
  53.2 1.9 %collective-permute-start.2 = (bf16[7,45,128]{2,1,0:T(8,128)(2,1)S(1)}, bf16[7,45,128]{2,1,0:T(8,128)(2,1)S(1)}, u32[]{:S(2)}, u32[]{:S(2)}) collective-permute-start(bf16[7,45,128]{2,1,0:T(8,128)(2,1)S(1)} %pad_maximum_fusion), channel_id=1, source_target_pairs={{64,0},{128,64},{192,128},{65,1},{129,65},{193,129},{66,2},{130,66... | collective-permute-start | bytes 241928 | tf_op jit(solution)/shard_map/below/ppermute | solution.py:403
  55.2 8.8 %all-to-all-done.1.low_ref = bf16[64,40,128]{2,1,0:T(8,128)(2,1)S(1)} async-done(((bf16[64,40,128]{2,1,0:T(8,128)(2,1)}), bf16[64,40,128]{2,1,0:T(8,128)(2,1)S(1)}, u32[]{:S(2)}, u32[]{:S(2)}) %all-to-all-start.1) | async-done | bytes 655392 | tf_op jit(solution)/shard_map/back/all_to_all | solution.py:399
  63.9 6.6 %collective-permute-start.4 = (bf16[2,40,128]{2,1,0:T(8,128)(2,1)S(1)}, bf16[2,40,128]{2,1,0:T(8,128)(2,1)S(1)}, u32[]{:S(2)}, u32[]{:S(2)}) collective-permute-start(bf16[2,40,128]{2,1,0:T(8,128)(2,1)S(1)} %pad_maximum_fusion.2), channel_id=1, source_target_pairs={{64,0},{65,1},{66,2},{67,3},{68,4},{69,5},{70,6},{71,7},{72,8},{73... | collective-permute-start | bytes 61448 | tf_op jit(solution)/shard_map/ppermute | solution.py:407
  70.5 2.3 %filter.1 = (bf16[3,45,16,128]{3,2,1,0:T(8,128)(2,1)}, f32[2,46,16,128]{3,2,1,0:T(8,128)S(1)}) custom-call(bf16[64,40,128]{2,1,0:T(8,128)(2,1)S(1)} %all-to-all-done.1.low_ref, f32[4,5,16,1]{3,2,1,0:T(8,128)S(1)} %copy-done.1, bf16[3,45,16,128]{3,2,1,0:T(8,128)(2,1)S(1)} %bitcast.40, f32[2,45,16,128]{3,2,1,0:T(8,128)} %bitcast.42, ...), custom_call_target="tpu_custom_call" | custom-call | tf_op jit(solution)/shard_map/filter/pallas_call | solution.py:409
  72.8 0.0 collective-permute-done.3.top_ref
  72.8 0.0 collective-permute-done.2.below_ref
  72.9 0.0 collective-permute-done.4.next_low_ref
  72.9 3.3 %advect.1 = f32[5,45,16,128]{3,2,1,0:T(8,128)} custom-call(f32[2,46,16,128]{3,2,1,0:T(8,128)S(1)} %get-tuple-element.24.courant_ref, f32[4,5,16,1]{3,2,1,0:T(8,128)S(1)} %copy-done.1, f32[5,45,16,128]{3,2,1,0:T(8,128)} %bitcast.41, bf16[7,16,128]{2,1,0:T(8,128)(2,1)S(1)} %collective-permute-done.high_ref, ...), custom_call_target="tpu_custom_call" | custom-call | tf_op jit(solution)/shard_map/advect/pallas_call | solution.py:428
  (16 shorter events, 0.1 us)
Async XLA Ops:
  0.6 17.1 %copy-start.2 = (f32[5,16,45,128]{3,1,2,0:T(8,128)S(1)}, f32[5,16,45,128]{3,1,2,0:T(8,128)}, u32[]{:S(2)}) copy-start(f32[5,16,45,128]{3,1,2,0:T(8,128)} %param.16) | copy-start | bytes 5529604
  3.8 15.8 %copy-start = (bf16[3,16,45,128]{3,1,2,0:T(8,128)(2,1)S(1)}, bf16[3,16,45,128]{3,1,2,0:T(8,128)(2,1)}, u32[]{:S(2)}) copy-start(bf16[3,16,45,128]{3,1,2,0:T(8,128)(2,1)} %param.13) | copy-start | bytes 1658884
  3.8 31.7 %all-to-all-start = ((bf16[64,40,128]{2,1,0:T(8,128)(2,1)}), bf16[64,40,128]{2,1,0:T(8,128)(2,1)}, u32[]{:S(2)}, u32[]{:S(2)}) async-start(bf16[64,40,128]{2,1,0:T(8,128)(2,1)} %pack.1), calls=%async_computation | async-start | bytes 1310720 | tf_op jit(solution)/shard_map/forth/all_to_all | solution.py:340
  17.7 2.0 %copy-start.3 = (f32[2,16,45,128]{3,1,2,0:T(8,128)S(1)}, f32[2,16,45,128]{3,1,2,0:T(8,128)}, u32[]{:S(2)}) copy-start(f32[2,16,45,128]{3,1,2,0:T(8,128)} %param.15) | copy-start | bytes 2211844
  18.4 6.5 %copy-start.12 = (s32[64]{0:T(128)S(1)}, s32[64]{0:T(128)}, u32[]{:S(2)}) copy-start(s32[64]{0:T(128)} %param.14) | copy-start | bytes 772
  18.4 7.1 %copy-start.10 = (s32[384]{0:T(512)S(1)}, s32[384]{0:T(512)}, u32[]{:S(2)}) copy-start(s32[384]{0:T(512)} %constant.59.clone) | copy-start | bytes 4612
  18.4 7.1 %copy-start.11 = (f32[384]{0:T(512)S(1)}, f32[384]{0:T(512)}, u32[]{:S(2)}) copy-start(f32[384]{0:T(512)} %constant.58.clone) | copy-start | bytes 4612
  18.4 7.8 %copy-start.4 = (f32[64,384]{1,0:T(8,128)S(1)}, f32[64,384]{1,0:T(8,128)}, u32[]{:S(2)}) copy-start(f32[64,384]{1,0:T(8,128)} %constant.62.clone) | copy-start | bytes 294916
  18.4 7.8 %copy-start.5 = (f32[64,384]{1,0:T(8,128)S(1)}, f32[64,384]{1,0:T(8,128)}, u32[]{:S(2)}) copy-start(f32[64,384]{1,0:T(8,128)} %constant.60.clone) | copy-start | bytes 294916
  18.4 7.8 %copy-start.8 = (f32[8,384]{1,0:T(8,128)S(1)}, f32[8,384]{1,0:T(8,128)}, u32[]{:S(2)}) copy-start(f32[8,384]{1,0:T(8,128)} %constant.65.clone) | copy-start | bytes 36868
  18.5 7.8 %copy-start.9 = (f32[8,384]{1,0:T(8,128)S(1)}, f32[8,384]{1,0:T(8,128)}, u32[]{:S(2)}) copy-start(f32[8,384]{1,0:T(8,128)} %constant.64.clone) | copy-start | bytes 36868
  18.5 7.9 %copy-start.6 = (f32[40,384]{1,0:T(8,128)S(1)}, f32[40,384]{1,0:T(8,128)}, u32[]{:S(2)}) copy-start(f32[40,384]{1,0:T(8,128)} %constant.63.clone) | copy-start | bytes 184324
  18.5 7.9 %copy-start.7 = (f32[40,384]{1,0:T(8,128)S(1)}, f32[40,384]{1,0:T(8,128)}, u32[]{:S(2)}) copy-start(f32[40,384]{1,0:T(8,128)} %constant.61.clone) | copy-start | bytes 184324
  18.6 16.2 %collective-permute-start.1 = (bf16[5,16,128]{2,1,0:T(8,128)(2,1)S(1)}, bf16[5,16,128]{2,1,0:T(8,128)(2,1)S(1)}, u32[]{:S(2)}, u32[]{:S(2)}) collective-permute-start(bf16[5,16,128]{2,1,0:T(8,128)(2,1)S(1)} %bitcast.52), channel_id=1, source_target_pairs={{0,1},{1,2},{2,3},{3,4},{4,5},{5,6},{6,7},{7,8},{8,9},{9,10},{10,1... | collective-permute-start | bytes 61448 | tf_op jit(solution)/shard_map/columns/ppermute | solution.py:373
  20.1 14.6 %collective-permute-start = (bf16[7,16,128]{2,1,0:T(8,128)(2,1)S(1)}, bf16[7,16,128]{2,1,0:T(8,128)(2,1)S(1)}, u32[]{:S(2)}, u32[]{:S(2)}) collective-permute-start(bf16[7,16,128]{2,1,0:T(8,128)(2,1)S(1)} %pad_maximum_fusion.1), channel_id=1, source_target_pairs={{1,0},{2,1},{3,2},{4,3},{5,4},{6,5},{7,6},{8,7},{9,8},{10,9},{11,1... | collective-permute-start | bytes 86024 | tf_op jit(solution)/shard_map/columns/ppermute | solution.py:372
  35.5 35.0 %copy-start.1 = (f32[4,5,16,1]{3,2,1,0:T(8,128)S(1)}, f32[4,5,16,1]{3,2,1,0:T(8,128)}, u32[]{:S(2)}) copy-start(f32[4,5,16,1]{3,2,1,0:T(8,128)} %constant.57.clone.factor_ref) | copy-start | bytes 3844
  39.3 24.6 %all-to-all-start.1 = ((bf16[64,40,128]{2,1,0:T(8,128)(2,1)}), bf16[64,40,128]{2,1,0:T(8,128)(2,1)S(1)}, u32[]{:S(2)}, u32[]{:S(2)}) async-start(bf16[64,40,128]{2,1,0:T(8,128)(2,1)} %bitcast.43), calls=%async_computation.1 | async-start | bytes 1310720 | tf_op jit(solution)/shard_map/back/all_to_all | solution.py:399
  47.0 25.9 %collective-permute-start.3 = (bf16[5,45,128]{2,1,0:T(8,128)(2,1)S(1)}, bf16[5,45,128]{2,1,0:T(8,128)(2,1)S(1)}, u32[]{:S(2)}, u32[]{:S(2)}) collective-permute-start(bf16[5,45,128]{2,1,0:T(8,128)(2,1)S(1)} %get-tuple-element.27), channel_id=1, source_target_pairs={{0,64},{64,128},{128,192},{1,65},{65,129},{129,193},{2,66},{66,130... | collective-permute-start | bytes 172808 | tf_op jit(solution)/shard_map/top/ppermute | solution.py:405
  53.2 19.6 %collective-permute-start.2 = (bf16[7,45,128]{2,1,0:T(8,128)(2,1)S(1)}, bf16[7,45,128]{2,1,0:T(8,128)(2,1)S(1)}, u32[]{:S(2)}, u32[]{:S(2)}) collective-permute-start(bf16[7,45,128]{2,1,0:T(8,128)(2,1)S(1)} %pad_maximum_fusion), channel_id=1, source_target_pairs={{64,0},{128,64},{192,128},{65,1},{129,65},{193,129},{66,2},{130,66... | collective-permute-start | bytes 241928 | tf_op jit(solution)/shard_map/below/ppermute | solution.py:403
  63.9 8.9 %collective-permute-start.4 = (bf16[2,40,128]{2,1,0:T(8,128)(2,1)S(1)}, bf16[2,40,128]{2,1,0:T(8,128)(2,1)S(1)}, u32[]{:S(2)}, u32[]{:S(2)}) collective-permute-start(bf16[2,40,128]{2,1,0:T(8,128)(2,1)S(1)} %pad_maximum_fusion.2), channel_id=1, source_target_pairs={{64,0},{65,1},{66,2},{67,3},{68,4},{69,5},{70,6},{71,7},{72,8},{73... | collective-permute-start | bytes 61448 | tf_op jit(solution)/shard_map/ppermute | solution.py:407

commit v5 on v4

--- a/solution.py
+++ b/solution.py
@@ -1,3 +1,4 @@
+import functools
 import math
 
 import jax
@@ -149,28 +150,92 @@
         store.wait()
 
 
-def filter_kernel(
+def finish_kernel(late, waiting_bands, fields, *refs):
+    refs = list(refs)
+    low_ref, factor_ref, tend_ref, wind_hbm, tracer_hbm, high_ref, side_ref, below_ref, top_ref = refs[:9]
+    refs = refs[9:]
+    lat = lax.axis_index("lat")
+    lat_rows = tend_ref.shape[2]
+    if late:
+        next_low_ref, _, _, filt_hbm, out_hbm = refs[:5]
+        refs = refs[5:]
+        due = lat < waiting_bands
+    else:
+        filt_hbm, out_hbm, first_ref = refs[:3]
+        refs = refs[3:]
+        next_low_ref = None
+        due = lat >= waiting_bands
+        first_ref[0] = low_ref[lat_rows]
+        first_ref[1] = low_ref[fields * lat_rows]
+
+    @pl.when(due)
+    def _():
+        finish(
+            lat,
+            low_ref,
+            factor_ref,
+            tend_ref,
+            wind_hbm,
+            tracer_hbm,
+            high_ref,
+            side_ref,
+            below_ref,
+            top_ref,
+            next_low_ref,
+            filt_hbm,
+            out_hbm,
+            *refs,
+        )
+
+
+def finish(
+    lat,
     low_ref,
     factor_ref,
     tend_ref,
     wind_hbm,
+    tracer_hbm,
     high_ref,
-    filt_ref,
-    courant_ref,
+    side_ref,
+    below_ref,
+    top_ref,
+    next_low_ref,
+    filt_hbm,
+    out_hbm,
     wide_ref,
     rest_ref,
     filt,
     wind_ref,
-    sems,
+    courant_ref,
+    tracer_ref,
+    out_ref,
+    north_ref,
+    below_wide,
+    top_wide,
+    filt_sems,
     wind_sems,
+    in_sems,
+    out_sems,
 ):
     fields, width, lat_rows, levels = tend_ref.shape
-    loads = [pltpu.make_async_copy(wind_hbm.at[f], wind_ref.at[f], wind_sems.at[f]) for f in range(2)]
-    for load in loads:
+    count = tracer_ref.shape[0]
+    size = width * lat_rows
+    pieces = width // COLS
+    winds = [pltpu.make_async_copy(wind_hbm.at[f], wind_ref.at[f], wind_sems.at[f]) for f in range(2)]
+    loads = []
+    stores = []
+    for i in range(pieces):
+        part = pl.ds(i * COLS, COLS)
+        loads.append(
+            pltpu.make_async_copy(tracer_hbm.at[:, part], tracer_ref.at[:, part], in_sems.at[i])
+        )
+        stores.append(pltpu.make_async_copy(out_ref.at[:, part], out_hbm.at[:, part], out_sems.at[i]))
+    for load in winds + loads[::-1]:
         load.start()
-    size = width * lat_rows
-    damp = jnp.broadcast_to(factor_ref[lax.axis_index("lat"), 0], (lat_rows, levels))
-    stores = []
+    damp, face, face_next, inverse = (
+        jnp.broadcast_to(factor_ref[lat, i], (lat_rows, levels)) for i in range(4)
+    )
+
     for r in range(lat_rows):
         rest_ref[r] = expand(low_ref[fields * lat_rows + r].astype(jnp.float32))
     for f in range(fields):
@@ -180,63 +245,27 @@
         low = wide_ref[f, :size].reshape(width, lat_rows, levels)
         value = (damp[None] * tend_ref[f].astype(jnp.float32) + low).astype(jnp.bfloat16)
         filt[f] = value
-        stores.append(pltpu.make_async_copy(filt.at[f], filt_ref.at[f], sems.at[f]))
-        stores[f].start()
+        stores.append(pltpu.make_async_copy(filt.at[f], filt_hbm.at[f], filt_sems.at[f]))
+        stores[-1].start()
         if f < 2:
-            loads[f].wait()
+            winds[f].wait()
             courant_ref[f, :width] = (0.5, 0.25)[f] * jnp.tanh(wind_ref[f] + value.astype(jnp.float32))
         if f == 0:
-            last = high_ref.shape[0] - 1
-            edge = damp * high_ref[last].astype(jnp.float32) + wide_ref[f, size : size + lat_rows]
+            edge = damp * high_ref[count + 1].astype(jnp.float32) + wide_ref[f, size : size + lat_rows]
             edge = edge.astype(jnp.bfloat16).astype(jnp.float32)
-            courant_ref[f, width] = 0.5 * jnp.tanh(high_ref[last - 1].astype(jnp.float32) + edge)
-    for store in stores:
-        store.wait()
-
-
-def advect_kernel(
-    courant_ref,
-    factor_ref,
-    tracer_hbm,
-    high_ref,
-    side_ref,
-    below_ref,
-    top_ref,
-    next_low_ref,
-    out_hbm,
-    tracer_ref,
-    out_ref,
-    north_ref,
-    below_wide,
-    top_wide,
-    in_sems,
-    out_sems,
-):
-    count, width, lat_rows, levels = tracer_ref.shape
-    pieces = width // COLS
-    loads = []
-    stores = []
-    for i in range(pieces):
-        part = pl.ds(i * COLS, COLS)
-        loads.append(
-            pltpu.make_async_copy(tracer_hbm.at[:, part], tracer_ref.at[:, part], in_sems.at[i])
-        )
-        stores.append(pltpu.make_async_copy(out_ref.at[:, part], out_hbm.at[:, part], out_sems.at[i]))
-    for load in reversed(loads):
-        load.start()
-    lat = lax.axis_index("lat")
-    face, face_next, inverse = (
-        jnp.broadcast_to(factor_ref[lat, i], (lat_rows, levels)) for i in (1, 2, 3)
-    )
+            courant_ref[f, width] = 0.5 * jnp.tanh(high_ref[count].astype(jnp.float32) + edge)
+
     sublane = lax.broadcasted_iota(jnp.int32, (lat_rows, levels), 0)
     is_first = sublane == 0
     is_last = sublane == lat_rows - 1
     below_wide[:, :width] = below_ref[...].astype(jnp.float32)
     top_wide[:, :width] = top_ref[...].astype(jnp.float32)
-    filt = factor_ref[lat, 4, 0:1] * below_wide[count + 1, :width]
-    row, rest = (expand(next_low_ref[i].astype(jnp.float32)) for i in range(2))
-    filt = (filt + with_rest(row, rest, 1)[:width]).astype(jnp.bfloat16)
-    north_ref[:width] = 0.25 * jnp.tanh(below_wide[count, :width] + filt.astype(jnp.float32))
+    edge = factor_ref[lat, 4, 0:1] * below_wide[count + 1, :width]
+    if next_low_ref is not None:
+        row, rest = (expand(next_low_ref[i].astype(jnp.float32)) for i in range(2))
+        edge += with_rest(row, rest, 1)[:width]
+    edge = edge.astype(jnp.bfloat16).astype(jnp.float32)
+    north_ref[:width] = 0.25 * jnp.tanh(below_wide[count, :width] + edge)
     loads[pieces - 1].wait()
     east = courant_ref[0, width]
     flux = [
@@ -403,54 +432,56 @@
         below = lax.ppermute(below, "lat", to_prior)
     with jax.named_scope("top"):
         top = lax.ppermute(top, "lat", to_next)
-    next_low = jnp.stack([low[lat_rows], low[fields * lat_rows]])
-    next_low = lax.ppermute(next_low, "lat", to_prior[: lat_devices // 2 - 1])
-
-    filtered, courant = pl.pallas_call(
-        filter_kernel,
-        in_specs=[vmem, vmem, vmem, hbm, vmem],
-        out_specs=[hbm, vmem],
-        out_shape=[
-            pltpu.HBM(tendencies.shape, bf16),
-            pltpu.VMEM((2, width + 1, lat_rows, levels), jnp.float32),
-        ],
-        scratch_shapes=[
-            pltpu.VMEM((fields, SEG * lat_rows, levels), jnp.float32),
-            pltpu.VMEM((lat_rows, SEG, levels), jnp.float32),
-            pltpu.VMEM(tendencies.shape, bf16),
-            pltpu.VMEM(winds.shape, jnp.float32),
-            pltpu.SemaphoreType.DMA((fields,)),
-            pltpu.SemaphoreType.DMA((2,)),
-        ],
-        compiler_params=params,
-        name="filter",
-    )(in_vmem(low), in_vmem(factors), in_vmem(tendencies), in_hbm(winds), in_vmem(high))
-    advected = pl.pallas_call(
-        advect_kernel,
-        in_specs=[vmem, vmem, hbm] + [vmem] * 5,
-        out_specs=hbm,
-        out_shape=pltpu.HBM(tracers.shape, jnp.float32),
-        scratch_shapes=[
-            pltpu.VMEM(tracers.shape, jnp.float32),
-            pltpu.VMEM(tracers.shape, jnp.float32),
-            pltpu.VMEM((SEG, levels), jnp.float32),
-            pltpu.VMEM((count + 2, SEG, levels), jnp.float32),
-            pltpu.VMEM((count, SEG, levels), jnp.float32),
-            pltpu.SemaphoreType.DMA((width // COLS,)),
-            pltpu.SemaphoreType.DMA((width // COLS,)),
-        ],
-        compiler_params=params,
-        name="advect",
-    )(
-        courant,
+    waiting = lat_devices // 2 - 1
+    outs = [pltpu.HBM(tendencies.shape, bf16), pltpu.HBM(tracers.shape, jnp.float32)]
+    scratch = [
+        pltpu.VMEM((fields, SEG * lat_rows, levels), jnp.float32),
+        pltpu.VMEM((lat_rows, SEG, levels), jnp.float32),
+        pltpu.VMEM(tendencies.shape, bf16),
+        pltpu.VMEM(winds.shape, jnp.float32),
+        pltpu.VMEM((2, width + 1, lat_rows, levels), jnp.float32),
+        pltpu.VMEM(tracers.shape, jnp.float32),
+        pltpu.VMEM(tracers.shape, jnp.float32),
+        pltpu.VMEM((SEG, levels), jnp.float32),
+        pltpu.VMEM((count + 2, SEG, levels), jnp.float32),
+        pltpu.VMEM((count, SEG, levels), jnp.float32),
+        pltpu.SemaphoreType.DMA((fields,)),
+        pltpu.SemaphoreType.DMA((2,)),
+        pltpu.SemaphoreType.DMA((width // COLS,)),
+        pltpu.SemaphoreType.DMA((width // COLS,)),
+    ]
+    operands = (
+        in_vmem(low),
         in_vmem(factors),
+        in_vmem(tendencies),
+        in_hbm(winds),
         in_hbm(tracers),
         in_vmem(high),
         in_vmem(side),
         in_vmem(below),
         in_vmem(top),
-        in_vmem(next_low),
     )
+    specs = [vmem] * 3 + [hbm] * 2 + [vmem] * 4
+    filtered, advected, first = pl.pallas_call(
+        functools.partial(finish_kernel, False, waiting, fields),
+        in_specs=specs,
+        out_specs=[hbm, hbm, vmem],
+        out_shape=outs + [jax.ShapeDtypeStruct((2, HEAD, levels), bf16)],
+        scratch_shapes=scratch,
+        compiler_params=params,
+        name="early",
+    )(*operands)
+    next_low = lax.ppermute(first, "lat", to_prior[:waiting])
+    filtered, advected = pl.pallas_call(
+        functools.partial(finish_kernel, True, waiting, fields),
+        in_specs=specs + [vmem, hbm, hbm],
+        out_specs=[hbm, hbm],
+        out_shape=outs,
+        scratch_shapes=scratch,
+        input_output_aliases={10: 0, 11: 1},
+        compiler_params=params,
+        name="late",
+    )(*operands, in_vmem(next_low), filtered, advected)
     return (filtered.transpose(0, 2, 1, 3), advected.transpose(0, 2, 1, 3))
 
 

time: 76.6 us -> 74.7 us (0.975)
  the two profiles are of different devices: /device:TPU:1 before, /device:TPU:2 now
where the time goes in v5:
time: 74.7 us; the launch traced here: 74.3 us
  starting transfers between devices  29.9 us (40%)
  waiting for transfers between devices  28.8 us (39%)
  Pallas kernels  11.4 us (15%)
  local copies, waits for them, and re-layouts  1.8 us (2%)
  other arithmetic  1.42 us (2%)
  between operations  1 us (1%)
    all_to_all x1, waiting for transfers between devices, per_device(): lax.all_to_all(low.reshape(segments, HEAD, levels), 'lon', split_axis=0,...  14 us
    all_to_all x1, starting transfers between devices, per_device(): rows = lax.all_to_all(send, 'lon', split_axis=0, concat_axis=0, tiled=True)  13.4 us
    all_to_all x1, waiting for transfers between devices, per_device(): rows = lax.all_to_all(send, 'lon', split_axis=0, concat_axis=0, tiled=True)  12.1 us
    all_to_all x1, starting transfers between devices, per_device(): lax.all_to_all(low.reshape(segments, HEAD, levels), 'lon', split_axis=0,...  6.61 us
    pallas_call x1, Pallas kernels, per_device(): pl.pallas_call(functools.partial(finish_kernel, True, waiting, fields), i...  4.27 us
    pallas_call x1, Pallas kernels, per_device(): pl.pallas_call(transform_kernel, in_specs=[hbm, vmem, vmem, vmem], out_sp...  3.83 us
    pallas_call x1, Pallas kernels, per_device(): pl.pallas_call(pack_kernel, in_specs=[hbm], out_specs=hbm, out_shape=pltp...  3.12 us
    ppermute x1, starting transfers between devices, per_device(): top = lax.ppermute(top, 'lat', to_next)  3.03 us
  transfers between devices with their start and end apart: 7, of which 4 were waited for; matrix products, arithmetic and copies ran while one was open for 4% of the time, Pallas kernels for 0%

profile of v5, /device:TPU:2, one launch (start us, length us, event | category | flops | bytes accessed | tf_op | source)
XLA Modules:
  0.0 74.3 jit_solution(9429006637293612624)
XLA Ops:
  0.6 0.0 copy-start.2
  0.6 3.1 %pack.1 = bf16[64,40,128]{2,1,0:T(8,128)(2,1)} custom-call(bf16[3,45,16,128]{3,2,1,0:T(8,128)(2,1)} %bitcast.38), custom_call_target="tpu_custom_call" | custom-call | tf_op jit(solution)/shard_map/pack/pallas_call | solution.py:353
  3.8 0.0 copy-start
  3.8 13.4 %all-to-all-start = ((bf16[64,40,128]{2,1,0:T(8,128)(2,1)}), bf16[64,40,128]{2,1,0:T(8,128)(2,1)}, u32[]{:S(2)}, u32[]{:S(2)}) async-start(bf16[64,40,128]{2,1,0:T(8,128)(2,1)} %pack.1), calls=%async_computation | async-start | bytes 1310720 | tf_op jit(solution)/shard_map/forth/all_to_all | solution.py:369
  17.2 0.0 copy-done.2
  17.2 0.0 copy-start.3
  17.2 0.6 copy.57
  17.9 0.0 copy-start.12
  17.9 0.0 copy-start.10
  17.9 0.0 copy-start.11
  17.9 0.0 copy-start.4
  17.9 0.0 copy-start.5
  17.9 0.0 copy-start.8
  17.9 0.0 copy-start.9
  17.9 0.0 copy-start.6
  18.0 0.0 copy-start.7
  18.0 0.1 fusion.1
  18.1 1.5 %collective-permute-start.1 = (bf16[5,16,128]{2,1,0:T(8,128)(2,1)S(1)}, bf16[5,16,128]{2,1,0:T(8,128)(2,1)S(1)}, u32[]{:S(2)}, u32[]{:S(2)}) collective-permute-start(bf16[5,16,128]{2,1,0:T(8,128)(2,1)S(1)} %bitcast.56), channel_id=1, source_target_pairs={{0,1},{1,2},{2,3},{3,4},{4,5},{5,6},{6,7},{7,8},{8,9},{9,10},{10,1... | collective-permute-start | bytes 61448 | tf_op jit(solution)/shard_map/columns/ppermute | solution.py:402
  19.6 0.0 copy-done
  19.6 0.2 copy.59
  19.8 0.0 copy-done.3
  19.8 0.2 copy.58
  20.1 2.7 %collective-permute-start = (bf16[7,16,128]{2,1,0:T(8,128)(2,1)S(1)}, bf16[7,16,128]{2,1,0:T(8,128)(2,1)S(1)}, u32[]{:S(2)}, u32[]{:S(2)}) collective-permute-start(bf16[7,16,128]{2,1,0:T(8,128)(2,1)S(1)} %pad_maximum_fusion.1), channel_id=1, source_target_pairs={{1,0},{2,1},{3,2},{4,3},{5,4},{6,5},{7,6},{8,7},{9,8},{10,9},{11,1... | collective-permute-start | bytes 86024 | tf_op jit(solution)/shard_map/columns/ppermute | solution.py:401
  22.9 0.0 copy-done.12
  22.9 0.6 dynamic_slice.3
  23.4 0.0 copy-done.10
  23.4 0.0 copy-done.11
  23.4 0.6 multiply_select_fusion
  24.1 0.0 copy-done.4
  24.1 0.0 copy-done.5
  24.1 0.0 copy-done.8
  24.2 0.1 fusion.tail_ref
  24.3 0.6 add_convert_fusion
  25.0 0.0 collective-permute-done.1.refs_6_
  25.0 0.0 collective-permute-done.refs_5_
  25.0 12.1 %all-to-all-done = bf16[64,40,128]{2,1,0:T(8,128)(2,1)} async-done(((bf16[64,40,128]{2,1,0:T(8,128)(2,1)}), bf16[64,40,128]{2,1,0:T(8,128)(2,1)}, u32[]{:S(2)}, u32[]{:S(2)}) %all-to-all-start) | async-done | bytes 655392 | tf_op jit(solution)/shard_map/forth/all_to_all | solution.py:369
  37.1 3.8 %transform.1 = bf16[2560,128]{1,0:T(8,128)(2,1)} custom-call(bf16[2560,128]{1,0:T(8,128)(2,1)} %bitcast.13.rows_ref, f32[1,384]{1,0:T(1,128)S(1)} %select_n.25.weight_ref, bf16[2560,384]{1,0:T(8,128)(2,1)S(1)} %bitcast.41, bf16[512,384]{1,0:T(8,128)(2,1)S(1)} %fusion.tail_ref), custom_call_target="tpu_custom_call" | custom-call | tf_op jit(solution)/shard_map/transform/pallas_call | solution.py:407
  41.0 6.6 %all-to-all-start.1 = ((bf16[64,40,128]{2,1,0:T(8,128)(2,1)}), bf16[64,40,128]{2,1,0:T(8,128)(2,1)S(1)}, u32[]{:S(2)}, u32[]{:S(2)}) async-start(bf16[64,40,128]{2,1,0:T(8,128)(2,1)} %bitcast.46), calls=%async_computation.1 | async-start | bytes 1310720 | tf_op jit(solution)/shard_map/back/all_to_all | solution.py:428
  47.6 1.3 %collective-permute-start.2 = (bf16[7,45,128]{2,1,0:T(8,128)(2,1)S(1)}, bf16[7,45,128]{2,1,0:T(8,128)(2,1)S(1)}, u32[]{:S(2)}, u32[]{:S(2)}) collective-permute-start(bf16[7,45,128]{2,1,0:T(8,128)(2,1)S(1)} %pad_maximum_fusion), channel_id=1, source_target_pairs={{64,0},{128,64},{192,128},{65,1},{129,65},{193,129},{66,2},{130,66... | collective-permute-start | bytes 241928 | tf_op jit(solution)/shard_map/below/ppermute | solution.py:432
  48.9 3.0 %collective-permute-start.3 = (bf16[5,45,128]{2,1,0:T(8,128)(2,1)S(1)}, bf16[5,45,128]{2,1,0:T(8,128)(2,1)S(1)}, u32[]{:S(2)}, u32[]{:S(2)}) collective-permute-start(bf16[5,45,128]{2,1,0:T(8,128)(2,1)S(1)} %get-tuple-element.28), channel_id=1, source_target_pairs={{0,64},{64,128},{128,192},{1,65},{65,129},{129,193},{2,66},{66,130... | collective-permute-start | bytes 172808 | tf_op jit(solution)/shard_map/top/ppermute | solution.py:434
  51.9 0.9 %collective-permute-done.3.refs_8_ = bf16[5,45,128]{2,1,0:T(8,128)(2,1)S(1)} collective-permute-done((bf16[5,45,128]{2,1,0:T(8,128)(2,1)S(1)}, bf16[5,45,128]{2,1,0:T(8,128)(2,1)S(1)}, u32[]{:S(2)}, u32[]{:S(2)}) %collective-permute-start.3) | collective-permute-done | bytes 57632 | tf_op jit(solution)/shard_map/top/ppermute | solution.py:434
  52.8 0.0 collective-permute-done.2.refs_7_
  52.8 14.0 %all-to-all-done.1.refs_0_ = bf16[64,40,128]{2,1,0:T(8,128)(2,1)S(1)} async-done(((bf16[64,40,128]{2,1,0:T(8,128)(2,1)}), bf16[64,40,128]{2,1,0:T(8,128)(2,1)S(1)}, u32[]{:S(2)}, u32[]{:S(2)}) %all-to-all-start.1) | async-done | bytes 655392 | tf_op jit(solution)/shard_map/back/all_to_all | solution.py:428
  66.8 0.0 copy-done.1
  66.8 0.1 early.1
  66.9 1.3 %collective-permute-start.4 = (bf16[2,40,128]{2,1,0:T(8,128)(2,1)S(1)}, bf16[2,40,128]{2,1,0:T(8,128)(2,1)S(1)}, u32[]{:S(2)}, u32[]{:S(2)}) collective-permute-start(bf16[2,40,128]{2,1,0:T(8,128)(2,1)S(1)} %get-tuple-element.29), channel_id=1, source_target_pairs={{64,0},{65,1},{66,2},{67,3},{68,4},{69,5},{70,6},{71,7},{72,8},{73... | collective-permute-start | bytes 61448 | tf_op jit(solution)/shard_map/ppermute | solution.py:474
  68.2 1.8 %collective-permute-done.4.refs_9_ = bf16[2,40,128]{2,1,0:T(8,128)(2,1)S(1)} collective-permute-done((bf16[2,40,128]{2,1,0:T(8,128)(2,1)S(1)}, bf16[2,40,128]{2,1,0:T(8,128)(2,1)S(1)}, u32[]{:S(2)}, u32[]{:S(2)}) %collective-permute-start.4) | collective-permute-done | bytes 20512 | tf_op jit(solution)/shard_map/ppermute | solution.py:474
  70.0 4.3 %late.1 = (bf16[3,45,16,128]{3,2,1,0:T(8,128)(2,1)}, f32[5,45,16,128]{3,2,1,0:T(8,128)}) custom-call(bf16[64,40,128]{2,1,0:T(8,128)(2,1)S(1)} %all-to-all-done.1.refs_0_, f32[4,5,16,1]{3,2,1,0:T(8,128)S(1)} %copy-done.1, bf16[3,45,16,128]{3,2,1,0:T(8,128)(2,1)S(1)} %bitcast.40, ...), custom_call_target="tpu_custom_call", output_to_operand_aliasing={{0}: (10, {}), {1}: (11, {})} | custom-call | tf_op jit(solution)/shard_map/late/pallas_call | solution.py:475
  (14 shorter events, 0.1 us)
Async XLA Ops:
  0.6 16.6 %copy-start.2 = (f32[5,16,45,128]{3,1,2,0:T(8,128)S(1)}, f32[5,16,45,128]{3,1,2,0:T(8,128)}, u32[]{:S(2)}) copy-start(f32[5,16,45,128]{3,1,2,0:T(8,128)} %param.16) | copy-start | bytes 5529604
  3.8 15.8 %copy-start = (bf16[3,16,45,128]{3,1,2,0:T(8,128)(2,1)S(1)}, bf16[3,16,45,128]{3,1,2,0:T(8,128)(2,1)}, u32[]{:S(2)}) copy-start(bf16[3,16,45,128]{3,1,2,0:T(8,128)(2,1)} %param.13) | copy-start | bytes 1658884
  3.8 33.3 %all-to-all-start = ((bf16[64,40,128]{2,1,0:T(8,128)(2,1)}), bf16[64,40,128]{2,1,0:T(8,128)(2,1)}, u32[]{:S(2)}, u32[]{:S(2)}) async-start(bf16[64,40,128]{2,1,0:T(8,128)(2,1)} %pack.1), calls=%async_computation | async-start | bytes 1310720 | tf_op jit(solution)/shard_map/forth/all_to_all | solution.py:369
  17.2 2.5 %copy-start.3 = (f32[2,16,45,128]{3,1,2,0:T(8,128)S(1)}, f32[2,16,45,128]{3,1,2,0:T(8,128)}, u32[]{:S(2)}) copy-start(f32[2,16,45,128]{3,1,2,0:T(8,128)} %param.15) | copy-start | bytes 2211844
  17.9 5.0 %copy-start.12 = (s32[64]{0:T(128)S(1)}, s32[64]{0:T(128)}, u32[]{:S(2)}) copy-start(s32[64]{0:T(128)} %param.14) | copy-start | bytes 772
  17.9 5.6 %copy-start.10 = (s32[384]{0:T(512)S(1)}, s32[384]{0:T(512)}, u32[]{:S(2)}) copy-start(s32[384]{0:T(512)} %constant.59.clone) | copy-start | bytes 4612
  17.9 5.6 %copy-start.11 = (f32[384]{0:T(512)S(1)}, f32[384]{0:T(512)}, u32[]{:S(2)}) copy-start(f32[384]{0:T(512)} %constant.58.clone) | copy-start | bytes 4612
  17.9 6.2 %copy-start.4 = (f32[64,384]{1,0:T(8,128)S(1)}, f32[64,384]{1,0:T(8,128)}, u32[]{:S(2)}) copy-start(f32[64,384]{1,0:T(8,128)} %constant.62.clone) | copy-start | bytes 294916
  17.9 6.2 %copy-start.5 = (f32[64,384]{1,0:T(8,128)S(1)}, f32[64,384]{1,0:T(8,128)}, u32[]{:S(2)}) copy-start(f32[64,384]{1,0:T(8,128)} %constant.60.clone) | copy-start | bytes 294916
  17.9 6.2 %copy-start.8 = (f32[8,384]{1,0:T(8,128)S(1)}, f32[8,384]{1,0:T(8,128)}, u32[]{:S(2)}) copy-start(f32[8,384]{1,0:T(8,128)} %constant.65.clone) | copy-start | bytes 36868
  17.9 6.2 %copy-start.9 = (f32[8,384]{1,0:T(8,128)S(1)}, f32[8,384]{1,0:T(8,128)}, u32[]{:S(2)}) copy-start(f32[8,384]{1,0:T(8,128)} %constant.64.clone) | copy-start | bytes 36868
  17.9 6.3 %copy-start.6 = (f32[40,384]{1,0:T(8,128)S(1)}, f32[40,384]{1,0:T(8,128)}, u32[]{:S(2)}) copy-start(f32[40,384]{1,0:T(8,128)} %constant.63.clone) | copy-start | bytes 184324
  18.0 6.3 %copy-start.7 = (f32[40,384]{1,0:T(8,128)S(1)}, f32[40,384]{1,0:T(8,128)}, u32[]{:S(2)}) copy-start(f32[40,384]{1,0:T(8,128)} %constant.61.clone) | copy-start | bytes 184324
  18.1 6.9 %collective-permute-start.1 = (bf16[5,16,128]{2,1,0:T(8,128)(2,1)S(1)}, bf16[5,16,128]{2,1,0:T(8,128)(2,1)S(1)}, u32[]{:S(2)}, u32[]{:S(2)}) collective-permute-start(bf16[5,16,128]{2,1,0:T(8,128)(2,1)S(1)} %bitcast.56), channel_id=1, source_target_pairs={{0,1},{1,2},{2,3},{3,4},{4,5},{5,6},{6,7},{7,8},{8,9},{9,10},{10,1... | collective-permute-start | bytes 61448 | tf_op jit(solution)/shard_map/columns/ppermute | solution.py:402
  20.1 4.9 %collective-permute-start = (bf16[7,16,128]{2,1,0:T(8,128)(2,1)S(1)}, bf16[7,16,128]{2,1,0:T(8,128)(2,1)S(1)}, u32[]{:S(2)}, u32[]{:S(2)}) collective-permute-start(bf16[7,16,128]{2,1,0:T(8,128)(2,1)S(1)} %pad_maximum_fusion.1), channel_id=1, source_target_pairs={{1,0},{2,1},{3,2},{4,3},{5,4},{6,5},{7,6},{8,7},{9,8},{10,9},{11,1... | collective-permute-start | bytes 86024 | tf_op jit(solution)/shard_map/columns/ppermute | solution.py:401
  37.1 29.7 %copy-start.1 = (f32[4,5,16,1]{3,2,1,0:T(8,128)S(1)}, f32[4,5,16,1]{3,2,1,0:T(8,128)}, u32[]{:S(2)}) copy-start(f32[4,5,16,1]{3,2,1,0:T(8,128)} %constant.57.clone.refs_1_) | copy-start | bytes 3844
  41.0 25.8 %all-to-all-start.1 = ((bf16[64,40,128]{2,1,0:T(8,128)(2,1)}), bf16[64,40,128]{2,1,0:T(8,128)(2,1)S(1)}, u32[]{:S(2)}, u32[]{:S(2)}) async-start(bf16[64,40,128]{2,1,0:T(8,128)(2,1)} %bitcast.46), calls=%async_computation.1 | async-start | bytes 1310720 | tf_op jit(solution)/shard_map/back/all_to_all | solution.py:428
  47.6 5.2 %collective-permute-start.2 = (bf16[7,45,128]{2,1,0:T(8,128)(2,1)S(1)}, bf16[7,45,128]{2,1,0:T(8,128)(2,1)S(1)}, u32[]{:S(2)}, u32[]{:S(2)}) collective-permute-start(bf16[7,45,128]{2,1,0:T(8,128)(2,1)S(1)} %pad_maximum_fusion), channel_id=1, source_target_pairs={{64,0},{128,64},{192,128},{65,1},{129,65},{193,129},{66,2},{130,66... | collective-permute-start | bytes 241928 | tf_op jit(solution)/shard_map/below/ppermute | solution.py:432
  48.9 3.9 %collective-permute-start.3 = (bf16[5,45,128]{2,1,0:T(8,128)(2,1)S(1)}, bf16[5,45,128]{2,1,0:T(8,128)(2,1)S(1)}, u32[]{:S(2)}, u32[]{:S(2)}) collective-permute-start(bf16[5,45,128]{2,1,0:T(8,128)(2,1)S(1)} %get-tuple-element.28), channel_id=1, source_target_pairs={{0,64},{64,128},{128,192},{1,65},{65,129},{129,193},{2,66},{66,130... | collective-permute-start | bytes 172808 | tf_op jit(solution)/shard_map/top/ppermute | solution.py:434
  66.9 3.1 %collective-permute-start.4 = (bf16[2,40,128]{2,1,0:T(8,128)(2,1)S(1)}, bf16[2,40,128]{2,1,0:T(8,128)(2,1)S(1)}, u32[]{:S(2)}, u32[]{:S(2)}) collective-permute-start(bf16[2,40,128]{2,1,0:T(8,128)(2,1)S(1)} %get-tuple-element.29), channel_id=1, source_target_pairs={{64,0},{65,1},{66,2},{67,3},{68,4},{69,5},{70,6},{71,7},{72,8},{73... | collective-permute-start | bytes 61448 | tf_op jit(solution)/shard_map/ppermute | solution.py:474

commit v6 on v4

--- a/solution.py
+++ b/solution.py
@@ -1,3 +1,4 @@
+import functools
 import math
 
 import jax
@@ -149,28 +150,153 @@
         store.wait()
 
 
-def filter_kernel(
+def early_kernel(
+    waiting,
+    low_ref,
+    factor_ref,
+    tend_ref,
+    wind_hbm,
+    tracer_hbm,
+    high_ref,
+    side_ref,
+    below_ref,
+    top_ref,
+    filt_hbm,
+    out_hbm,
+    first_ref,
+    courant_ref,
+    tracer_ref,
+    *scratch,
+):
+    fields, _, lat_rows, _ = tend_ref.shape
+    lat = lax.axis_index("lat")
+    first_ref[0] = low_ref[lat_rows]
+    first_ref[1] = low_ref[fields * lat_rows]
+    add_scratch, advect_scratch = scratch[:6], scratch[6:]
+
+    @pl.when(lat >= waiting)
+    def _():
+        loads = tracer_loads(tracer_hbm, tracer_ref, add_scratch[5])
+        for load in loads[::-1]:
+            load.start()
+        stores = add_rows(
+            lat, low_ref, factor_ref, tend_ref, wind_hbm, high_ref, filt_hbm, courant_ref, *add_scratch[:5]
+        )
+        advect(
+            lat,
+            factor_ref,
+            courant_ref,
+            tracer_ref,
+            high_ref,
+            side_ref,
+            below_ref,
+            top_ref,
+            None,
+            loads,
+            out_hbm,
+            *advect_scratch,
+        )
+        for store in stores:
+            store.wait()
+
+
+def middle_kernel(
+    waiting,
+    low_ref,
+    factor_ref,
+    tend_ref,
+    wind_hbm,
+    tracer_hbm,
+    high_ref,
+    _,
+    filt_hbm,
+    courant_ref,
+    tracer_ref,
+    *scratch,
+):
+    lat = lax.axis_index("lat")
+
+    @pl.when(lat < waiting)
+    def _():
+        loads = tracer_loads(tracer_hbm, tracer_ref, scratch[5])
+        for load in loads:
+            load.start()
+        stores = add_rows(
+            lat, low_ref, factor_ref, tend_ref, wind_hbm, high_ref, filt_hbm, courant_ref, *scratch[:5]
+        )
+        for copy in loads + stores:
+            copy.wait()
+
+
+def late_kernel(
+    waiting,
+    factor_ref,
+    courant_ref,
+    tracer_ref,
+    high_ref,
+    side_ref,
+    below_ref,
+    top_ref,
+    next_low_ref,
+    _,
+    out_hbm,
+    *scratch,
+):
+    lat = lax.axis_index("lat")
+
+    @pl.when(lat < waiting)
+    def _():
+        advect(
+            lat,
+            factor_ref,
+            courant_ref,
+            tracer_ref,
+            high_ref,
+            side_ref,
+            below_ref,
+            top_ref,
+            next_low_ref,
+            None,
+            out_hbm,
+            *scratch,
+        )
+
+
+def tracer_loads(tracer_hbm, tracer_ref, sems):
+    return [
+        pltpu.make_async_copy(
+            tracer_hbm.at[:, pl.ds(i * COLS, COLS)], tracer_ref.at[:, pl.ds(i * COLS, COLS)], sems.at[i]
+        )
+        for i in range(tracer_ref.shape[1] // COLS)
+    ]
+
+
+def add_rows(
+    lat,
     low_ref,
     factor_ref,
     tend_ref,
     wind_hbm,
     high_ref,
-    filt_ref,
+    filt_hbm,
     courant_ref,
     wide_ref,
     rest_ref,
     filt,
     wind_ref,
     sems,
-    wind_sems,
 ):
     fields, width, lat_rows, levels = tend_ref.shape
-    loads = [pltpu.make_async_copy(wind_hbm.at[f], wind_ref.at[f], wind_sems.at[f]) for f in range(2)]
-    for load in loads:
+    count = high_ref.shape[0] - 2
+    size = width * lat_rows
+    winds = [
+        pltpu.make_async_copy(wind_hbm.at[f], wind_ref.at[f], sems.at[fields + f]) for f in range(2)
+    ]
+    for load in winds:
         load.start()
-    size = width * lat_rows
-    damp = jnp.broadcast_to(factor_ref[lax.axis_index("lat"), 0], (lat_rows, levels))
     stores = []
+    damp = jnp.broadcast_to(factor_ref[lat, 0], (lat_rows, levels))
+
     for r in range(lat_rows):
         rest_ref[r] = expand(low_ref[fields * lat_rows + r].astype(jnp.float32))
     for f in range(fields):
@@ -180,51 +306,44 @@
         low = wide_ref[f, :size].reshape(width, lat_rows, levels)
         value = (damp[None] * tend_ref[f].astype(jnp.float32) + low).astype(jnp.bfloat16)
         filt[f] = value
-        stores.append(pltpu.make_async_copy(filt.at[f], filt_ref.at[f], sems.at[f]))
-        stores[f].start()
+        stores.append(pltpu.make_async_copy(filt.at[f], filt_hbm.at[f], sems.at[f]))
+        stores[-1].start()
         if f < 2:
-            loads[f].wait()
+            winds[f].wait()
             courant_ref[f, :width] = (0.5, 0.25)[f] * jnp.tanh(wind_ref[f] + value.astype(jnp.float32))
         if f == 0:
-            last = high_ref.shape[0] - 1
-            edge = damp * high_ref[last].astype(jnp.float32) + wide_ref[f, size : size + lat_rows]
+            edge = damp * high_ref[count + 1].astype(jnp.float32) + wide_ref[f, size : size + lat_rows]
             edge = edge.astype(jnp.bfloat16).astype(jnp.float32)
-            courant_ref[f, width] = 0.5 * jnp.tanh(high_ref[last - 1].astype(jnp.float32) + edge)
-    for store in stores:
-        store.wait()
-
-
-def advect_kernel(
+            courant_ref[f, width] = 0.5 * jnp.tanh(high_ref[count].astype(jnp.float32) + edge)
+    return stores
+
+
+def advect(
+    lat,
+    factor_ref,
     courant_ref,
-    factor_ref,
-    tracer_hbm,
+    tracer_ref,
     high_ref,
     side_ref,
     below_ref,
     top_ref,
     next_low_ref,
+    loads,
     out_hbm,
-    tracer_ref,
     out_ref,
     north_ref,
     below_wide,
     top_wide,
-    in_sems,
-    out_sems,
+    sems,
 ):
     count, width, lat_rows, levels = tracer_ref.shape
     pieces = width // COLS
-    loads = []
-    stores = []
-    for i in range(pieces):
-        part = pl.ds(i * COLS, COLS)
-        loads.append(
-            pltpu.make_async_copy(tracer_hbm.at[:, part], tracer_ref.at[:, part], in_sems.at[i])
-        )
-        stores.append(pltpu.make_async_copy(out_ref.at[:, part], out_hbm.at[:, part], out_sems.at[i]))
-    for load in reversed(loads):
-        load.start()
-    lat = lax.axis_index("lat")
+    stores = [
+        pltpu.make_async_copy(
+            out_ref.at[:, pl.ds(i * COLS, COLS)], out_hbm.at[:, pl.ds(i * COLS, COLS)], sems.at[i]
+        )
+        for i in range(pieces)
+    ]
     face, face_next, inverse = (
         jnp.broadcast_to(factor_ref[lat, i], (lat_rows, levels)) for i in (1, 2, 3)
     )
@@ -233,11 +352,14 @@
     is_last = sublane == lat_rows - 1
     below_wide[:, :width] = below_ref[...].astype(jnp.float32)
     top_wide[:, :width] = top_ref[...].astype(jnp.float32)
-    filt = factor_ref[lat, 4, 0:1] * below_wide[count + 1, :width]
-    row, rest = (expand(next_low_ref[i].astype(jnp.float32)) for i in range(2))
-    filt = (filt + with_rest(row, rest, 1)[:width]).astype(jnp.bfloat16)
-    north_ref[:width] = 0.25 * jnp.tanh(below_wide[count, :width] + filt.astype(jnp.float32))
-    loads[pieces - 1].wait()
+    edge = factor_ref[lat, 4, 0:1] * below_wide[count + 1, :width]
+    if next_low_ref is not None:
+        row, rest = (expand(next_low_ref[i].astype(jnp.float32)) for i in range(2))
+        edge += with_rest(row, rest, 1)[:width]
+    edge = edge.astype(jnp.bfloat16).astype(jnp.float32)
+    north_ref[:width] = 0.25 * jnp.tanh(below_wide[count, :width] + edge)
+    if loads is not None:
+        loads[pieces - 1].wait()
     east = courant_ref[0, width]
     flux = [
         jnp.maximum(east, 0.0) * tracer_ref[q, width - 1]
@@ -245,7 +367,7 @@
         for q in range(count)
     ]
     for piece in reversed(range(pieces)):
-        if piece > 0:
+        if piece > 0 and loads is not None:
             loads[piece - 1].wait()
         for column in reversed(range(piece * COLS, (piece + 1) * COLS)):
             east = courant_ref[0, column]
@@ -403,54 +525,61 @@
         below = lax.ppermute(below, "lat", to_prior)
     with jax.named_scope("top"):
         top = lax.ppermute(top, "lat", to_next)
-    next_low = jnp.stack([low[lat_rows], low[fields * lat_rows]])
-    next_low = lax.ppermute(next_low, "lat", to_prior[: lat_devices // 2 - 1])
-
-    filtered, courant = pl.pallas_call(
-        filter_kernel,
-        in_specs=[vmem, vmem, vmem, hbm, vmem],
-        out_specs=[hbm, vmem],
-        out_shape=[
-            pltpu.HBM(tendencies.shape, bf16),
-            pltpu.VMEM((2, width + 1, lat_rows, levels), jnp.float32),
-        ],
-        scratch_shapes=[
-            pltpu.VMEM((fields, SEG * lat_rows, levels), jnp.float32),
-            pltpu.VMEM((lat_rows, SEG, levels), jnp.float32),
-            pltpu.VMEM(tendencies.shape, bf16),
-            pltpu.VMEM(winds.shape, jnp.float32),
-            pltpu.SemaphoreType.DMA((fields,)),
-            pltpu.SemaphoreType.DMA((2,)),
-        ],
+    waiting = lat_devices // 2 - 1
+    filtered_out = pltpu.HBM(tendencies.shape, bf16)
+    advected_out = pltpu.HBM(tracers.shape, jnp.float32)
+    on_chip = [
+        pltpu.VMEM((2, width + 1, lat_rows, levels), jnp.float32),
+        pltpu.VMEM(tracers.shape, jnp.float32),
+    ]
+    add_scratch = [
+        pltpu.VMEM((fields, SEG * lat_rows, levels), jnp.float32),
+        pltpu.VMEM((lat_rows, SEG, levels), jnp.float32),
+        pltpu.VMEM(tendencies.shape, bf16),
+        pltpu.VMEM(winds.shape, jnp.float32),
+        pltpu.SemaphoreType.DMA((fields + 2,)),
+        pltpu.SemaphoreType.DMA((width // COLS,)),
+    ]
+    advect_scratch = [
+        pltpu.VMEM(tracers.shape, jnp.float32),
+        pltpu.VMEM((SEG, levels), jnp.float32),
+        pltpu.VMEM((count + 2, SEG, levels), jnp.float32),
+        pltpu.VMEM((count, SEG, levels), jnp.float32),
+        pltpu.SemaphoreType.DMA((width // COLS,)),
+    ]
+    factors, high, side, below, top = (in_vmem(a) for a in (factors, high, side, below, top))
+    operands = (in_vmem(low), factors, in_vmem(tendencies), in_hbm(winds), in_hbm(tracers), high)
+    specs = [vmem] * 3 + [hbm] * 2 + [vmem]
+    filtered, advected, first = pl.pallas_call(
+        functools.partial(early_kernel, waiting),
+        in_specs=specs + [vmem] * 3,
+        out_specs=[hbm, hbm, vmem],
+        out_shape=[filtered_out, advected_out, jax.ShapeDtypeStruct((2, HEAD, levels), bf16)],
+        scratch_shapes=on_chip + add_scratch + advect_scratch,
         compiler_params=params,
-        name="filter",
-    )(in_vmem(low), in_vmem(factors), in_vmem(tendencies), in_hbm(winds), in_vmem(high))
+        name="early",
+    )(*operands, side, below, top)
+    next_low = lax.ppermute(first, "lat", to_prior[:waiting])
+    filtered, courant, held = pl.pallas_call(
+        functools.partial(middle_kernel, waiting),
+        in_specs=specs + [hbm],
+        out_specs=[hbm, vmem, vmem],
+        out_shape=[filtered_out] + on_chip,
+        scratch_shapes=add_scratch,
+        input_output_aliases={6: 0},
+        compiler_params=params,
+        name="middle",
+    )(*operands, filtered)
     advected = pl.pallas_call(
-        advect_kernel,
-        in_specs=[vmem, vmem, hbm] + [vmem] * 5,
+        functools.partial(late_kernel, waiting),
+        in_specs=[vmem] * 8 + [hbm],
         out_specs=hbm,
-        out_shape=pltpu.HBM(tracers.shape, jnp.float32),
-        scratch_shapes=[
-            pltpu.VMEM(tracers.shape, jnp.float32),
-            pltpu.VMEM(tracers.shape, jnp.float32),
-            pltpu.VMEM((SEG, levels), jnp.float32),
-            pltpu.VMEM((count + 2, SEG, levels), jnp.float32),
-            pltpu.VMEM((count, SEG, levels), jnp.float32),
-            pltpu.SemaphoreType.DMA((width // COLS,)),
-            pltpu.SemaphoreType.DMA((width // COLS,)),
-        ],
+        out_shape=advected_out,
+        scratch_shapes=advect_scratch,
+        input_output_aliases={8: 0},
         compiler_params=params,
-        name="advect",
-    )(
-        courant,
-        in_vmem(factors),
-        in_hbm(tracers),
-        in_vmem(high),
-        in_vmem(side),
-        in_vmem(below),
-        in_vmem(top),
-        in_vmem(next_low),
-    )
+        name="late",
+    )(factors, courant, held, high, side, below, top, in_vmem(next_low), advected)
     return (filtered.transpose(0, 2, 1, 3), advected.transpose(0, 2, 1, 3))
 
 

time: 76.6 us -> 73.5 us (0.960)
  the two profiles are of different devices: /device:TPU:1 before, /device:TPU:2 now
where the time goes in v6:
time: 73.5 us; the launch traced here: 73 us
  starting transfers between devices  28.5 us (39%)
  waiting for transfers between devices  26.2 us (36%)
  Pallas kernels  11.9 us (16%)
  local copies, waits for them, and re-layouts  4.08 us (6%)
  other arithmetic  1.35 us (2%)
  between operations  1.05 us (1%)
    all_to_all x1, waiting for transfers between devices, per_device(): lax.all_to_all(low.reshape(segments, HEAD, levels), 'lon', split_axis=0,...  14 us
    all_to_all x1, starting transfers between devices, per_device(): rows = lax.all_to_all(send, 'lon', split_axis=0, concat_axis=0, tiled=True)  13.4 us
    all_to_all x1, waiting for transfers between devices, per_device(): rows = lax.all_to_all(send, 'lon', split_axis=0, concat_axis=0, tiled=True)  8.64 us
    all_to_all x1, starting transfers between devices, per_device(): lax.all_to_all(low.reshape(segments, HEAD, levels), 'lon', split_axis=0,...  6.6 us
    pallas_call x1, Pallas kernels, per_device(): pl.pallas_call(transform_kernel, in_specs=[hbm, vmem, vmem, vmem], out_sp...  3.84 us
    pallas_call x1, Pallas kernels, per_device(): pl.pallas_call(pack_kernel, in_specs=[hbm], out_specs=hbm, out_shape=pltp...  3.09 us
    ppermute x1, starting transfers between devices, per_device(): top = lax.ppermute(top, 'lat', to_next)  3.03 us
    ppermute x1, starting transfers between devices, per_device(): high = lax.ppermute(high, 'lon', west_ring)  2.75 us
  transfers between devices with their start and end apart: 7, of which 4 were waited for; matrix products, arithmetic and copies ran while one was open for 6% of the time, Pallas kernels for 4%

profile of v6, /device:TPU:2, one launch (start us, length us, event | category | flops | bytes accessed | tf_op | source)
XLA Modules:
  0.0 73.0 jit_solution(14272861178304668281)
XLA Ops:
  0.6 0.0 copy-start
  0.6 0.0 copy-start.3
  0.7 3.1 %pack.1 = bf16[64,40,128]{2,1,0:T(8,128)(2,1)} custom-call(bf16[3,45,16,128]{3,2,1,0:T(8,128)(2,1)} %bitcast.38), custom_call_target="tpu_custom_call" | custom-call | tf_op jit(solution)/shard_map/pack/pallas_call | solution.py:446
  3.7 0.0 copy-start.2
  3.8 13.4 %all-to-all-start = ((bf16[64,40,128]{2,1,0:T(8,128)(2,1)}), bf16[64,40,128]{2,1,0:T(8,128)(2,1)}, u32[]{:S(2)}, u32[]{:S(2)}) async-start(bf16[64,40,128]{2,1,0:T(8,128)(2,1)} %pack.1), calls=%async_computation | async-start | bytes 1310720 | tf_op jit(solution)/shard_map/forth/all_to_all | solution.py:462
  17.2 0.0 copy-done
  17.2 0.2 copy.60
  17.4 0.0 copy-start.15
  17.4 0.0 copy-start.13
  17.4 0.0 copy-start.14
  17.4 0.2 copy.59
  17.7 0.0 copy-start.6
  17.7 0.0 copy-start.7
  17.7 0.0 copy-start.8
  17.7 0.0 copy-start.11
  17.7 0.0 copy-start.12
  17.8 0.4 copy-done.5
  18.2 0.2 copy-done.6
  18.5 0.0 copy-start.9
  18.5 0.0 copy-start.10
  18.5 0.6 copy.58
  19.1 0.0 copy-start.4
  19.1 0.1 fusion.1
  19.2 2.8 %collective-permute-start = (bf16[7,16,128]{2,1,0:T(8,128)(2,1)S(1)}, bf16[7,16,128]{2,1,0:T(8,128)(2,1)S(1)}, u32[]{:S(2)}, u32[]{:S(2)}) collective-permute-start(bf16[7,16,128]{2,1,0:T(8,128)(2,1)S(1)} %pad_maximum_fusion.1), channel_id=1, source_target_pairs={{1,0},{2,1},{3,2},{4,3},{5,4},{6,5},{7,6},{8,7},{9,8},{10,9},{11,1... | collective-permute-start | bytes 86024 | tf_op jit(solution)/shard_map/columns/ppermute | solution.py:494
  22.0 0.1 collective-permute-start.1
  22.1 0.6 dynamic_slice.3
  22.7 0.0 copy-done.14
  22.7 0.6 multiply_select_fusion
  23.3 0.7 slice_bitcast_fusion.2
  24.0 0.9 %slice_bitcast_fusion = (bf16[5,45,128]{2,1,0:T(8,128)(2,1)S(1)}, bf16[5,45,128]{2,1,0:T(8,128)(2,1)S(1)}) fusion(bf16[5,45,16,128]{3,1,0,2:T(8,128)(2,1)} %bitcast.49), kind=kLoop, calls=%fused_computation.7 | loop fusion | bytes 230400 | tf_op jit(solution)/shard_map/edges/convert_element_type | solution.py:492
  24.9 0.1 fusion.tail_ref
  25.1 0.7 add_convert_fusion
  25.8 2.7 %collective-permute-done.1.side_ref = bf16[5,16,128]{2,1,0:T(8,128)(2,1)S(1)} collective-permute-done((bf16[5,16,128]{2,1,0:T(8,128)(2,1)S(1)}, bf16[5,16,128]{2,1,0:T(8,128)(2,1)S(1)}, u32[]{:S(2)}, u32[]{:S(2)}) %collective-permute-start.1) | collective-permute-done | bytes 20512 | tf_op jit(solution)/shard_map/columns/ppermute | solution.py:495
  28.5 0.0 collective-permute-done.high_ref
  28.5 8.6 %all-to-all-done = bf16[64,40,128]{2,1,0:T(8,128)(2,1)} async-done(((bf16[64,40,128]{2,1,0:T(8,128)(2,1)}), bf16[64,40,128]{2,1,0:T(8,128)(2,1)}, u32[]{:S(2)}, u32[]{:S(2)}) %all-to-all-start) | async-done | bytes 655392 | tf_op jit(solution)/shard_map/forth/all_to_all | solution.py:462
  37.1 3.8 %transform.1 = bf16[2560,128]{1,0:T(8,128)(2,1)} custom-call(bf16[2560,128]{1,0:T(8,128)(2,1)} %bitcast.13.rows_ref, f32[1,384]{1,0:T(1,128)S(1)} %select_n.25.weight_ref, bf16[2560,384]{1,0:T(8,128)(2,1)S(1)} %bitcast.41, bf16[512,384]{1,0:T(8,128)(2,1)S(1)} %fusion.tail_ref), custom_call_target="tpu_custom_call" | custom-call | tf_op jit(solution)/shard_map/transform/pallas_call | solution.py:500
  40.9 6.6 %all-to-all-start.1 = ((bf16[64,40,128]{2,1,0:T(8,128)(2,1)}), bf16[64,40,128]{2,1,0:T(8,128)(2,1)S(1)}, u32[]{:S(2)}, u32[]{:S(2)}) async-start(bf16[64,40,128]{2,1,0:T(8,128)(2,1)} %bitcast.46), calls=%async_computation.1 | async-start | bytes 1310720 | tf_op jit(solution)/shard_map/back/all_to_all | solution.py:521
  47.6 1.3 %collective-permute-start.2 = (bf16[7,45,128]{2,1,0:T(8,128)(2,1)S(1)}, bf16[7,45,128]{2,1,0:T(8,128)(2,1)S(1)}, u32[]{:S(2)}, u32[]{:S(2)}) collective-permute-start(bf16[7,45,128]{2,1,0:T(8,128)(2,1)S(1)} %pad_maximum_fusion), channel_id=1, source_target_pairs={{64,0},{128,64},{192,128},{65,1},{129,65},{193,129},{66,2},{130,66... | collective-permute-start | bytes 241928 | tf_op jit(solution)/shard_map/below/ppermute | solution.py:525
  48.9 3.0 %collective-permute-start.3 = (bf16[5,45,128]{2,1,0:T(8,128)(2,1)S(1)}, bf16[5,45,128]{2,1,0:T(8,128)(2,1)S(1)}, u32[]{:S(2)}, u32[]{:S(2)}) collective-permute-start(bf16[5,45,128]{2,1,0:T(8,128)(2,1)S(1)} %get-tuple-element.29), channel_id=1, source_target_pairs={{0,64},{64,128},{128,192},{1,65},{65,129},{129,193},{2,66},{66,130... | collective-permute-start | bytes 172808 | tf_op jit(solution)/shard_map/top/ppermute | solution.py:527
  51.9 0.9 %collective-permute-done.3.top_ref = bf16[5,45,128]{2,1,0:T(8,128)(2,1)S(1)} collective-permute-done((bf16[5,45,128]{2,1,0:T(8,128)(2,1)S(1)}, bf16[5,45,128]{2,1,0:T(8,128)(2,1)S(1)}, u32[]{:S(2)}, u32[]{:S(2)}) %collective-permute-start.3) | collective-permute-done | bytes 57632 | tf_op jit(solution)/shard_map/top/ppermute | solution.py:527
  52.8 0.0 collective-permute-done.2.below_ref
  52.8 14.0 %all-to-all-done.1.low_ref = bf16[64,40,128]{2,1,0:T(8,128)(2,1)S(1)} async-done(((bf16[64,40,128]{2,1,0:T(8,128)(2,1)}), bf16[64,40,128]{2,1,0:T(8,128)(2,1)S(1)}, u32[]{:S(2)}, u32[]{:S(2)}) %all-to-all-start.1) | async-done | bytes 655392 | tf_op jit(solution)/shard_map/back/all_to_all | solution.py:521
  66.8 0.0 copy-done.1
  66.8 0.1 early.1
  66.9 1.3 %collective-permute-start.4 = (bf16[2,40,128]{2,1,0:T(8,128)(2,1)S(1)}, bf16[2,40,128]{2,1,0:T(8,128)(2,1)S(1)}, u32[]{:S(2)}, u32[]{:S(2)}) collective-permute-start(bf16[2,40,128]{2,1,0:T(8,128)(2,1)S(1)} %get-tuple-element.34), channel_id=1, source_target_pairs={{64,0},{65,1},{66,2},{67,3},{68,4},{69,5},{70,6},{71,7},{72,8},{73... | collective-permute-start | bytes 61448 | tf_op jit(solution)/shard_map/ppermute | solution.py:562
  68.2 2.6 %middle.1 = (bf16[3,45,16,128]{3,2,1,0:T(8,128)(2,1)}, f32[2,46,16,128]{3,2,1,0:T(8,128)S(1)}, f32[5,45,16,128]{3,2,1,0:T(8,128)S(1)}) custom-call(bf16[64,40,128]{2,1,0:T(8,128)(2,1)S(1)} %all-to-all-done.1.low_ref, f32[4,5,16,1]{3,2,1,0:T(8,128)S(1)} %copy-done.1, bf16[3,45,16,128]{3,2,1,0:T(8,128)(2,1)S(1)} %bitcast.40, ...), custom_call_target="tpu_custom_call", output_to_operand_aliasing={{0}: (6, {})} | custom-call | tf_op jit(solution)/shard_map/middle/pallas_call | solution.py:563
  70.8 0.0 collective-permute-done.4.next_low_ref
  70.8 2.2 %late.1 = f32[5,45,16,128]{3,2,1,0:T(8,128)} custom-call(f32[4,5,16,1]{3,2,1,0:T(8,128)S(1)} %copy-done.1, f32[2,46,16,128]{3,2,1,0:T(8,128)S(1)} %get-tuple-element.32.courant_ref, f32[5,45,16,128]{3,2,1,0:T(8,128)S(1)} %get-tuple-element.33.tracer_ref, bf16[7,16,128]{2,1,0:T(8,128)(2,1)S(1)} %collective-permute-done.high_ref, ...), custom_call_target="tpu_custom_call", output_to_operand_aliasing={{}: (8, {})} | custom-call | tf_op jit(solution)/shard_map/late/pallas_call | solution.py:573
  (21 shorter events, 0.1 us)
Async XLA Ops:
  0.6 16.6 %copy-start = (bf16[3,16,45,128]{3,1,2,0:T(8,128)(2,1)S(1)}, bf16[3,16,45,128]{3,1,2,0:T(8,128)(2,1)}, u32[]{:S(2)}) copy-start(bf16[3,16,45,128]{3,1,2,0:T(8,128)(2,1)} %param.13) | copy-start | bytes 1658884
  0.6 16.8 %copy-start.3 = (f32[2,16,45,128]{3,1,2,0:T(8,128)S(1)}, f32[2,16,45,128]{3,1,2,0:T(8,128)}, u32[]{:S(2)}) copy-start(f32[2,16,45,128]{3,1,2,0:T(8,128)} %param.15) | copy-start | bytes 2211844
  3.7 14.7 %copy-start.2 = (f32[5,16,45,128]{3,1,2,0:T(8,128)S(1)}, f32[5,16,45,128]{3,1,2,0:T(8,128)}, u32[]{:S(2)}) copy-start(f32[5,16,45,128]{3,1,2,0:T(8,128)} %param.16) | copy-start | bytes 5529604
  3.8 33.3 %all-to-all-start = ((bf16[64,40,128]{2,1,0:T(8,128)(2,1)}), bf16[64,40,128]{2,1,0:T(8,128)(2,1)}, u32[]{:S(2)}, u32[]{:S(2)}) async-start(bf16[64,40,128]{2,1,0:T(8,128)(2,1)} %pack.1), calls=%async_computation | async-start | bytes 1310720 | tf_op jit(solution)/shard_map/forth/all_to_all | solution.py:462
  17.4 0.8 %copy-start.5 = (bf16[3,16,45,128]{3,2,1,0:T(8,128)(2,1)}, bf16[3,16,45,128]{3,2,1,0:T(8,128)(2,1)S(1)}, u32[]{:S(2)}) copy-start(bf16[3,16,45,128]{3,2,1,0:T(8,128)(2,1)S(1)} %copy.60) | copy-start | bytes 1658884
  17.4 4.7 %copy-start.15 = (s32[64]{0:T(128)S(1)}, s32[64]{0:T(128)}, u32[]{:S(2)}) copy-start(s32[64]{0:T(128)} %param.14) | copy-start | bytes 772
  17.4 5.3 %copy-start.13 = (f32[384]{0:T(512)S(1)}, f32[384]{0:T(512)}, u32[]{:S(2)}) copy-start(f32[384]{0:T(512)} %constant.58.clone) | copy-start | bytes 4612
  17.4 5.3 %copy-start.14 = (s32[384]{0:T(512)S(1)}, s32[384]{0:T(512)}, u32[]{:S(2)}) copy-start(s32[384]{0:T(512)} %constant.59.clone) | copy-start | bytes 4612
  17.7 0.7 %copy-start.6 = (bf16[2,16,45,128]{3,2,1,0:T(8,128)(2,1)}, bf16[2,16,45,128]{3,2,1,0:T(8,128)(2,1)S(1)}, u32[]{:S(2)}) copy-start(bf16[2,16,45,128]{3,2,1,0:T(8,128)(2,1)S(1)} %copy.59) | copy-start | bytes 1105924
  17.7 7.2 %copy-start.7 = (f32[64,384]{1,0:T(8,128)S(1)}, f32[64,384]{1,0:T(8,128)}, u32[]{:S(2)}) copy-start(f32[64,384]{1,0:T(8,128)} %constant.62.clone) | copy-start | bytes 294916
  17.7 7.2 %copy-start.8 = (f32[64,384]{1,0:T(8,128)S(1)}, f32[64,384]{1,0:T(8,128)}, u32[]{:S(2)}) copy-start(f32[64,384]{1,0:T(8,128)} %constant.60.clone) | copy-start | bytes 294916
  17.7 7.2 %copy-start.11 = (f32[8,384]{1,0:T(8,128)S(1)}, f32[8,384]{1,0:T(8,128)}, u32[]{:S(2)}) copy-start(f32[8,384]{1,0:T(8,128)} %constant.65.clone) | copy-start | bytes 36868
  17.7 7.2 %copy-start.12 = (f32[8,384]{1,0:T(8,128)S(1)}, f32[8,384]{1,0:T(8,128)}, u32[]{:S(2)}) copy-start(f32[8,384]{1,0:T(8,128)} %constant.64.clone) | copy-start | bytes 36868
  18.5 6.6 %copy-start.9 = (f32[40,384]{1,0:T(8,128)S(1)}, f32[40,384]{1,0:T(8,128)}, u32[]{:S(2)}) copy-start(f32[40,384]{1,0:T(8,128)} %constant.63.clone) | copy-start | bytes 184324
  18.5 6.6 %copy-start.10 = (f32[40,384]{1,0:T(8,128)S(1)}, f32[40,384]{1,0:T(8,128)}, u32[]{:S(2)}) copy-start(f32[40,384]{1,0:T(8,128)} %constant.61.clone) | copy-start | bytes 184324
  19.1 2.9 %copy-start.4 = (bf16[5,16,45,128]{3,2,0,1:T(8,128)(2,1)}, bf16[5,16,45,128]{3,2,0,1:T(8,128)(2,1)S(1)}, u32[]{:S(2)}) copy-start(bf16[5,16,45,128]{3,2,0,1:T(8,128)(2,1)S(1)} %copy.58) | copy-start | bytes 2764804
  19.2 9.2 %collective-permute-start = (bf16[7,16,128]{2,1,0:T(8,128)(2,1)S(1)}, bf16[7,16,128]{2,1,0:T(8,128)(2,1)S(1)}, u32[]{:S(2)}, u32[]{:S(2)}) collective-permute-start(bf16[7,16,128]{2,1,0:T(8,128)(2,1)S(1)} %pad_maximum_fusion.1), channel_id=1, source_target_pairs={{1,0},{2,1},{3,2},{4,3},{5,4},{6,5},{7,6},{8,7},{9,8},{10,9},{11,1... | collective-permute-start | bytes 86024 | tf_op jit(solution)/shard_map/columns/ppermute | solution.py:494
  22.0 6.5 %collective-permute-start.1 = (bf16[5,16,128]{2,1,0:T(8,128)(2,1)S(1)}, bf16[5,16,128]{2,1,0:T(8,128)(2,1)S(1)}, u32[]{:S(2)}, u32[]{:S(2)}) collective-permute-start(bf16[5,16,128]{2,1,0:T(8,128)(2,1)S(1)} %bitcast.56), channel_id=1, source_target_pairs={{0,1},{1,2},{2,3},{3,4},{4,5},{5,6},{6,7},{7,8},{8,9},{9,10},{10,1... | collective-permute-start | bytes 61448 | tf_op jit(solution)/shard_map/columns/ppermute | solution.py:495
  37.1 29.7 %copy-start.1 = (f32[4,5,16,1]{3,2,1,0:T(8,128)S(1)}, f32[4,5,16,1]{3,2,1,0:T(8,128)}, u32[]{:S(2)}) copy-start(f32[4,5,16,1]{3,2,1,0:T(8,128)} %constant.57.clone.factor_ref) | copy-start | bytes 3844
  40.9 25.8 %all-to-all-start.1 = ((bf16[64,40,128]{2,1,0:T(8,128)(2,1)}), bf16[64,40,128]{2,1,0:T(8,128)(2,1)S(1)}, u32[]{:S(2)}, u32[]{:S(2)}) async-start(bf16[64,40,128]{2,1,0:T(8,128)(2,1)} %bitcast.46), calls=%async_computation.1 | async-start | bytes 1310720 | tf_op jit(solution)/shard_map/back/all_to_all | solution.py:521
  47.6 5.2 %collective-permute-start.2 = (bf16[7,45,128]{2,1,0:T(8,128)(2,1)S(1)}, bf16[7,45,128]{2,1,0:T(8,128)(2,1)S(1)}, u32[]{:S(2)}, u32[]{:S(2)}) collective-permute-start(bf16[7,45,128]{2,1,0:T(8,128)(2,1)S(1)} %pad_maximum_fusion), channel_id=1, source_target_pairs={{64,0},{128,64},{192,128},{65,1},{129,65},{193,129},{66,2},{130,66... | collective-permute-start | bytes 241928 | tf_op jit(solution)/shard_map/below/ppermute | solution.py:525
  48.9 3.9 %collective-permute-start.3 = (bf16[5,45,128]{2,1,0:T(8,128)(2,1)S(1)}, bf16[5,45,128]{2,1,0:T(8,128)(2,1)S(1)}, u32[]{:S(2)}, u32[]{:S(2)}) collective-permute-start(bf16[5,45,128]{2,1,0:T(8,128)(2,1)S(1)} %get-tuple-element.29), channel_id=1, source_target_pairs={{0,64},{64,128},{128,192},{1,65},{65,129},{129,193},{2,66},{66,130... | collective-permute-start | bytes 172808 | tf_op jit(solution)/shard_map/top/ppermute | solution.py:527
  66.9 3.9 %collective-permute-start.4 = (bf16[2,40,128]{2,1,0:T(8,128)(2,1)S(1)}, bf16[2,40,128]{2,1,0:T(8,128)(2,1)S(1)}, u32[]{:S(2)}, u32[]{:S(2)}) collective-permute-start(bf16[2,40,128]{2,1,0:T(8,128)(2,1)S(1)} %get-tuple-element.34), channel_id=1, source_target_pairs={{64,0},{65,1},{66,2},{67,3},{68,4},{69,5},{70,6},{71,7},{72,8},{73... | collective-permute-start | bytes 61448 | tf_op jit(solution)/shard_map/ppermute | solution.py:562

commit v7 on v6

--- a/solution.py
+++ b/solution.py
@@ -13,43 +13,49 @@
 KMAX = 180
 COEF = 384
 SEG = 48
-HEAD = 40
+HEAD = 36
+PAIR = 2 * HEAD
 QUARTER = 32
 MAIN = 96
 LIMIT = 24 << 20
-LOADS = 5
+LOADS = 3
 CHUNKS = 4
 COLS = 9
 
 
-def trig_tables(lon_count, segments):
-    width = lon_count // segments
-    k = np.zeros(COEF)
+HEAD_ORDER = [(side, q) for side in range(2) for q in range(HEAD)]
+TAIL_ORDER = [(side, q) for side in range(2) for q in range(HEAD, SEG)]
+
+
+def wave_rows():
+    k = np.zeros(COEF, np.int32)
     k[: KMAX + 1] = np.arange(KMAX + 1)
     k[KMAX + 1 : 2 * KMAX + 1] = np.arange(1, KMAX + 1)
-    is_cos = np.zeros(COEF, bool)
-    is_cos[: KMAX + 1] = True
-    used = np.arange(COEF) < 2 * KMAX + 1
-    over_p = 2 * np.pi * np.outer(np.arange(segments) * width, k) / lon_count
-    over_q = 2 * np.pi * np.outer(np.arange(SEG), k) / lon_count
+    place = np.arange(COEF)
+    return k, place <= KMAX, place < 2 * KMAX + 1
+
+
+def trig_table(lon_count, segments, order):
+    width = lon_count // segments
+    k, is_cos, used = wave_rows()
+    over_p = 2 * np.pi * np.outer(np.arange(0, segments, 2) * width, k) / lon_count
+    over_q = 2 * np.pi * np.outer([side * width + q for side, q in order], k) / lon_count
     p_one = np.where(is_cos, np.cos(over_p), np.sin(over_p)) * used
     p_two = np.where(is_cos, -np.sin(over_p), np.cos(over_p)) * used
-    tables = (p_one, p_two, np.cos(over_q), np.sin(over_q))
-    return tuple(t.astype(np.float32) for t in tables), k.astype(np.int32), used
+    p_one, p_two, q_one, q_two = (
+        jnp.asarray(t, jnp.float32) for t in (p_one, p_two, np.cos(over_q), np.sin(over_q))
+    )
+    table = p_one[:, None, :] * q_one[None, :, :] + p_two[:, None, :] * q_two[None, :, :]
+    return table.astype(jnp.bfloat16).reshape(-1, COEF)
+
+
+def lanes(like):
+    return lax.broadcasted_iota(jnp.int32, like.shape, like.ndim - 1)
 
 
 def squeeze(head, tail):
-    lane = lax.broadcasted_iota(jnp.int32, tail.shape, tail.ndim - 1)
-    size = tail.shape[-2]
-    groups = [
-        jnp.where(
-            lane < MAIN,
-            head[..., i * size : (i + 1) * size, :],
-            pltpu.roll(tail, MAIN - i * QUARTER, tail.ndim - 1),
-        )
-        for i in range(MAIN // QUARTER)
-    ]
-    return jnp.concatenate(groups + [head[..., MAIN // QUARTER * size :, :]], axis=-2)
+    last = [pltpu.roll(tail, MAIN - i * QUARTER, tail.ndim - 1) for i in range(MAIN // QUARTER)]
+    return jnp.where(lanes(head) < MAIN, head, jnp.concatenate(last, axis=-2))
 
 
 def tail_of(head):
@@ -58,50 +64,60 @@
         pltpu.roll(head[..., i * size : (i + 1) * size, :], (i + 1) * QUARTER, head.ndim - 1)
         for i in range(MAIN // QUARTER)
     ]
-    lane = lax.broadcasted_iota(jnp.int32, moved[0].shape, head.ndim - 1)
+    lane = lanes(moved[0])
     return jnp.where(lane < QUARTER, moved[0], jnp.where(lane < 2 * QUARTER, moved[1], moved[2]))
 
 
-def expand(head):
-    return jnp.concatenate([head, tail_of(head)], axis=-2)
+def halves(pair):
+    size = pair.shape[-2] // 2
+    return pair[..., :size, :], pair[..., size:, :]
+
+
+def expand(pair):
+    return [jnp.concatenate([head, tail_of(head)], axis=-2) for head in halves(pair)]
 
 
 def with_rest(row, rest, f):
-    lane = lax.broadcasted_iota(jnp.int32, row.shape, row.ndim - 1)
-    return jnp.where(lane < MAIN, row, pltpu.roll(rest, MAIN - f * QUARTER, row.ndim - 1))
+    return jnp.where(lanes(row) < MAIN, row, pltpu.roll(rest, MAIN - f * QUARTER, row.ndim - 1))
 
 
 def pack_kernel(tend_ref, out_ref, tend, wide, rows, in_sems, out_sems):
     fields, width, lat_rows, levels = tend.shape
     size = width * lat_rows
+    half = lat_rows // 2
     loads = [pltpu.make_async_copy(tend_ref.at[f], tend.at[f], in_sems.at[f]) for f in range(fields)]
     for load in loads:
         load.start()
     stores = []
 
     def send(block):
-        part = pl.ds(block * lat_rows, lat_rows)
+        part = pl.ds(block * half, half)
         store = pltpu.make_async_copy(rows.at[part], out_ref.at[part], out_sems.at[block])
         store.start()
         stores.append(store)
+
+    def put(pair, *slots):
+        slots = [squeeze(slot[:HEAD], slot[HEAD:]) for slot in slots]
+        rows[pair] = jnp.concatenate(slots, axis=0).astype(jnp.bfloat16)
+
+    def whole(f, r):
+        return wide[f, pl.ds(r, SEG, stride=lat_rows), :]
+
+    def left(r):
+        moved = [pltpu.roll(whole(f, r), (f + 1) * QUARTER, 1) for f in range(fields)]
+        lane = lanes(moved[0])
+        return jnp.where(lane < QUARTER, moved[0], jnp.where(lane < 2 * QUARTER, moved[1], moved[2]))
 
     for f in range(fields):
         wide[f, size:] = jnp.zeros((SEG * lat_rows - size, levels), jnp.float32)
     for f in range(fields):
         loads[f].wait()
         wide[f, :size] = tend[f].astype(jnp.float32).reshape(size, levels)
-        for r in range(lat_rows):
-            row = wide[f, pl.ds(r, SEG, stride=lat_rows), :]
-            rows[f * lat_rows + r] = squeeze(row[:HEAD], row[HEAD:]).astype(jnp.bfloat16)
+        for r in range(half):
+            put(f * half + r, whole(f, 2 * r), whole(f, 2 * r + 1))
         send(f)
-    lane = lax.broadcasted_iota(jnp.int32, (SEG, levels), 1)
-    for r in range(lat_rows):
-        moved = [
-            pltpu.roll(wide[f, pl.ds(r, SEG, stride=lat_rows), :], (f + 1) * QUARTER, 1)
-            for f in range(fields)
-        ]
-        row = jnp.where(lane < QUARTER, moved[0], jnp.where(lane < 2 * QUARTER, moved[1], moved[2]))
-        rows[fields * lat_rows + r] = squeeze(row[:HEAD], row[HEAD:]).astype(jnp.bfloat16)
+    for r in range(half):
+        put(fields * half + r, left(2 * r), left(2 * r + 1))
     send(fields)
     for store in stores:
         store.wait()
@@ -111,8 +127,7 @@
     rows_ref, weight_ref, head_ref, tail_ref, out_ref, rows, result, in_sems, out_sems
 ):
     total, levels = rows.shape
-    tails = SEG - HEAD
-    segments = total // HEAD
+    pairs = total // PAIR
     piece = total // LOADS
     loads = [
         pltpu.make_async_copy(
@@ -131,19 +146,22 @@
         spectrum += lax.dot_general(
             rows[part], head_ref[part], forward, preferred_element_type=jnp.float32
         )
-    tail = tail_of(rows[...].astype(jnp.float32).reshape(segments, HEAD, levels))
-    tail = tail.reshape(segments * tails, levels).astype(jnp.bfloat16)
+    tail = [tail_of(head) for head in halves(rows[...].astype(jnp.float32).reshape(pairs, PAIR, levels))]
+    tail = jnp.concatenate(tail, axis=-2)
+    tail = tail.reshape(tail_ref.shape[0], levels).astype(jnp.bfloat16)
     spectrum += lax.dot_general(tail, tail_ref[...], forward, preferred_element_type=jnp.float32)
     weighted = (spectrum * weight_ref[...]).astype(jnp.bfloat16)
     tail = lax.dot_general(tail_ref[...], weighted, back, preferred_element_type=jnp.float32)
-    tail = tail.reshape(segments, tails, levels)
-    count = segments // CHUNKS
+    tail = tail.reshape(pairs, 2 * (SEG - HEAD), levels)
+    count = pairs // CHUNKS
     stores = []
     for i in range(CHUNKS):
-        part = pl.ds(i * count * HEAD, count * HEAD)
+        part = pl.ds(i * count * PAIR, count * PAIR)
         head = lax.dot_general(head_ref[part], weighted, back, preferred_element_type=jnp.float32)
-        head = squeeze(head.reshape(count, HEAD, levels), tail[i * count : (i + 1) * count])
-        result[part] = head.reshape(count * HEAD, levels).astype(jnp.bfloat16)
+        head = halves(head.reshape(count, PAIR, levels))
+        last = halves(tail[i * count : (i + 1) * count])
+        head = jnp.concatenate([squeeze(h, t) for h, t in zip(head, last)], axis=-2)
+        result[part] = head.reshape(count * PAIR, levels).astype(jnp.bfloat16)
         stores.append(pltpu.make_async_copy(result.at[part], out_ref.at[part], out_sems.at[i]))
         stores[i].start()
     for store in stores:
@@ -170,8 +188,8 @@
 ):
     fields, _, lat_rows, _ = tend_ref.shape
     lat = lax.axis_index("lat")
-    first_ref[0] = low_ref[lat_rows]
-    first_ref[1] = low_ref[fields * lat_rows]
+    first_ref[0] = low_ref[lat_rows // 2]
+    first_ref[1] = low_ref[fields * lat_rows // 2]
     add_scratch, advect_scratch = scratch[:6], scratch[6:]
 
     @pl.when(lat >= waiting)
@@ -297,12 +315,17 @@
     stores = []
     damp = jnp.broadcast_to(factor_ref[lat, 0], (lat_rows, levels))
 
-    for r in range(lat_rows):
-        rest_ref[r] = expand(low_ref[fields * lat_rows + r].astype(jnp.float32))
+    half = lat_rows // 2
+    for r in range(half):
+        pair = expand(low_ref[fields * half + r].astype(jnp.float32))
+        for i in range(2):
+            rest_ref[2 * r + i] = pair[i]
     for f in range(fields):
-        for r in range(lat_rows):
-            row = expand(low_ref[f * lat_rows + r].astype(jnp.float32))
-            wide_ref[f, pl.ds(r, SEG, stride=lat_rows), :] = with_rest(row, rest_ref[r], f)
+        for r in range(half):
+            pair = expand(low_ref[f * half + r].astype(jnp.float32))
+            for i in range(2):
+                row = with_rest(pair[i], rest_ref[2 * r + i], f)
+                wide_ref[f, pl.ds(2 * r + i, SEG, stride=lat_rows), :] = row
         low = wide_ref[f, :size].reshape(width, lat_rows, levels)
         value = (damp[None] * tend_ref[f].astype(jnp.float32) + low).astype(jnp.bfloat16)
         filt[f] = value
@@ -354,7 +377,7 @@
     top_wide[:, :width] = top_ref[...].astype(jnp.float32)
     edge = factor_ref[lat, 4, 0:1] * below_wide[count + 1, :width]
     if next_low_ref is not None:
-        row, rest = (expand(next_low_ref[i].astype(jnp.float32)) for i in range(2))
+        row, rest = (expand(next_low_ref[i].astype(jnp.float32))[0] for i in range(2))
         edge += with_rest(row, rest, 1)[:width]
     edge = edge.astype(jnp.bfloat16).astype(jnp.float32)
     north_ref[:width] = 0.25 * jnp.tanh(below_wide[count, :width] + edge)
@@ -442,16 +465,18 @@
     hbm = pl.BlockSpec(memory_space=pltpu.HBM)
     params = pltpu.CompilerParams(vmem_limit_bytes=LIMIT)
     bf16 = jnp.bfloat16
+    total = segments // 2 * PAIR
+    sent = (segments, HEAD // 4, 4, levels)
 
     send = pl.pallas_call(
         pack_kernel,
         in_specs=[hbm],
         out_specs=hbm,
-        out_shape=pltpu.HBM((segments, HEAD, levels), bf16),
+        out_shape=pltpu.HBM((segments // 2, PAIR, levels), bf16),
         scratch_shapes=[
             pltpu.VMEM(tendencies.shape, bf16),
             pltpu.VMEM((fields, SEG * lat_rows, levels), jnp.float32),
-            pltpu.VMEM((segments, HEAD, levels), bf16),
+            pltpu.VMEM((segments // 2, PAIR, levels), bf16),
             pltpu.SemaphoreType.DMA((fields,)),
             pltpu.SemaphoreType.DMA((segments // lat_rows,)),
         ],
@@ -459,10 +484,10 @@
         name="pack",
     )(in_hbm(tendencies))
     with jax.named_scope("forth"):
-        rows = lax.all_to_all(send, "lon", split_axis=0, concat_axis=0, tiled=True)
+        rows = lax.all_to_all(send.reshape(sent), "lon", split_axis=0, concat_axis=0, tiled=True)
 
     factors = jnp.asarray(row_factors(lat_devices, lat_rows))
-    (p_one, p_two, q_one, q_two), waves, used = trig_tables(segments * width, segments)
+    waves, _, used = wave_rows()
     row = lat_place * lat_rows + lon_place % lat_rows
     half = lat_devices * lat_rows // 2
     damping = 0.25 + 0.5 * (row.astype(jnp.float32) + 0.5) / half
@@ -472,13 +497,7 @@
     weight = jnp.where(jnp.asarray(waves)[None] <= bands[row], weight, 0.0)
     with jax.named_scope("table"):
         head_table, tail_table = (
-            (
-                jnp.asarray(p_one)[:, None, :] * jnp.asarray(q_one[part])[None, :, :]
-                + jnp.asarray(p_two)[:, None, :] * jnp.asarray(q_two[part])[None, :, :]
-            )
-            .astype(bf16)
-            .reshape(-1, COEF)
-            for part in (slice(0, HEAD), slice(HEAD, SEG))
+            trig_table(segments * width, segments, order) for order in (HEAD_ORDER, TAIL_ORDER)
         )
 
     with jax.named_scope("edges"):
@@ -501,17 +520,17 @@
         transform_kernel,
         in_specs=[hbm, vmem, vmem, vmem],
         out_specs=hbm,
-        out_shape=pltpu.HBM((segments * HEAD, levels), bf16),
+        out_shape=pltpu.HBM((total, levels), bf16),
         scratch_shapes=[
-            pltpu.VMEM((segments * HEAD, levels), bf16),
-            pltpu.VMEM((segments * HEAD, levels), bf16),
+            pltpu.VMEM((total, levels), bf16),
+            pltpu.VMEM((total, levels), bf16),
             pltpu.SemaphoreType.DMA((LOADS,)),
             pltpu.SemaphoreType.DMA((CHUNKS,)),
         ],
         compiler_params=params,
         name="transform",
     )(
-        in_hbm(rows.reshape(segments * HEAD, levels)),
+        in_hbm(rows.reshape(total, levels)),
         in_vmem(weight),
         in_vmem(head_table),
         in_vmem(tail_table),
@@ -519,8 +538,8 @@
     low, below, top = lax.optimization_barrier((low, below, top))
     with jax.named_scope("back"):
         low = lax.all_to_all(
-            low.reshape(segments, HEAD, levels), "lon", split_axis=0, concat_axis=0, tiled=True
-        )
+            low.reshape(sent), "lon", split_axis=0, concat_axis=0, tiled=True
+        ).reshape(segments // 2, PAIR, levels)
     with jax.named_scope("below"):
         below = lax.ppermute(below, "lat", to_prior)
     with jax.named_scope("top"):
@@ -554,7 +573,7 @@
         functools.partial(early_kernel, waiting),
         in_specs=specs + [vmem] * 3,
         out_specs=[hbm, hbm, vmem],
-        out_shape=[filtered_out, advected_out, jax.ShapeDtypeStruct((2, HEAD, levels), bf16)],
+        out_shape=[filtered_out, advected_out, jax.ShapeDtypeStruct((2, PAIR, levels), bf16)],
         scratch_shapes=on_chip + add_scratch + advect_scratch,
         compiler_params=params,
         name="early",

time: 73.5 us -> 71 us (0.966)
  waiting for transfers between devices: 26.2 us -> 24 us
    all_to_all x2, waiting for transfers between devices: 22.6 us -> 20.9 us  [the longest x1 12.9 us: per_device(): lax.all_to_all(low.reshape(sent), 'lon', split_axis=0, concat_axis=0, til...]
  transfers between devices with their start and end apart: 7 -> 7, of which waited for: 4 -> 4; matrix products, arithmetic and copies ran while one was open for 6% -> 7% of each run, Pallas kernels for 4% -> 4%
where the time goes in v7:
time: 71 us; the launch traced here: 70.4 us
  starting transfers between devices  28.1 us (40%)
  waiting for transfers between devices  24 us (34%)
  Pallas kernels  11.8 us (17%)
  local copies, waits for them, and re-layouts  4.11 us (6%)
  other arithmetic  1.41 us (2%)
  between operations  1.05 us (1%)
    all_to_all x1, starting transfers between devices, per_device(): lax.all_to_all(send.reshape(sent), 'lon', split_axis=0, concat_axis=0, ti...  13.4 us
    all_to_all x1, waiting for transfers between devices, per_device(): lax.all_to_all(low.reshape(sent), 'lon', split_axis=0, concat_axis=0, til...  12.9 us
    all_to_all x1, waiting for transfers between devices, per_device(): lax.all_to_all(send.reshape(sent), 'lon', split_axis=0, concat_axis=0, ti...  8 us
    all_to_all x1, starting transfers between devices, per_device(): lax.all_to_all(low.reshape(sent), 'lon', split_axis=0, concat_axis=0, til...  6.23 us
    pallas_call x1, Pallas kernels, per_device(): pl.pallas_call(transform_kernel, in_specs=[hbm, vmem, vmem, vmem], out_sp...  3.73 us
    ppermute x1, starting transfers between devices, per_device(): top = lax.ppermute(top, 'lat', to_next)  3.03 us
    pallas_call x1, Pallas kernels, per_device(): pl.pallas_call(pack_kernel, in_specs=[hbm], out_specs=hbm, out_shape=pltp...  3.01 us
    ppermute x1, starting transfers between devices, per_device(): high = lax.ppermute(high, 'lon', west_ring)  2.75 us
  transfers between devices with their start and end apart: 7, of which 4 were waited for; matrix products, arithmetic and copies ran while one was open for 7% of the time, Pallas kernels for 4%

profile of v7, /device:TPU:2, one launch (start us, length us, event | category | flops | bytes accessed | tf_op | source)
XLA Modules:
  0.0 70.4 jit_solution(13057610191095215336)
XLA Ops:
  0.6 0.0 copy-start
  0.6 0.0 copy-start.3
  0.7 3.0 %pack.1 = bf16[32,72,128]{2,1,0:T(8,128)(2,1)} custom-call(bf16[3,45,16,128]{3,2,1,0:T(8,128)(2,1)} %bitcast.39), custom_call_target="tpu_custom_call" | custom-call | tf_op jit(solution)/shard_map/pack/pallas_call | solution.py:471
  3.7 0.0 copy-start.2
  3.7 13.4 %all-to-all-start = ((bf16[64,9,4,128]{3,2,1,0:T(4,128)(2,1)}), bf16[64,9,4,128]{3,2,1,0:T(4,128)(2,1)}, u32[]{:S(2)}, u32[]{:S(2)}) async-start(bf16[64,9,4,128]{3,2,1,0:T(4,128)(2,1)} %bitcast.50), calls=%async_computation | async-start | bytes 1179648 | tf_op jit(solution)/shard_map/forth/all_to_all | solution.py:487
  17.1 0.0 copy-done
  17.1 0.2 copy.62
  17.3 0.0 copy-start.5
  17.3 0.2 copy.61
  17.6 0.0 copy-start.6
  17.6 0.0 copy-start.15
  17.6 0.0 copy-start.13
  17.6 0.0 copy-start.14
  17.6 0.0 copy-start.7
  17.6 0.0 copy-start.8
  17.7 0.0 copy-start.11
  17.7 0.0 copy-start.12
  17.7 0.4 copy-done.5
  18.1 0.2 copy-done.6
  18.3 0.0 copy-start.9
  18.4 0.0 copy-start.10
  18.4 0.6 copy.60
  19.0 0.0 copy-start.4
  19.0 0.1 fusion
  19.1 2.8 %collective-permute-start = (bf16[7,16,128]{2,1,0:T(8,128)(2,1)S(1)}, bf16[7,16,128]{2,1,0:T(8,128)(2,1)S(1)}, u32[]{:S(2)}, u32[]{:S(2)}) collective-permute-start(bf16[7,16,128]{2,1,0:T(8,128)(2,1)S(1)} %pad_maximum_fusion.1), channel_id=1, source_target_pairs={{1,0},{2,1},{3,2},{4,3},{5,4},{6,5},{7,6},{8,7},{9,8},{10,9},{11,1... | collective-permute-start | bytes 86024 | tf_op jit(solution)/shard_map/columns/ppermute | solution.py:513
  21.9 0.1 collective-permute-start.1
  22.0 0.7 dynamic_slice.3
  22.7 0.7 multiply_select_fusion
  23.4 0.7 %slice_bitcast_fusion.2 = (bf16[1,45,128]{2,1,0:T(8,128)(2,1)S(1)}, bf16[1,45,128]{2,1,0:T(8,128)(2,1)S(1)}) fusion(bf16[3,45,16,128]{3,1,2,0:T(8,128)(2,1)} %bitcast.56, bf16[2,45,16,128]{3,1,2,0:T(8,128)(2,1)} %bitcast.59), kind=kLoop, calls=%fused_computation.11 | loop fusion | bytes 46080 | tf_op jit(solution)/shard_map/edges/squeeze | solution.py:509
  24.1 0.9 %slice_bitcast_fusion = (bf16[5,45,128]{2,1,0:T(8,128)(2,1)S(1)}, bf16[5,45,128]{2,1,0:T(8,128)(2,1)S(1)}) fusion(bf16[5,45,16,128]{3,1,0,2:T(8,128)(2,1)} %bitcast.54), kind=kLoop, calls=%fused_computation.6 | loop fusion | bytes 230400 | tf_op jit(solution)/shard_map/edges/convert_element_type | solution.py:511
  25.0 0.2 add_convert_fusion.1
  25.2 0.5 add_convert_fusion
  25.8 2.2 %collective-permute-done.1.side_ref = bf16[5,16,128]{2,1,0:T(8,128)(2,1)S(1)} collective-permute-done((bf16[5,16,128]{2,1,0:T(8,128)(2,1)S(1)}, bf16[5,16,128]{2,1,0:T(8,128)(2,1)S(1)}, u32[]{:S(2)}, u32[]{:S(2)}) %collective-permute-start.1) | collective-permute-done | bytes 20512 | tf_op jit(solution)/shard_map/columns/ppermute | solution.py:514
  28.0 0.0 collective-permute-done.high_ref
  28.0 8.0 %all-to-all-done = bf16[64,9,4,128]{3,2,1,0:T(4,128)(2,1)} async-done(((bf16[64,9,4,128]{3,2,1,0:T(4,128)(2,1)}), bf16[64,9,4,128]{3,2,1,0:T(4,128)(2,1)}, u32[]{:S(2)}, u32[]{:S(2)}) %all-to-all-start) | async-done | bytes 589856 | tf_op jit(solution)/shard_map/forth/all_to_all | solution.py:487
  36.0 3.7 %transform.1 = bf16[2304,128]{1,0:T(8,128)(2,1)} custom-call(bf16[2304,128]{1,0:T(8,128)(2,1)} %bitcast.14.rows_ref, f32[1,384]{1,0:T(1,128)S(1)} %select_n.25.weight_ref, bf16[2304,384]{1,0:T(8,128)(2,1)S(1)} %bitcast.42, bf16[768,384]{1,0:T(8,128)(2,1)S(1)} %bitcast.45), custom_call_target="tpu_custom_call" | custom-call | tf_op jit(solution)/shard_map/transform/pallas_call | solution.py:519
  39.7 6.2 %all-to-all-start.1 = ((bf16[64,9,4,128]{3,2,1,0:T(4,128)(2,1)}), bf16[64,9,4,128]{3,2,1,0:T(4,128)(2,1)S(1)}, u32[]{:S(2)}, u32[]{:S(2)}) async-start(bf16[64,9,4,128]{3,2,1,0:T(4,128)(2,1)} %bitcast.51), calls=%async_computation.1 | async-start | bytes 1179648 | tf_op jit(solution)/shard_map/back/all_to_all | solution.py:540
  46.0 1.3 %collective-permute-start.2 = (bf16[7,45,128]{2,1,0:T(8,128)(2,1)S(1)}, bf16[7,45,128]{2,1,0:T(8,128)(2,1)S(1)}, u32[]{:S(2)}, u32[]{:S(2)}) collective-permute-start(bf16[7,45,128]{2,1,0:T(8,128)(2,1)S(1)} %pad_maximum_fusion), channel_id=1, source_target_pairs={{64,0},{128,64},{192,128},{65,1},{129,65},{193,129},{66,2},{130,66... | collective-permute-start | bytes 241928 | tf_op jit(solution)/shard_map/below/ppermute | solution.py:544
  47.3 3.0 %collective-permute-start.3 = (bf16[5,45,128]{2,1,0:T(8,128)(2,1)S(1)}, bf16[5,45,128]{2,1,0:T(8,128)(2,1)S(1)}, u32[]{:S(2)}, u32[]{:S(2)}) collective-permute-start(bf16[5,45,128]{2,1,0:T(8,128)(2,1)S(1)} %get-tuple-element.29), channel_id=1, source_target_pairs={{0,64},{64,128},{128,192},{1,65},{65,129},{129,193},{2,66},{66,130... | collective-permute-start | bytes 172808 | tf_op jit(solution)/shard_map/top/ppermute | solution.py:546
  50.3 0.9 %collective-permute-done.3.top_ref = bf16[5,45,128]{2,1,0:T(8,128)(2,1)S(1)} collective-permute-done((bf16[5,45,128]{2,1,0:T(8,128)(2,1)S(1)}, bf16[5,45,128]{2,1,0:T(8,128)(2,1)S(1)}, u32[]{:S(2)}, u32[]{:S(2)}) %collective-permute-start.3) | collective-permute-done | bytes 57632 | tf_op jit(solution)/shard_map/top/ppermute | solution.py:546
  51.2 0.0 collective-permute-done.2.below_ref
  51.2 12.9 %all-to-all-done.1 = bf16[64,9,4,128]{3,2,1,0:T(4,128)(2,1)S(1)} async-done(((bf16[64,9,4,128]{3,2,1,0:T(4,128)(2,1)}), bf16[64,9,4,128]{3,2,1,0:T(4,128)(2,1)S(1)}, u32[]{:S(2)}, u32[]{:S(2)}) %all-to-all-start.1) | async-done | bytes 589856 | tf_op jit(solution)/shard_map/back/all_to_all | solution.py:540
  64.0 0.0 copy-done.1
  64.0 0.1 early.1
  64.2 1.3 %collective-permute-start.4 = (bf16[2,72,128]{2,1,0:T(8,128)(2,1)S(1)}, bf16[2,72,128]{2,1,0:T(8,128)(2,1)S(1)}, u32[]{:S(2)}, u32[]{:S(2)}) collective-permute-start(bf16[2,72,128]{2,1,0:T(8,128)(2,1)S(1)} %get-tuple-element.34), channel_id=1, source_target_pairs={{64,0},{65,1},{66,2},{67,3},{68,4},{69,5},{70,6},{71,7},{72,8},{73... | collective-permute-start | bytes 110600 | tf_op jit(solution)/shard_map/ppermute | solution.py:581
  65.5 2.7 %middle.1 = (bf16[3,45,16,128]{3,2,1,0:T(8,128)(2,1)}, f32[2,46,16,128]{3,2,1,0:T(8,128)S(1)}, f32[5,45,16,128]{3,2,1,0:T(8,128)S(1)}) custom-call(bf16[32,72,128]{2,1,0:T(8,128)(2,1)S(1)} %bitcast.44, f32[4,5,16,1]{3,2,1,0:T(8,128)S(1)} %copy-done.1, bf16[3,45,16,128]{3,2,1,0:T(8,128)(2,1)S(1)} %bitcast.41, ...), custom_call_target="tpu_custom_call", output_to_operand_aliasing={{0}: (6, {})} | custom-call | tf_op jit(solution)/shard_map/middle/pallas_call | solution.py:582
  68.2 0.0 collective-permute-done.4.next_low_ref
  68.2 2.2 %late.1 = f32[5,45,16,128]{3,2,1,0:T(8,128)} custom-call(f32[4,5,16,1]{3,2,1,0:T(8,128)S(1)} %copy-done.1, f32[2,46,16,128]{3,2,1,0:T(8,128)S(1)} %get-tuple-element.32.courant_ref, f32[5,45,16,128]{3,2,1,0:T(8,128)S(1)} %get-tuple-element.33.tracer_ref, bf16[7,16,128]{2,1,0:T(8,128)(2,1)S(1)} %collective-permute-done.high_ref, ...), custom_call_target="tpu_custom_call", output_to_operand_aliasing={{}: (8, {})} | custom-call | tf_op jit(solution)/shard_map/late/pallas_call | solution.py:592
  (21 shorter events, 0.1 us)
Async XLA Ops:
  0.6 16.5 %copy-start = (bf16[3,16,45,128]{3,1,2,0:T(8,128)(2,1)S(1)}, bf16[3,16,45,128]{3,1,2,0:T(8,128)(2,1)}, u32[]{:S(2)}) copy-start(bf16[3,16,45,128]{3,1,2,0:T(8,128)(2,1)} %param.15) | copy-start | bytes 1658884
  0.6 16.7 %copy-start.3 = (f32[2,16,45,128]{3,1,2,0:T(8,128)S(1)}, f32[2,16,45,128]{3,1,2,0:T(8,128)}, u32[]{:S(2)}) copy-start(f32[2,16,45,128]{3,1,2,0:T(8,128)} %param.17) | copy-start | bytes 2211844
  3.7 14.7 %copy-start.2 = (f32[5,16,45,128]{3,1,2,0:T(8,128)S(1)}, f32[5,16,45,128]{3,1,2,0:T(8,128)}, u32[]{:S(2)}) copy-start(f32[5,16,45,128]{3,1,2,0:T(8,128)} %param.18) | copy-start | bytes 5529604
  3.7 32.3 %all-to-all-start = ((bf16[64,9,4,128]{3,2,1,0:T(4,128)(2,1)}), bf16[64,9,4,128]{3,2,1,0:T(4,128)(2,1)}, u32[]{:S(2)}, u32[]{:S(2)}) async-start(bf16[64,9,4,128]{3,2,1,0:T(4,128)(2,1)} %bitcast.50), calls=%async_computation | async-start | bytes 1179648 | tf_op jit(solution)/shard_map/forth/all_to_all | solution.py:487
  17.3 0.8 %copy-start.5 = (bf16[3,16,45,128]{3,2,1,0:T(8,128)(2,1)}, bf16[3,16,45,128]{3,2,1,0:T(8,128)(2,1)S(1)}, u32[]{:S(2)}) copy-start(bf16[3,16,45,128]{3,2,1,0:T(8,128)(2,1)S(1)} %copy.62) | copy-start | bytes 1658884
  17.6 0.7 %copy-start.6 = (bf16[2,16,45,128]{3,2,1,0:T(8,128)(2,1)}, bf16[2,16,45,128]{3,2,1,0:T(8,128)(2,1)S(1)}, u32[]{:S(2)}) copy-start(bf16[2,16,45,128]{3,2,1,0:T(8,128)(2,1)S(1)} %copy.61) | copy-start | bytes 1105924
  17.6 4.4 %copy-start.15 = (s32[64]{0:T(128)S(1)}, s32[64]{0:T(128)}, u32[]{:S(2)}) copy-start(s32[64]{0:T(128)} %param.16) | copy-start | bytes 772
  17.6 5.1 %copy-start.13 = (f32[384]{0:T(512)S(1)}, f32[384]{0:T(512)}, u32[]{:S(2)}) copy-start(f32[384]{0:T(512)} %constant.58.clone) | copy-start | bytes 4612
  17.6 5.1 %copy-start.14 = (s32[384]{0:T(512)S(1)}, s32[384]{0:T(512)}, u32[]{:S(2)}) copy-start(s32[384]{0:T(512)} %constant.59.clone) | copy-start | bytes 4612
  17.6 7.3 %copy-start.7 = (f32[32,384]{1,0:T(8,128)S(1)}, f32[32,384]{1,0:T(8,128)}, u32[]{:S(2)}) copy-start(f32[32,384]{1,0:T(8,128)} %constant.61.clone) | copy-start | bytes 147460
  17.6 7.3 %copy-start.8 = (f32[32,384]{1,0:T(8,128)S(1)}, f32[32,384]{1,0:T(8,128)}, u32[]{:S(2)}) copy-start(f32[32,384]{1,0:T(8,128)} %constant.60.clone) | copy-start | bytes 147460
  17.7 7.3 %copy-start.11 = (f32[24,384]{1,0:T(8,128)S(1)}, f32[24,384]{1,0:T(8,128)}, u32[]{:S(2)}) copy-start(f32[24,384]{1,0:T(8,128)} %constant.65.clone) | copy-start | bytes 110596
  17.7 7.3 %copy-start.12 = (f32[24,384]{1,0:T(8,128)S(1)}, f32[24,384]{1,0:T(8,128)}, u32[]{:S(2)}) copy-start(f32[24,384]{1,0:T(8,128)} %constant.64.clone) | copy-start | bytes 110596
  18.3 6.8 %copy-start.9 = (f32[72,384]{1,0:T(8,128)S(1)}, f32[72,384]{1,0:T(8,128)}, u32[]{:S(2)}) copy-start(f32[72,384]{1,0:T(8,128)} %constant.63.clone) | copy-start | bytes 331780
  18.4 6.8 %copy-start.10 = (f32[72,384]{1,0:T(8,128)S(1)}, f32[72,384]{1,0:T(8,128)}, u32[]{:S(2)}) copy-start(f32[72,384]{1,0:T(8,128)} %constant.62.clone) | copy-start | bytes 331780
  19.0 2.9 %copy-start.4 = (bf16[5,16,45,128]{3,2,0,1:T(8,128)(2,1)}, bf16[5,16,45,128]{3,2,0,1:T(8,128)(2,1)S(1)}, u32[]{:S(2)}) copy-start(bf16[5,16,45,128]{3,2,0,1:T(8,128)(2,1)S(1)} %copy.60) | copy-start | bytes 2764804
  19.1 8.9 %collective-permute-start = (bf16[7,16,128]{2,1,0:T(8,128)(2,1)S(1)}, bf16[7,16,128]{2,1,0:T(8,128)(2,1)S(1)}, u32[]{:S(2)}, u32[]{:S(2)}) collective-permute-start(bf16[7,16,128]{2,1,0:T(8,128)(2,1)S(1)} %pad_maximum_fusion.1), channel_id=1, source_target_pairs={{1,0},{2,1},{3,2},{4,3},{5,4},{6,5},{7,6},{8,7},{9,8},{10,9},{11,1... | collective-permute-start | bytes 86024 | tf_op jit(solution)/shard_map/columns/ppermute | solution.py:513
  21.9 6.1 %collective-permute-start.1 = (bf16[5,16,128]{2,1,0:T(8,128)(2,1)S(1)}, bf16[5,16,128]{2,1,0:T(8,128)(2,1)S(1)}, u32[]{:S(2)}, u32[]{:S(2)}) collective-permute-start(bf16[5,16,128]{2,1,0:T(8,128)(2,1)S(1)} %bitcast.61), channel_id=1, source_target_pairs={{0,1},{1,2},{2,3},{3,4},{4,5},{5,6},{6,7},{7,8},{8,9},{9,10},{10,1... | collective-permute-start | bytes 61448 | tf_op jit(solution)/shard_map/columns/ppermute | solution.py:514
  36.0 28.1 %copy-start.1 = (f32[4,5,16,1]{3,2,1,0:T(8,128)S(1)}, f32[4,5,16,1]{3,2,1,0:T(8,128)}, u32[]{:S(2)}) copy-start(f32[4,5,16,1]{3,2,1,0:T(8,128)} %constant.57.clone.factor_ref) | copy-start | bytes 3844
  39.7 24.3 %all-to-all-start.1 = ((bf16[64,9,4,128]{3,2,1,0:T(4,128)(2,1)}), bf16[64,9,4,128]{3,2,1,0:T(4,128)(2,1)S(1)}, u32[]{:S(2)}, u32[]{:S(2)}) async-start(bf16[64,9,4,128]{3,2,1,0:T(4,128)(2,1)} %bitcast.51), calls=%async_computation.1 | async-start | bytes 1179648 | tf_op jit(solution)/shard_map/back/all_to_all | solution.py:540
  46.0 5.2 %collective-permute-start.2 = (bf16[7,45,128]{2,1,0:T(8,128)(2,1)S(1)}, bf16[7,45,128]{2,1,0:T(8,128)(2,1)S(1)}, u32[]{:S(2)}, u32[]{:S(2)}) collective-permute-start(bf16[7,45,128]{2,1,0:T(8,128)(2,1)S(1)} %pad_maximum_fusion), channel_id=1, source_target_pairs={{64,0},{128,64},{192,128},{65,1},{129,65},{193,129},{66,2},{130,66... | collective-permute-start | bytes 241928 | tf_op jit(solution)/shard_map/below/ppermute | solution.py:544
  47.3 3.9 %collective-permute-start.3 = (bf16[5,45,128]{2,1,0:T(8,128)(2,1)S(1)}, bf16[5,45,128]{2,1,0:T(8,128)(2,1)S(1)}, u32[]{:S(2)}, u32[]{:S(2)}) collective-permute-start(bf16[5,45,128]{2,1,0:T(8,128)(2,1)S(1)} %get-tuple-element.29), channel_id=1, source_target_pairs={{0,64},{64,128},{128,192},{1,65},{65,129},{129,193},{2,66},{66,130... | collective-permute-start | bytes 172808 | tf_op jit(solution)/shard_map/top/ppermute | solution.py:546
  64.2 4.0 %collective-permute-start.4 = (bf16[2,72,128]{2,1,0:T(8,128)(2,1)S(1)}, bf16[2,72,128]{2,1,0:T(8,128)(2,1)S(1)}, u32[]{:S(2)}, u32[]{:S(2)}) collective-permute-start(bf16[2,72,128]{2,1,0:T(8,128)(2,1)S(1)} %get-tuple-element.34), channel_id=1, source_target_pairs={{64,0},{65,1},{66,2},{67,3},{68,4},{69,5},{70,6},{71,7},{72,8},{73... | collective-permute-start | bytes 110600 | tf_op jit(solution)/shard_map/ppermute | solution.py:581

commit v8 on v7

--- a/solution.py
+++ b/solution.py
@@ -83,7 +83,7 @@
 
 def pack_kernel(tend_ref, out_ref, tend, wide, rows, in_sems, out_sems):
     fields, width, lat_rows, levels = tend.shape
-    size = width * lat_rows
+    stride = lat_rows + 1
     half = lat_rows // 2
     loads = [pltpu.make_async_copy(tend_ref.at[f], tend.at[f], in_sems.at[f]) for f in range(fields)]
     for load in loads:
@@ -101,7 +101,7 @@
         rows[pair] = jnp.concatenate(slots, axis=0).astype(jnp.bfloat16)
 
     def whole(f, r):
-        return wide[f, pl.ds(r, SEG, stride=lat_rows), :]
+        return wide[f, pl.ds(r, SEG, stride=stride), :]
 
     def left(r):
         moved = [pltpu.roll(whole(f, r), (f + 1) * QUARTER, 1) for f in range(fields)]
@@ -109,10 +109,11 @@
         return jnp.where(lane < QUARTER, moved[0], jnp.where(lane < 2 * QUARTER, moved[1], moved[2]))
 
     for f in range(fields):
-        wide[f, size:] = jnp.zeros((SEG * lat_rows - size, levels), jnp.float32)
+        wide[f, width * stride :] = jnp.zeros(((SEG - width) * stride, levels), jnp.float32)
     for f in range(fields):
         loads[f].wait()
-        wide[f, :size] = tend[f].astype(jnp.float32).reshape(size, levels)
+        for q in range(width):
+            wide[f, q * stride : q * stride + lat_rows] = tend[f, q].astype(jnp.float32)
         for r in range(half):
             put(f * half + r, whole(f, 2 * r), whole(f, 2 * r + 1))
         send(f)
@@ -306,7 +307,7 @@
 ):
     fields, width, lat_rows, levels = tend_ref.shape
     count = high_ref.shape[0] - 2
-    size = width * lat_rows
+    stride = lat_rows + 1
     winds = [
         pltpu.make_async_copy(wind_hbm.at[f], wind_ref.at[f], sems.at[fields + f]) for f in range(2)
     ]
@@ -325,17 +326,17 @@
             pair = expand(low_ref[f * half + r].astype(jnp.float32))
             for i in range(2):
                 row = with_rest(pair[i], rest_ref[2 * r + i], f)
-                wide_ref[f, pl.ds(2 * r + i, SEG, stride=lat_rows), :] = row
-        low = wide_ref[f, :size].reshape(width, lat_rows, levels)
-        value = (damp[None] * tend_ref[f].astype(jnp.float32) + low).astype(jnp.bfloat16)
-        filt[f] = value
+                wide_ref[f, pl.ds(2 * r + i, SEG, stride=stride), :] = row
+        for q in range(width):
+            low = wide_ref[f, q * stride : q * stride + lat_rows]
+            filt[f, q] = (damp * tend_ref[f, q].astype(jnp.float32) + low).astype(jnp.bfloat16)
         stores.append(pltpu.make_async_copy(filt.at[f], filt_hbm.at[f], sems.at[f]))
         stores[-1].start()
         if f < 2:
             winds[f].wait()
-            courant_ref[f, :width] = (0.5, 0.25)[f] * jnp.tanh(wind_ref[f] + value.astype(jnp.float32))
+            courant_ref[f, :width] = (0.5, 0.25)[f] * jnp.tanh(wind_ref[f] + filt[f].astype(jnp.float32))
         if f == 0:
-            edge = damp * high_ref[count + 1].astype(jnp.float32) + wide_ref[f, size : size + lat_rows]
+            edge = damp * high_ref[count + 1].astype(jnp.float32) + wide_ref[f, width * stride : width * stride + lat_rows]
             edge = edge.astype(jnp.bfloat16).astype(jnp.float32)
             courant_ref[f, width] = 0.5 * jnp.tanh(high_ref[count].astype(jnp.float32) + edge)
     return stores
@@ -475,7 +476,7 @@
         out_shape=pltpu.HBM((segments // 2, PAIR, levels), bf16),
         scratch_shapes=[
             pltpu.VMEM(tendencies.shape, bf16),
-            pltpu.VMEM((fields, SEG * lat_rows, levels), jnp.float32),
+            pltpu.VMEM((fields, SEG * (lat_rows + 1), levels), jnp.float32),
             pltpu.VMEM((segments // 2, PAIR, levels), bf16),
             pltpu.SemaphoreType.DMA((fields,)),
             pltpu.SemaphoreType.DMA((segments // lat_rows,)),
@@ -552,7 +553,7 @@
         pltpu.VMEM(tracers.shape, jnp.float32),
     ]
     add_scratch = [
-        pltpu.VMEM((fields, SEG * lat_rows, levels), jnp.float32),
+        pltpu.VMEM((fields, SEG * (lat_rows + 1), levels), jnp.float32),
         pltpu.VMEM((lat_rows, SEG, levels), jnp.float32),
         pltpu.VMEM(tendencies.shape, bf16),
         pltpu.VMEM(winds.shape, jnp.float32),

time: 71 us -> 70.7 us (level)
  no operation moved by 1% of the time
where the time goes in v8:
time: 70.7 us; the launch traced here: 70.2 us
  starting transfers between devices  28.1 us (40%)
  waiting for transfers between devices  24 us (34%)
  Pallas kernels  11.5 us (16%)
  local copies, waits for them, and re-layouts  4.11 us (6%)
  other arithmetic  1.41 us (2%)
  between operations  1.05 us (1%)
    all_to_all x1, starting transfers between devices, per_device(): lax.all_to_all(send.reshape(sent), 'lon', split_axis=0, concat_axis=0, ti...  13.4 us
    all_to_all x1, waiting for transfers between devices, per_device(): lax.all_to_all(low.reshape(sent), 'lon', split_axis=0, concat_axis=0, til...  12.9 us
    all_to_all x1, waiting for transfers between devices, per_device(): lax.all_to_all(send.reshape(sent), 'lon', split_axis=0, concat_axis=0, ti...  8 us
    all_to_all x1, starting transfers between devices, per_device(): lax.all_to_all(low.reshape(sent), 'lon', split_axis=0, concat_axis=0, til...  6.25 us
    pallas_call x1, Pallas kernels, per_device(): pl.pallas_call(transform_kernel, in_specs=[hbm, vmem, vmem, vmem], out_sp...  3.72 us
    ppermute x1, starting transfers between devices, per_device(): top = lax.ppermute(top, 'lat', to_next)  3.03 us
    pallas_call x1, Pallas kernels, per_device(): pl.pallas_call(pack_kernel, in_specs=[hbm], out_specs=hbm, out_shape=pltp...  2.81 us
    ppermute x1, starting transfers between devices, per_device(): high = lax.ppermute(high, 'lon', west_ring)  2.75 us
  transfers between devices with their start and end apart: 7, of which 4 were waited for; matrix products, arithmetic and copies ran while one was open for 7% of the time, Pallas kernels for 4%

profile of v8, /device:TPU:2, one launch (start us, length us, event | category | flops | bytes accessed | tf_op | source)
XLA Modules:
  0.0 70.2 jit_solution(17177693869149704124)
XLA Ops:
  0.6 0.0 copy-start
  0.6 0.0 copy-start.3
  0.7 2.8 %pack.1 = bf16[32,72,128]{2,1,0:T(8,128)(2,1)} custom-call(bf16[3,45,16,128]{3,2,1,0:T(8,128)(2,1)} %bitcast.39), custom_call_target="tpu_custom_call" | custom-call | tf_op jit(solution)/shard_map/pack/pallas_call | solution.py:472
  3.5 0.0 copy-start.2
  3.5 13.4 %all-to-all-start = ((bf16[64,9,4,128]{3,2,1,0:T(4,128)(2,1)}), bf16[64,9,4,128]{3,2,1,0:T(4,128)(2,1)}, u32[]{:S(2)}, u32[]{:S(2)}) async-start(bf16[64,9,4,128]{3,2,1,0:T(4,128)(2,1)} %bitcast.50), calls=%async_computation | async-start | bytes 1179648 | tf_op jit(solution)/shard_map/forth/all_to_all | solution.py:488
  16.9 0.0 copy-done
  16.9 0.2 copy.62
  17.1 0.0 copy-start.5
  17.1 0.2 copy.61
  17.4 0.0 copy-start.6
  17.4 0.0 copy-start.15
  17.4 0.0 copy-start.13
  17.4 0.0 copy-start.14
  17.4 0.0 copy-start.7
  17.4 0.0 copy-start.8
  17.5 0.0 copy-start.11
  17.5 0.0 copy-start.12
  17.5 0.4 copy-done.5
  17.9 0.2 copy-done.6
  18.1 0.0 copy-start.9
  18.2 0.0 copy-start.10
  18.2 0.6 copy.60
  18.8 0.0 copy-start.4
  18.8 0.1 fusion
  18.9 2.8 %collective-permute-start = (bf16[7,16,128]{2,1,0:T(8,128)(2,1)S(1)}, bf16[7,16,128]{2,1,0:T(8,128)(2,1)S(1)}, u32[]{:S(2)}, u32[]{:S(2)}) collective-permute-start(bf16[7,16,128]{2,1,0:T(8,128)(2,1)S(1)} %pad_maximum_fusion.1), channel_id=1, source_target_pairs={{1,0},{2,1},{3,2},{4,3},{5,4},{6,5},{7,6},{8,7},{9,8},{10,9},{11,1... | collective-permute-start | bytes 86024 | tf_op jit(solution)/shard_map/columns/ppermute | solution.py:514
  21.7 0.1 collective-permute-start.1
  21.8 0.7 dynamic_slice.3
  22.5 0.7 multiply_select_fusion
  23.2 0.7 %slice_bitcast_fusion.2 = (bf16[1,45,128]{2,1,0:T(8,128)(2,1)S(1)}, bf16[1,45,128]{2,1,0:T(8,128)(2,1)S(1)}) fusion(bf16[3,45,16,128]{3,1,2,0:T(8,128)(2,1)} %bitcast.56, bf16[2,45,16,128]{3,1,2,0:T(8,128)(2,1)} %bitcast.59), kind=kLoop, calls=%fused_computation.11 | loop fusion | bytes 46080 | tf_op jit(solution)/shard_map/edges/squeeze | solution.py:510
  23.9 0.9 %slice_bitcast_fusion = (bf16[5,45,128]{2,1,0:T(8,128)(2,1)S(1)}, bf16[5,45,128]{2,1,0:T(8,128)(2,1)S(1)}) fusion(bf16[5,45,16,128]{3,1,0,2:T(8,128)(2,1)} %bitcast.54), kind=kLoop, calls=%fused_computation.6 | loop fusion | bytes 230400 | tf_op jit(solution)/shard_map/edges/convert_element_type | solution.py:512
  24.8 0.2 add_convert_fusion.1
  25.0 0.5 add_convert_fusion
  25.6 2.2 %collective-permute-done.1.side_ref = bf16[5,16,128]{2,1,0:T(8,128)(2,1)S(1)} collective-permute-done((bf16[5,16,128]{2,1,0:T(8,128)(2,1)S(1)}, bf16[5,16,128]{2,1,0:T(8,128)(2,1)S(1)}, u32[]{:S(2)}, u32[]{:S(2)}) %collective-permute-start.1) | collective-permute-done | bytes 20512 | tf_op jit(solution)/shard_map/columns/ppermute | solution.py:515
  27.8 0.0 collective-permute-done.high_ref
  27.8 8.0 %all-to-all-done = bf16[64,9,4,128]{3,2,1,0:T(4,128)(2,1)} async-done(((bf16[64,9,4,128]{3,2,1,0:T(4,128)(2,1)}), bf16[64,9,4,128]{3,2,1,0:T(4,128)(2,1)}, u32[]{:S(2)}, u32[]{:S(2)}) %all-to-all-start) | async-done | bytes 589856 | tf_op jit(solution)/shard_map/forth/all_to_all | solution.py:488
  35.8 3.7 %transform.1 = bf16[2304,128]{1,0:T(8,128)(2,1)} custom-call(bf16[2304,128]{1,0:T(8,128)(2,1)} %bitcast.14.rows_ref, f32[1,384]{1,0:T(1,128)S(1)} %select_n.25.weight_ref, bf16[2304,384]{1,0:T(8,128)(2,1)S(1)} %bitcast.42, bf16[768,384]{1,0:T(8,128)(2,1)S(1)} %bitcast.45), custom_call_target="tpu_custom_call" | custom-call | tf_op jit(solution)/shard_map/transform/pallas_call | solution.py:520
  39.5 6.3 %all-to-all-start.1 = ((bf16[64,9,4,128]{3,2,1,0:T(4,128)(2,1)}), bf16[64,9,4,128]{3,2,1,0:T(4,128)(2,1)S(1)}, u32[]{:S(2)}, u32[]{:S(2)}) async-start(bf16[64,9,4,128]{3,2,1,0:T(4,128)(2,1)} %bitcast.51), calls=%async_computation.1 | async-start | bytes 1179648 | tf_op jit(solution)/shard_map/back/all_to_all | solution.py:541
  45.8 1.3 %collective-permute-start.2 = (bf16[7,45,128]{2,1,0:T(8,128)(2,1)S(1)}, bf16[7,45,128]{2,1,0:T(8,128)(2,1)S(1)}, u32[]{:S(2)}, u32[]{:S(2)}) collective-permute-start(bf16[7,45,128]{2,1,0:T(8,128)(2,1)S(1)} %pad_maximum_fusion), channel_id=1, source_target_pairs={{64,0},{128,64},{192,128},{65,1},{129,65},{193,129},{66,2},{130,66... | collective-permute-start | bytes 241928 | tf_op jit(solution)/shard_map/below/ppermute | solution.py:545
  47.1 3.0 %collective-permute-start.3 = (bf16[5,45,128]{2,1,0:T(8,128)(2,1)S(1)}, bf16[5,45,128]{2,1,0:T(8,128)(2,1)S(1)}, u32[]{:S(2)}, u32[]{:S(2)}) collective-permute-start(bf16[5,45,128]{2,1,0:T(8,128)(2,1)S(1)} %get-tuple-element.29), channel_id=1, source_target_pairs={{0,64},{64,128},{128,192},{1,65},{65,129},{129,193},{2,66},{66,130... | collective-permute-start | bytes 172808 | tf_op jit(solution)/shard_map/top/ppermute | solution.py:547
  50.1 0.9 %collective-permute-done.3.top_ref = bf16[5,45,128]{2,1,0:T(8,128)(2,1)S(1)} collective-permute-done((bf16[5,45,128]{2,1,0:T(8,128)(2,1)S(1)}, bf16[5,45,128]{2,1,0:T(8,128)(2,1)S(1)}, u32[]{:S(2)}, u32[]{:S(2)}) %collective-permute-start.3) | collective-permute-done | bytes 57632 | tf_op jit(solution)/shard_map/top/ppermute | solution.py:547
  51.0 0.0 collective-permute-done.2.below_ref
  51.0 12.9 %all-to-all-done.1 = bf16[64,9,4,128]{3,2,1,0:T(4,128)(2,1)S(1)} async-done(((bf16[64,9,4,128]{3,2,1,0:T(4,128)(2,1)}), bf16[64,9,4,128]{3,2,1,0:T(4,128)(2,1)S(1)}, u32[]{:S(2)}, u32[]{:S(2)}) %all-to-all-start.1) | async-done | bytes 589856 | tf_op jit(solution)/shard_map/back/all_to_all | solution.py:541
  63.8 0.0 copy-done.1
  63.9 0.1 early.1
  64.0 1.3 %collective-permute-start.4 = (bf16[2,72,128]{2,1,0:T(8,128)(2,1)S(1)}, bf16[2,72,128]{2,1,0:T(8,128)(2,1)S(1)}, u32[]{:S(2)}, u32[]{:S(2)}) collective-permute-start(bf16[2,72,128]{2,1,0:T(8,128)(2,1)S(1)} %get-tuple-element.34), channel_id=1, source_target_pairs={{64,0},{65,1},{66,2},{67,3},{68,4},{69,5},{70,6},{71,7},{72,8},{73... | collective-permute-start | bytes 110600 | tf_op jit(solution)/shard_map/ppermute | solution.py:582
  65.3 2.7 %middle.1 = (bf16[3,45,16,128]{3,2,1,0:T(8,128)(2,1)}, f32[2,46,16,128]{3,2,1,0:T(8,128)S(1)}, f32[5,45,16,128]{3,2,1,0:T(8,128)S(1)}) custom-call(bf16[32,72,128]{2,1,0:T(8,128)(2,1)S(1)} %bitcast.44, f32[4,5,16,1]{3,2,1,0:T(8,128)S(1)} %copy-done.1, bf16[3,45,16,128]{3,2,1,0:T(8,128)(2,1)S(1)} %bitcast.41, ...), custom_call_target="tpu_custom_call", output_to_operand_aliasing={{0}: (6, {})} | custom-call | tf_op jit(solution)/shard_map/middle/pallas_call | solution.py:583
  68.0 0.0 collective-permute-done.4.next_low_ref
  68.0 2.2 %late.1 = f32[5,45,16,128]{3,2,1,0:T(8,128)} custom-call(f32[4,5,16,1]{3,2,1,0:T(8,128)S(1)} %copy-done.1, f32[2,46,16,128]{3,2,1,0:T(8,128)S(1)} %get-tuple-element.32.courant_ref, f32[5,45,16,128]{3,2,1,0:T(8,128)S(1)} %get-tuple-element.33.tracer_ref, bf16[7,16,128]{2,1,0:T(8,128)(2,1)S(1)} %collective-permute-done.high_ref, ...), custom_call_target="tpu_custom_call", output_to_operand_aliasing={{}: (8, {})} | custom-call | tf_op jit(solution)/shard_map/late/pallas_call | solution.py:593
  (21 shorter events, 0.1 us)
Async XLA Ops:
  0.6 16.3 %copy-start = (bf16[3,16,45,128]{3,1,2,0:T(8,128)(2,1)S(1)}, bf16[3,16,45,128]{3,1,2,0:T(8,128)(2,1)}, u32[]{:S(2)}) copy-start(bf16[3,16,45,128]{3,1,2,0:T(8,128)(2,1)} %param.15) | copy-start | bytes 1658884
  0.6 16.5 %copy-start.3 = (f32[2,16,45,128]{3,1,2,0:T(8,128)S(1)}, f32[2,16,45,128]{3,1,2,0:T(8,128)}, u32[]{:S(2)}) copy-start(f32[2,16,45,128]{3,1,2,0:T(8,128)} %param.17) | copy-start | bytes 2211844
  3.5 14.7 %copy-start.2 = (f32[5,16,45,128]{3,1,2,0:T(8,128)S(1)}, f32[5,16,45,128]{3,1,2,0:T(8,128)}, u32[]{:S(2)}) copy-start(f32[5,16,45,128]{3,1,2,0:T(8,128)} %param.18) | copy-start | bytes 5529604
  3.5 32.3 %all-to-all-start = ((bf16[64,9,4,128]{3,2,1,0:T(4,128)(2,1)}), bf16[64,9,4,128]{3,2,1,0:T(4,128)(2,1)}, u32[]{:S(2)}, u32[]{:S(2)}) async-start(bf16[64,9,4,128]{3,2,1,0:T(4,128)(2,1)} %bitcast.50), calls=%async_computation | async-start | bytes 1179648 | tf_op jit(solution)/shard_map/forth/all_to_all | solution.py:488
  17.1 0.8 %copy-start.5 = (bf16[3,16,45,128]{3,2,1,0:T(8,128)(2,1)}, bf16[3,16,45,128]{3,2,1,0:T(8,128)(2,1)S(1)}, u32[]{:S(2)}) copy-start(bf16[3,16,45,128]{3,2,1,0:T(8,128)(2,1)S(1)} %copy.62) | copy-start | bytes 1658884
  17.4 0.7 %copy-start.6 = (bf16[2,16,45,128]{3,2,1,0:T(8,128)(2,1)}, bf16[2,16,45,128]{3,2,1,0:T(8,128)(2,1)S(1)}, u32[]{:S(2)}) copy-start(bf16[2,16,45,128]{3,2,1,0:T(8,128)(2,1)S(1)} %copy.61) | copy-start | bytes 1105924
  17.4 4.4 %copy-start.15 = (s32[64]{0:T(128)S(1)}, s32[64]{0:T(128)}, u32[]{:S(2)}) copy-start(s32[64]{0:T(128)} %param.16) | copy-start | bytes 772
  17.4 5.1 %copy-start.13 = (f32[384]{0:T(512)S(1)}, f32[384]{0:T(512)}, u32[]{:S(2)}) copy-start(f32[384]{0:T(512)} %constant.58.clone) | copy-start | bytes 4612
  17.4 5.1 %copy-start.14 = (s32[384]{0:T(512)S(1)}, s32[384]{0:T(512)}, u32[]{:S(2)}) copy-start(s32[384]{0:T(512)} %constant.59.clone) | copy-start | bytes 4612
  17.4 7.3 %copy-start.7 = (f32[32,384]{1,0:T(8,128)S(1)}, f32[32,384]{1,0:T(8,128)}, u32[]{:S(2)}) copy-start(f32[32,384]{1,0:T(8,128)} %constant.61.clone) | copy-start | bytes 147460
  17.4 7.3 %copy-start.8 = (f32[32,384]{1,0:T(8,128)S(1)}, f32[32,384]{1,0:T(8,128)}, u32[]{:S(2)}) copy-start(f32[32,384]{1,0:T(8,128)} %constant.60.clone) | copy-start | bytes 147460
  17.5 7.3 %copy-start.11 = (f32[24,384]{1,0:T(8,128)S(1)}, f32[24,384]{1,0:T(8,128)}, u32[]{:S(2)}) copy-start(f32[24,384]{1,0:T(8,128)} %constant.65.clone) | copy-start | bytes 110596
  17.5 7.3 %copy-start.12 = (f32[24,384]{1,0:T(8,128)S(1)}, f32[24,384]{1,0:T(8,128)}, u32[]{:S(2)}) copy-start(f32[24,384]{1,0:T(8,128)} %constant.64.clone) | copy-start | bytes 110596
  18.1 6.8 %copy-start.9 = (f32[72,384]{1,0:T(8,128)S(1)}, f32[72,384]{1,0:T(8,128)}, u32[]{:S(2)}) copy-start(f32[72,384]{1,0:T(8,128)} %constant.63.clone) | copy-start | bytes 331780
  18.2 6.8 %copy-start.10 = (f32[72,384]{1,0:T(8,128)S(1)}, f32[72,384]{1,0:T(8,128)}, u32[]{:S(2)}) copy-start(f32[72,384]{1,0:T(8,128)} %constant.62.clone) | copy-start | bytes 331780
  18.8 2.9 %copy-start.4 = (bf16[5,16,45,128]{3,2,0,1:T(8,128)(2,1)}, bf16[5,16,45,128]{3,2,0,1:T(8,128)(2,1)S(1)}, u32[]{:S(2)}) copy-start(bf16[5,16,45,128]{3,2,0,1:T(8,128)(2,1)S(1)} %copy.60) | copy-start | bytes 2764804
  18.9 8.9 %collective-permute-start = (bf16[7,16,128]{2,1,0:T(8,128)(2,1)S(1)}, bf16[7,16,128]{2,1,0:T(8,128)(2,1)S(1)}, u32[]{:S(2)}, u32[]{:S(2)}) collective-permute-start(bf16[7,16,128]{2,1,0:T(8,128)(2,1)S(1)} %pad_maximum_fusion.1), channel_id=1, source_target_pairs={{1,0},{2,1},{3,2},{4,3},{5,4},{6,5},{7,6},{8,7},{9,8},{10,9},{11,1... | collective-permute-start | bytes 86024 | tf_op jit(solution)/shard_map/columns/ppermute | solution.py:514
  21.7 6.1 %collective-permute-start.1 = (bf16[5,16,128]{2,1,0:T(8,128)(2,1)S(1)}, bf16[5,16,128]{2,1,0:T(8,128)(2,1)S(1)}, u32[]{:S(2)}, u32[]{:S(2)}) collective-permute-start(bf16[5,16,128]{2,1,0:T(8,128)(2,1)S(1)} %bitcast.61), channel_id=1, source_target_pairs={{0,1},{1,2},{2,3},{3,4},{4,5},{5,6},{6,7},{7,8},{8,9},{9,10},{10,1... | collective-permute-start | bytes 61448 | tf_op jit(solution)/shard_map/columns/ppermute | solution.py:515
  35.8 28.1 %copy-start.1 = (f32[4,5,16,1]{3,2,1,0:T(8,128)S(1)}, f32[4,5,16,1]{3,2,1,0:T(8,128)}, u32[]{:S(2)}) copy-start(f32[4,5,16,1]{3,2,1,0:T(8,128)} %constant.57.clone.factor_ref) | copy-start | bytes 3844
  39.5 24.3 %all-to-all-start.1 = ((bf16[64,9,4,128]{3,2,1,0:T(4,128)(2,1)}), bf16[64,9,4,128]{3,2,1,0:T(4,128)(2,1)S(1)}, u32[]{:S(2)}, u32[]{:S(2)}) async-start(bf16[64,9,4,128]{3,2,1,0:T(4,128)(2,1)} %bitcast.51), calls=%async_computation.1 | async-start | bytes 1179648 | tf_op jit(solution)/shard_map/back/all_to_all | solution.py:541
  45.8 5.2 %collective-permute-start.2 = (bf16[7,45,128]{2,1,0:T(8,128)(2,1)S(1)}, bf16[7,45,128]{2,1,0:T(8,128)(2,1)S(1)}, u32[]{:S(2)}, u32[]{:S(2)}) collective-permute-start(bf16[7,45,128]{2,1,0:T(8,128)(2,1)S(1)} %pad_maximum_fusion), channel_id=1, source_target_pairs={{64,0},{128,64},{192,128},{65,1},{129,65},{193,129},{66,2},{130,66... | collective-permute-start | bytes 241928 | tf_op jit(solution)/shard_map/below/ppermute | solution.py:545
  47.1 3.9 %collective-permute-start.3 = (bf16[5,45,128]{2,1,0:T(8,128)(2,1)S(1)}, bf16[5,45,128]{2,1,0:T(8,128)(2,1)S(1)}, u32[]{:S(2)}, u32[]{:S(2)}) collective-permute-start(bf16[5,45,128]{2,1,0:T(8,128)(2,1)S(1)} %get-tuple-element.29), channel_id=1, source_target_pairs={{0,64},{64,128},{128,192},{1,65},{65,129},{129,193},{2,66},{66,130... | collective-permute-start | bytes 172808 | tf_op jit(solution)/shard_map/top/ppermute | solution.py:547
  64.0 4.0 %collective-permute-start.4 = (bf16[2,72,128]{2,1,0:T(8,128)(2,1)S(1)}, bf16[2,72,128]{2,1,0:T(8,128)(2,1)S(1)}, u32[]{:S(2)}, u32[]{:S(2)}) collective-permute-start(bf16[2,72,128]{2,1,0:T(8,128)(2,1)S(1)} %get-tuple-element.34), channel_id=1, source_target_pairs={{64,0},{65,1},{66,2},{67,3},{68,4},{69,5},{70,6},{71,7},{72,8},{73... | collective-permute-start | bytes 110600 | tf_op jit(solution)/shard_map/ppermute | solution.py:582
